TPU v7x, 512 devices: a whole 4x8x8 slice. The times are simulated.
512 devices in a mesh: layer: 32 (over x_lo, y, core), tp: 16 (over z, x_hi).
Axes of the slice: x: 4 (x_hi: 2, x_lo: 2; x = x_hi * 2 + x_lo), y: 8, z: 8, core: 2. Of those that a mesh axis runs over, the one named last changes fastest.
Arguments:
- acts: bfloat16 [4096, 2048], P(('layer', 'tp')), may hold values from -12 to 12, as said below
- fresh: bfloat16 [2, 128, 2048], P(None, 'tp'), may hold values from -12 to 12, as said below
- norm_first: float32 [16, 2048], replicated, may hold values from 0.5 to 1.5
- norm_second: float32 [16, 2048], replicated, may hold values from 0.5 to 1.5
- proj_qkv: bfloat16 [512, 2048, 192], P(('layer', 'tp')), may hold values from -1 to 1
- proj_out: bfloat16 [32768, 2048], P(('layer', 'tp')), may hold values from -0.125 to 0.125
- proj_gate_up: bfloat16 [2048, 2, 131072], P(None, None, ('layer', 'tp')), may hold values from -0.125 to 0.125
- proj_down: bfloat16 [131072, 2048], P(('layer', 'tp')), may hold values from -0.0625 to 0.0625
- memory_state: float32 [512, 64, 64], P(('layer', 'tp')), may hold values from -768 to 768
- memory_norm: float32 [512, 64], P(('layer', 'tp')), may hold values from 16 to 256
- bias_gate: float32 [512], P(('layer', 'tp')), may hold values from -3 to 3
Outputs:
- first_out: bfloat16 [4096, 2048], P(('layer', 'tp'))
- second_out: bfloat16 [4096, 2048], P(('layer', 'tp'))
- memory_after: float32 [512, 64, 64], P(('layer', 'tp'))
- norm_after: float32 [512, 64], P(('layer', 'tp'))
Inputs may be any that keep to these rules, and one draw needn't show every extreme that they name: `acts`: activation rows. `fresh`: activation rows.
All inputs are finite; a program needn't handle non-finite values.
Results may differ from a plain program's by a relative error of at most 0.025.
Values may be sent and summed in bfloat16 or wider, within the bound.
No kernel may reach another device: no remote copies, remote signals or barrier semaphores. Data moves between devices by JAX's collectives and lax.ppermute only.
A program may use at most 64 MiB of HBM per device.

v0:
```python
import jax
import jax.numpy as jnp
from jax import lax
from jax.sharding import PartitionSpec as P


def partner_2(value, axis, distance):
    mask = 2**distance
    pairs = [(source, source ^ mask) for source in range(lax.axis_size(axis))]
    return lax.ppermute(value, axis, pairs)


def shifted(value, axis, steps):
    count = lax.axis_size(axis)
    initial, last = (max(0, -steps), min(count, count - steps))
    return lax.ppermute(value, axis, [(source, source + steps) for source in range(initial, last)])


def rms_norm(values, weight):
    floats = values.astype(jnp.float32)
    scaled = floats * lax.rsqrt(jnp.mean(floats * floats, axis=-1, keepdims=True) + 1e-05)
    return (scaled * weight).astype(jnp.bfloat16)


def attend(qkv, memory, totals, logits):
    head_dim = memory.shape[-1]
    seg_len = qkv.shape[0]
    queries = qkv[..., :head_dim]
    keyed = qkv[..., head_dim : 2 * head_dim]
    valued = qkv[..., 2 * head_dim :]
    scores = jnp.einsum(
        "qhc,khc->hqk", queries, keyed, preferred_element_type=jnp.float32
    ) * head_dim ** (-0.5)
    positions = jnp.arange(seg_len)
    allowed = positions[:, None] >= positions[None, :]
    probs = jax.nn.softmax(jnp.where(allowed[None], scores, -jnp.inf), axis=-1).astype(jnp.bfloat16)
    direct = jnp.einsum("hqk,khc->qhc", probs, valued, preferred_element_type=jnp.float32)
    lifted_q = jax.nn.elu(queries.astype(jnp.float32)) + 1.0
    lifted_k = jax.nn.elu(keyed.astype(jnp.float32)) + 1.0
    numer = jnp.einsum("qhc,hce->qhe", lifted_q, memory, precision=lax.Precision.HIGHEST)
    denom = jnp.einsum("qhc,hc->qh", lifted_q, totals, precision=lax.Precision.HIGHEST)[..., None]
    gate_open = jax.nn.sigmoid(logits)[None, :, None]
    blended = (gate_open * numer / denom + (1.0 - gate_open) * direct).astype(jnp.bfloat16)
    new_memory = memory + jnp.einsum(
        "khc,khe->hce", lifted_k, valued.astype(jnp.float32), precision=lax.Precision.HIGHEST
    )
    new_totals = totals + jnp.sum(lifted_k, axis=0)
    return (blended.reshape(seg_len, -1), new_memory, new_totals)


def body(
    acts,
    fresh,
    norm_first,
    norm_second,
    proj_qkv,
    proj_out,
    proj_gate_up,
    proj_down,
    memory_state,
    memory_norm,
    bias_gate,
):
    position = lax.axis_index("layer")
    lower = position % 2 == 0
    depth = position // 2
    member = lax.axis_index("tp")
    gain_one = lax.dynamic_index_in_dim(norm_first, depth, 0, keepdims=False)
    gain_two = lax.dynamic_index_in_dim(norm_second, depth, 0, keepdims=False)
    row_count = acts.shape[0]

    def ordered(mine, other):
        return jnp.concatenate(
            [jnp.where(lower, mine, other), jnp.where(lower, other, mine)], axis=0
        )

    def project(rows):
        return jnp.einsum("sd,hdc->shc", rows, proj_qkv, preferred_element_type=jnp.float32).astype(
            jnp.bfloat16
        )

    def expand(rows):
        gate_up = jnp.einsum("sd,dtf->stf", rows, proj_gate_up, preferred_element_type=jnp.float32)
        return (jax.nn.silu(gate_up[:, 0]) * gate_up[:, 1]).astype(jnp.bfloat16)

    def collect_all(values):
        partner = partner_2(values, "layer", 0)
        mine, other = (
            lax.all_gather(values, "tp", axis=0, tiled=True),
            lax.all_gather(partner, "tp", axis=0, tiled=True),
        )
        return ordered(mine, other)

    def total_all(local, weight):
        summed = lax.psum(
            jnp.dot(local, weight, preferred_element_type=jnp.float32).astype(jnp.bfloat16), "tp"
        ).astype(jnp.float32)
        return summed + partner_2(summed.astype(jnp.bfloat16), "layer", 0).astype(summed.dtype)

    def apply_layer(stream, memory, totals):
        gathered = collect_all(stream)
        seg_len = gathered.shape[0]
        qkv = project(rms_norm(gathered, gain_one))
        blended, memory, totals = attend(qkv, memory, totals, bias_gate)
        attn = total_all(blended, proj_out)
        hidden_one = (gathered.astype(jnp.float32) + attn).astype(jnp.bfloat16)
        hidden = expand(rms_norm(hidden_one, gain_two))
        ffn = total_all(hidden, proj_down)
        complete = (hidden_one.astype(jnp.float32) + ffn).astype(jnp.bfloat16)
        start = position % 2 * (seg_len // 2) + member * row_count
        output = lax.dynamic_slice_in_dim(complete, start, row_count, 0)
        return (output, memory, totals)

    first_rows, memory_one, totals_one = apply_layer(acts, memory_state, memory_norm)
    incoming = shifted(first_rows, "layer", 2)
    fresh_rows = lax.dynamic_index_in_dim(fresh, position % 2, 0, keepdims=False)
    entering = jnp.where(depth == 0, fresh_rows, incoming)
    second_rows, memory_two, totals_two = apply_layer(entering, memory_one, totals_one)
    return (first_rows, second_rows, memory_two, totals_two)


def solution(mesh):
    in_specs = (
        P(("layer", "tp"), None),
        P(None, "tp", None),
        P(),
        P(),
        P(("layer", "tp"), None, None),
        P(("layer", "tp"), None),
        P(None, None, ("layer", "tp")),
        P(("layer", "tp"), None),
        P(("layer", "tp"), None, None),
        P(("layer", "tp"), None),
        P(("layer", "tp")),
    )
    out_specs = (
        P(("layer", "tp"), None),
        P(("layer", "tp"), None),
        P(("layer", "tp"), None, None),
        P(("layer", "tp"), None),
    )
    return jax.shard_map(body, mesh=mesh, in_specs=in_specs, out_specs=out_specs, check_vma=False)
```

profile of v0, /device:TPU:1, one launch (start us, length us, event | category | flops | bytes accessed | tf_op | source)
XLA Modules:
  0.0 903.9 jit_solution(7788227879883312457)
XLA Ops:
  7.2 8.9 collective-permute-start
  16.1 40.0 %all_gather.12 = bf16[128,2048]{1,0:T(8,128)(2,1)} all-gather(bf16[8,2048]{1,0:T(8,128)(2,1)} %param.11), channel_id=1, replica_groups=mesh['layer'=32,'tp'=16] {'tp'}, dimensions={0}, use_global_device_ids=true | all-gather | bytes 557056 | tf_op jit(solution)/shard_map/all_gather | solution.py:89
  56.1 0.8 constant_dynamic-slice_fusion.1
  57.7 31.6 %all_gather.13 = bf16[128,2048]{1,0:T(8,128)(2,1)S(1)} all-gather(bf16[8,2048]{1,0:T(8,128)(2,1)S(1)} %collective-permute-done), channel_id=1, replica_groups=mesh['layer'=32,'tp'=16] {'tp'}, dimensions={0}, use_global_device_ids=true | all-gather | bytes 557056 | tf_op jit(solution)/shard_map/all_gather | solution.py:90
  89.3 1.1 broadcast_select_fusion.3
  90.7 1.7 fusion.14
  93.3 2.7 convolution_convert_fusion.3
  96.1 167.5 %all-reduce.5.cloned.1.call-done = bf16[256,2048]{1,0:T(8,128)(2,1)} async-done(((bf16[256,2048]{1,0:T(8,128)(2,1)}), bf16[256,2048]{1,0:T(8,128)(2,1)}) %all-reduce.5.cloned.1.call-update) | async-done | bytes 1048592 | tf_op jit(solution)/shard_map/psum | solution.py:95
  263.6 13.1 %collective-permute-start.1 = (bf16[256,2048]{1,0:T(8,128)(2,1)}, bf16[256,2048]{1,0:T(8,128)(2,1)S(1)}, u32[]{:S(2)}, u32[]{:S(2)}) collective-permute-start(bf16[256,2048]{1,0:T(8,128)(2,1)} %all-reduce.5.cloned.1.call-done), channel_id=1, source_target_pairs={{0,16},{16,0},{32,48},{48,32},{64,80},{80,64},{96,112},{112,96},{1... | collective-permute-start | bytes 3145736 | tf_op jit(solution)/shard_map/ppermute | solution.py:10
  276.7 0.9 constant_dynamic-slice_fusion
  277.5 1.6 collective-permute-done.1
  279.2 1.8 multiply_reduce_fusion.1
  283.0 1.5 convolution_convert_fusion.1
  284.5 153.8 %all-reduce.7.cloned.1.call-done = bf16[256,2048]{1,0:T(8,128)(2,1)} async-done(((bf16[256,2048]{1,0:T(8,128)(2,1)}), bf16[256,2048]{1,0:T(8,128)(2,1)}) %all-reduce.7.cloned.1.call-update) | async-done | bytes 1048592 | tf_op jit(solution)/shard_map/psum | solution.py:95
  438.3 13.1 %collective-permute-start.2 = (bf16[256,2048]{1,0:T(8,128)(2,1)}, bf16[256,2048]{1,0:T(8,128)(2,1)S(1)}, u32[]{:S(2)}, u32[]{:S(2)}) collective-permute-start(bf16[256,2048]{1,0:T(8,128)(2,1)} %all-reduce.7.cloned.1.call-done), channel_id=1, source_target_pairs={{0,16},{16,0},{32,48},{48,32},{64,80},{80,64},{96,112},{112,96},{1... | collective-permute-start | bytes 3145736 | tf_op jit(solution)/shard_map/ppermute | solution.py:10
  451.7 2.2 collective-permute-done.2
  453.9 0.9 fusion.77
  454.8 3.1 collective-permute-start.3
  458.0 0.9 collective-permute-done.3
  458.9 3.3 collective-permute-start.4
  462.2 36.4 %all_gather.14 = bf16[128,2048]{1,0:T(8,128)(2,1)S(1)} all-gather(bf16[8,2048]{1,0:T(8,128)(2,1)S(1)} %bitcast_select_fusion), channel_id=1, replica_groups=mesh['layer'=32,'tp'=16] {'tp'}, dimensions={0}, use_global_device_ids=true | all-gather | bytes 557056 | tf_op jit(solution)/shard_map/all_gather | solution.py:89
  498.7 32.0 %all_gather.15 = bf16[128,2048]{1,0:T(8,128)(2,1)S(1)} all-gather(bf16[8,2048]{1,0:T(8,128)(2,1)S(1)} %collective-permute-done.4), channel_id=1, replica_groups=mesh['layer'=32,'tp'=16] {'tp'}, dimensions={0}, use_global_device_ids=true | all-gather | bytes 557056 | tf_op jit(solution)/shard_map/all_gather | solution.py:90
  532.6 2.6 convolution_convert_fusion.2
  535.3 170.2 %all-reduce.9.cloned.1.call-done = bf16[256,2048]{1,0:T(8,128)(2,1)} async-done(((bf16[256,2048]{1,0:T(8,128)(2,1)}), bf16[256,2048]{1,0:T(8,128)(2,1)}) %all-reduce.9.cloned.1.call-update) | async-done | bytes 1048592 | tf_op jit(solution)/shard_map/psum | solution.py:95
  705.5 13.1 %collective-permute-start.5 = (bf16[256,2048]{1,0:T(8,128)(2,1)}, bf16[256,2048]{1,0:T(8,128)(2,1)S(1)}, u32[]{:S(2)}, u32[]{:S(2)}) collective-permute-start(bf16[256,2048]{1,0:T(8,128)(2,1)} %all-reduce.9.cloned.1.call-done), channel_id=1, source_target_pairs={{0,16},{16,0},{32,48},{48,32},{64,80},{80,64},{96,112},{112,96},{1... | collective-permute-start | bytes 3145736 | tf_op jit(solution)/shard_map/ppermute | solution.py:10
  718.6 2.5 collective-permute-done.5
  721.0 1.8 multiply_reduce_fusion
  724.8 1.4 convolution_convert_fusion
  726.3 154.0 %all-reduce.11.cloned.1.call-done = bf16[256,2048]{1,0:T(8,128)(2,1)} async-done(((bf16[256,2048]{1,0:T(8,128)(2,1)}), bf16[256,2048]{1,0:T(8,128)(2,1)}) %all-reduce.11.cloned.1.call-update) | async-done | bytes 1048592 | tf_op jit(solution)/shard_map/psum | solution.py:95
  880.3 13.1 %collective-permute-start.6 = (bf16[256,2048]{1,0:T(8,128)(2,1)}, bf16[256,2048]{1,0:T(8,128)(2,1)S(1)}, u32[]{:S(2)}, u32[]{:S(2)}) collective-permute-start(bf16[256,2048]{1,0:T(8,128)(2,1)} %all-reduce.11.cloned.1.call-done), channel_id=1, source_target_pairs={{0,16},{16,0},{32,48},{48,32},{64,80},{80,64},{96,112},{112,96},{1... | collective-permute-start | bytes 3145736 | tf_op jit(solution)/shard_map/ppermute | solution.py:10
  894.8 1.0 collective-permute-done.6
  895.9 1.5 fusion.76
  (68 shorter events, 9.1 us)
Async XLA Ops:
  7.2 273.8 %copy-start = (bf16[2048,2,256]{2,1,0:T(2,128)(2,1)S(1)}, bf16[2048,2,256]{2,1,0:T(2,128)(2,1)}, u32[]{:S(2)}) copy-start(bf16[2048,2,256]{2,1,0:T(2,128)(2,1)} %param.17) | copy-start | bytes 6291460
  7.2 256.4 %all-reduce.5.cloned.1.call-start = ((), (), s32[]{:S(2)}) async-start(), calls=%async_computation | async-start | bytes 2097152 | tf_op jit(solution)/shard_map/psum | solution.py:95
  7.2 50.5 %collective-permute-start = (bf16[8,2048]{1,0:T(8,128)(2,1)}, bf16[8,2048]{1,0:T(8,128)(2,1)S(1)}, u32[]{:S(2)}, u32[]{:S(2)}) collective-permute-start(bf16[8,2048]{1,0:T(8,128)(2,1)} %param.11), channel_id=1, source_target_pairs={{0,16},{16,0},{32,48},{48,32},{64,80},{80,64},{96,112},{112,96},{1... | collective-permute-start | bytes 98312 | tf_op jit(solution)/shard_map/ppermute | solution.py:10
  90.7 2.0 copy-start.9
  90.7 2.4 copy-start.13
  92.4 0.6 copy-start.3
  96.0 342.3 %all-reduce.7.cloned.1.call-start = ((), (), s32[]{:S(2)}) async-start(), calls=%async_computation.1 | async-start | bytes 2097152 | tf_op jit(solution)/shard_map/psum | solution.py:95
  263.6 15.6 %collective-permute-start.1 = (bf16[256,2048]{1,0:T(8,128)(2,1)}, bf16[256,2048]{1,0:T(8,128)(2,1)S(1)}, u32[]{:S(2)}, u32[]{:S(2)}) collective-permute-start(bf16[256,2048]{1,0:T(8,128)(2,1)} %all-reduce.5.cloned.1.call-done), channel_id=1, source_target_pairs={{0,16},{16,0},{32,48},{48,32},{64,80},{80,64},{96,112},{112,96},{1... | collective-permute-start | bytes 3145736 | tf_op jit(solution)/shard_map/ppermute | solution.py:10
  280.9 1.3 copy-start.1
  281.0 2.0 copy-start.10
  282.9 168.5 %copy-start.4 = (bf16[256,1,192]{0,2,1:T(8,128)(2,1)S(1)}, bf16[256,1,192]{0,2,1:T(8,128)(2,1)}, u32[]{:S(2)}) copy-start(bf16[256,1,192]{0,2,1:T(8,128)(2,1)} %copy-done.3) | copy-start | bytes 294916
  282.9 168.5 %copy-start.14 = (f32[1,64,64]{2,1,0:T(8,128)S(1)}, f32[1,64,64]{2,1,0:T(8,128)}, u32[]{:S(2)}) copy-start(f32[1,64,64]{2,1,0:T(8,128)} %param.19) | copy-start | bytes 49156
  283.0 176.0 %copy-start.8 = (bf16[2,8,2048]{2,1,0:T(8,128)(2,1)S(1)}, bf16[2,8,2048]{2,1,0:T(8,128)(2,1)}, u32[]{:S(2)}) copy-start(bf16[2,8,2048]{2,1,0:T(8,128)(2,1)} %param.12) | copy-start | bytes 196612
  284.4 421.0 %all-reduce.9.cloned.1.call-start = ((), (), s32[]{:S(2)}) async-start(), calls=%async_computation.2 | async-start | bytes 2097152 | tf_op jit(solution)/shard_map/psum | solution.py:95
  438.3 15.6 %collective-permute-start.2 = (bf16[256,2048]{1,0:T(8,128)(2,1)}, bf16[256,2048]{1,0:T(8,128)(2,1)S(1)}, u32[]{:S(2)}, u32[]{:S(2)}) collective-permute-start(bf16[256,2048]{1,0:T(8,128)(2,1)} %all-reduce.7.cloned.1.call-done), channel_id=1, source_target_pairs={{0,16},{16,0},{32,48},{48,32},{64,80},{80,64},{96,112},{112,96},{1... | collective-permute-start | bytes 3145736 | tf_op jit(solution)/shard_map/ppermute | solution.py:10
  451.7 80.4 %copy-start.15 = (f32[1,64,64]{2,1,0:T(8,128)}, f32[1,64,64]{2,1,0:T(8,128)S(1)}, u32[]{:S(2)}) copy-start(f32[1,64,64]{2,1,0:T(8,128)S(1)} %fusion.26) | copy-start | bytes 49156
  454.8 76.2 %copy-start.7 = (bf16[8,2048]{1,0:T(8,128)(2,1)}, bf16[8,2048]{1,0:T(8,128)(2,1)S(1)}, u32[]{:S(2)}) copy-start(bf16[8,2048]{1,0:T(8,128)(2,1)S(1)} %fusion.77) | copy-start | bytes 98308
  454.8 4.1 collective-permute-start.3
  458.9 72.1 %copy-start.12 = (bf16[1,2048,192]{1,2,0:T(8,128)(2,1)S(1)}, bf16[1,2048,192]{1,2,0:T(8,128)(2,1)}, u32[]{:S(2)}) copy-start(bf16[1,2048,192]{1,2,0:T(8,128)(2,1)} %param.15) | copy-start | bytes 2359300
  458.9 39.7 %collective-permute-start.4 = (bf16[8,2048]{1,0:T(8,128)(2,1)S(1)}, bf16[8,2048]{1,0:T(8,128)(2,1)S(1)}, u32[]{:S(2)}, u32[]{:S(2)}) collective-permute-start(bf16[8,2048]{1,0:T(8,128)(2,1)S(1)} %bitcast_select_fusion), channel_id=1, source_target_pairs={{0,16},{16,0},{32,48},{48,32},{64,80},{80,64},{96,112},{112,96},{1... | collective-permute-start | bytes 98312 | tf_op jit(solution)/shard_map/ppermute | solution.py:10
  531.6 0.6 copy-start.5
  535.3 345.0 %all-reduce.11.cloned.1.call-start = ((), (), s32[]{:S(2)}) async-start(), calls=%async_computation.3 | async-start | bytes 2097152 | tf_op jit(solution)/shard_map/psum | solution.py:95
  705.5 15.6 %collective-permute-start.5 = (bf16[256,2048]{1,0:T(8,128)(2,1)}, bf16[256,2048]{1,0:T(8,128)(2,1)S(1)}, u32[]{:S(2)}, u32[]{:S(2)}) collective-permute-start(bf16[256,2048]{1,0:T(8,128)(2,1)} %all-reduce.9.cloned.1.call-done), channel_id=1, source_target_pairs={{0,16},{16,0},{32,48},{48,32},{64,80},{80,64},{96,112},{112,96},{1... | collective-permute-start | bytes 3145736 | tf_op jit(solution)/shard_map/ppermute | solution.py:10
  722.8 1.3 copy-start.2
  722.8 2.0 copy-start.11
  724.8 168.5 %copy-start.6 = (bf16[256,1,192]{0,2,1:T(8,128)(2,1)S(1)}, bf16[256,1,192]{0,2,1:T(8,128)(2,1)}, u32[]{:S(2)}) copy-start(bf16[256,1,192]{0,2,1:T(8,128)(2,1)} %copy-done.5) | copy-start | bytes 294916
  724.8 169.2 %copy-start.16 = (f32[1,64,64]{2,1,0:T(8,128)S(1)}, f32[1,64,64]{2,1,0:T(8,128)}, u32[]{:S(2)}) copy-start(f32[1,64,64]{2,1,0:T(8,128)} %copy-done.15) | copy-start | bytes 49156
  880.3 15.6 %collective-permute-start.6 = (bf16[256,2048]{1,0:T(8,128)(2,1)}, bf16[256,2048]{1,0:T(8,128)(2,1)S(1)}, u32[]{:S(2)}, u32[]{:S(2)}) collective-permute-start(bf16[256,2048]{1,0:T(8,128)(2,1)} %all-reduce.11.cloned.1.call-done), channel_id=1, source_target_pairs={{0,16},{16,0},{32,48},{48,32},{64,80},{80,64},{96,112},{112,96},{1... | collective-permute-start | bytes 3145736 | tf_op jit(solution)/shard_map/ppermute | solution.py:10
Sparse Core Ops, SparseCore 0:
  96.1 167.3 all-reduce.4
  284.6 153.7 all-reduce.6
  535.4 170.0 all-reduce.8
  726.4 153.7 all-reduce.10
where the time goes:
time: 905 us; the launch traced here: 904 us
  waiting for transfers between devices  654 us (72%)
  blocking collectives  140 us (15%)
  starting transfers between devices  67.8 us (7%)
  between operations  14.8 us (2%)
  matrix products  14.4 us (2%)
    psum x4, waiting for transfers between devices, total_all(): lax.psum(jnp.dot(local, weight, preferred_element_type=jnp.float32).astyp...  645 us
    all_gather x2, blocking collectives, collect_all(): lax.all_gather(values, 'tp', axis=0, tiled=True)  76.4 us
    ppermute x6, starting transfers between devices, partner_2(): return lax.ppermute(value, axis, pairs)  64.6 us
    all_gather x2, blocking collectives, collect_all(): lax.all_gather(partner, 'tp', axis=0, tiled=True)  63.5 us
  transfers between devices with their start and end apart: 11, of which 9 were waited for; matrix products, arithmetic and copies ran while one was open for 0% of the time, Pallas kernels for 0%

commit v1 on v0

v1 whole, which is shorter than its diff:
```python
import jax
import jax.numpy as jnp
from jax import lax
from jax.sharding import PartitionSpec as P


def swap_halves(value):
    pairs = [(source, source ^ 1) for source in range(lax.axis_size("layer"))]
    return lax.ppermute(value, "layer", pairs)


def next_layer(value):
    count = lax.axis_size("layer")
    return lax.ppermute(value, "layer", [(source, source + 2) for source in range(count - 2)])


def exchange(blocks):
    return lax.all_to_all(blocks, "tp", 0, 0, tiled=True)


def gather_rows(rows):
    members = lax.axis_size("tp")
    blocks = exchange(jnp.broadcast_to(rows[None], (members,) + rows.shape))
    return blocks.reshape((-1, rows.shape[1]))


def scatter_sum(partial):
    members = lax.axis_size("tp")
    blocks = exchange(partial.reshape((members, -1, partial.shape[1])))
    return jnp.sum(blocks.astype(jnp.float32), axis=0)


def rms_norm(values, weight):
    floats = values.astype(jnp.float32)
    scaled = floats * lax.rsqrt(jnp.mean(floats * floats, axis=-1, keepdims=True) + 1e-05)
    return (scaled * weight).astype(jnp.bfloat16)


def attend(qkv, memory, totals, logits, allowed):
    head_dim = memory.shape[-1]
    queries = qkv[..., :head_dim]
    keyed = qkv[..., head_dim : 2 * head_dim]
    valued = qkv[..., 2 * head_dim :]
    scores = jnp.einsum(
        "qhc,khc->hqk", queries, keyed, preferred_element_type=jnp.float32
    ) * head_dim ** (-0.5)
    probs = jax.nn.softmax(jnp.where(allowed[None], scores, -jnp.inf), axis=-1).astype(jnp.bfloat16)
    direct = jnp.einsum("hqk,khc->qhc", probs, valued, preferred_element_type=jnp.float32)
    lifted_q = jax.nn.elu(queries.astype(jnp.float32)) + 1.0
    lifted_k = jax.nn.elu(keyed.astype(jnp.float32)) + 1.0
    numer = jnp.einsum("qhc,hce->qhe", lifted_q, memory, precision=lax.Precision.HIGHEST)
    denom = jnp.einsum("qhc,hc->qh", lifted_q, totals, precision=lax.Precision.HIGHEST)[..., None]
    gate_open = jax.nn.sigmoid(logits)[None, :, None]
    blended = (gate_open * numer / denom + (1.0 - gate_open) * direct).astype(jnp.bfloat16)
    new_memory = memory + jnp.einsum(
        "khc,khe->hce", lifted_k, valued.astype(jnp.float32), precision=lax.Precision.HIGHEST
    )
    new_totals = totals + jnp.sum(lifted_k, axis=0)
    return (blended.reshape(qkv.shape[0], -1), new_memory, new_totals)


def body(
    acts,
    fresh,
    norm_first,
    norm_second,
    proj_qkv,
    proj_out,
    proj_gate_up,
    proj_down,
    memory_state,
    memory_norm,
    bias_gate,
):
    position = lax.axis_index("layer")
    half = position % 2
    depth = position // 2
    gain_one = lax.dynamic_index_in_dim(norm_first, depth, 0, keepdims=False)
    gain_two = lax.dynamic_index_in_dim(norm_second, depth, 0, keepdims=False)
    other_gate_up = swap_halves(proj_gate_up)
    other_down = swap_halves(proj_down)
    half_len = acts.shape[0] * lax.axis_size("tp")
    index = jnp.arange(2 * half_len)
    places = jnp.where(index < half_len, index + half * half_len, index - half * half_len)
    allowed = places[:, None] >= places[None, :]

    def project(rows):
        return jnp.einsum("sd,hdc->shc", rows, proj_qkv, preferred_element_type=jnp.float32).astype(
            jnp.bfloat16
        )

    def expand(rows, weight):
        gate_up = jnp.einsum("sd,dtf->stf", rows, weight, preferred_element_type=jnp.float32)
        return (jax.nn.silu(gate_up[:, 0]) * gate_up[:, 1]).astype(jnp.bfloat16)

    def apply_layer(rows, memory, totals):
        mine = gather_rows(rms_norm(rows, gain_one))
        normed = jnp.concatenate([mine, swap_halves(mine)], axis=0)
        blended, memory, totals = attend(project(normed), memory, totals, bias_gate, allowed)
        partial = jnp.dot(blended, proj_out, preferred_element_type=jnp.float32)
        away = swap_halves(partial[half_len:].astype(jnp.bfloat16))
        pair = (partial[:half_len] + away.astype(jnp.float32)).astype(jnp.bfloat16)
        hidden_one = (rows.astype(jnp.float32) + scatter_sum(pair)).astype(jnp.bfloat16)
        normed_two = gather_rows(rms_norm(hidden_one, gain_two))
        down = jnp.dot(
            expand(normed_two, proj_gate_up), proj_down, preferred_element_type=jnp.float32
        ) + jnp.dot(
            expand(normed_two, other_gate_up), other_down, preferred_element_type=jnp.float32
        )
        ffn = scatter_sum(down.astype(jnp.bfloat16))
        output = (hidden_one.astype(jnp.float32) + ffn).astype(jnp.bfloat16)
        return (output, memory, totals)

    first_rows, memory_one, totals_one = apply_layer(acts, memory_state, memory_norm)
    incoming = next_layer(first_rows)
    fresh_rows = lax.dynamic_index_in_dim(fresh, half, 0, keepdims=False)
    entering = jnp.where(depth == 0, fresh_rows, incoming)
    second_rows, memory_two, totals_two = apply_layer(entering, memory_one, totals_one)
    return (first_rows, second_rows, memory_two, totals_two)


def solution(mesh):
    in_specs = (
        P(("layer", "tp"), None),
        P(None, "tp", None),
        P(),
        P(),
        P(("layer", "tp"), None, None),
        P(("layer", "tp"), None),
        P(None, None, ("layer", "tp")),
        P(("layer", "tp"), None),
        P(("layer", "tp"), None, None),
        P(("layer", "tp"), None),
        P(("layer", "tp")),
    )
    out_specs = (
        P(("layer", "tp"), None),
        P(("layer", "tp"), None),
        P(("layer", "tp"), None, None),
        P(("layer", "tp"), None),
    )
    return jax.shard_map(body, mesh=mesh, in_specs=in_specs, out_specs=out_specs, check_vma=False)
```

time: 905 us -> 231 us (0.26)
  the two profiles are of different devices: /device:TPU:1 before, /device:TPU:2 now
where the time goes in v1:
time: 231 us; the launch traced here: 229 us
  blocking collectives  114 us (49%)
  waiting for transfers between devices  57.6 us (25%)
  starting transfers between devices  26.3 us (11%)
  matrix products  15.6 us (7%)
  local copies, waits for them, and re-layouts  7.48 us (3%)
  other arithmetic  6.58 us (3%)
    all_to_all x5, blocking collectives, exchange(): return lax.all_to_all(blocks, 'tp', 0, 0, tiled=True)  114 us
    all_to_all x3, waiting for transfers between devices, exchange(): return lax.all_to_all(blocks, 'tp', 0, 0, tiled=True)  46.7 us
    ppermute x6, starting transfers between devices, swap_halves(): return lax.ppermute(value, 'layer', pairs)  12.1 us
    all_to_all x3, starting transfers between devices, exchange(): return lax.all_to_all(blocks, 'tp', 0, 0, tiled=True)  10.7 us
    ppermute x6, waiting for transfers between devices, swap_halves(): return lax.ppermute(value, 'layer', pairs)  6.16 us
    ppermute x1, waiting for transfers between devices, next_layer(): lax.ppermute(value, 'layer', [(source, source + 2) for source in range(co...  4.73 us
  transfers between devices with their start and end apart: 10, of which 8 were waited for; matrix products, arithmetic and copies ran while one was open for 4% of the time, Pallas kernels for 0%

profile of v1, /device:TPU:2, one launch (start us, length us, event | category | flops | bytes accessed | tf_op | source)
XLA Modules:
  0.0 229.3 jit_solution(4349063269492496314)
XLA Ops:
  0.7 1.0 fusion.62
  3.4 30.6 %all_to_all.40 = bf16[16,8,2048]{2,1,0:T(8,128)(2,1)S(1)} all-to-all(bf16[16,8,2048]{2,1,0:T(8,128)(2,1)S(1)} %broadcast_in_dim.19), channel_id=1, replica_groups=mesh['layer'=32,'tp'=16] {'tp'}, dimensions={0} | all-to-all | bytes 1048576 | tf_op jit(solution)/shard_map/all_to_all | solution.py:18
  34.0 2.0 collective-permute-start
  36.8 1.1 collective-permute-done
  39.2 1.4 fusion.32
  40.7 2.0 collective-permute-start.1
  42.8 1.7 collective-permute-done.1
  45.4 3.6 %all-to-all-start.1 = ((bf16[16,8,2048]{2,1,0:T(8,128)(2,1)}), bf16[16,8,2048]{2,1,0:T(8,128)(2,1)S(1)}, u32[]{:S(2)}, u32[]{:S(2)}) async-start(bf16[16,8,2048]{2,1,0:T(8,128)(2,1)} %fusion.34), calls=%async_computation.1 | async-start | bytes 1048576 | tf_op jit(solution)/shard_map/all_to_all | solution.py:18
  49.0 3.2 %copy.15 = bf16[2048,2,256]{2,0,1:T(8,128)(2,1)} copy(bf16[2048,2,256]{2,1,0:T(2,128)(2,1)} %param.17) | data formatting | bytes 4194304 | tf_op args[6]
  52.3 2.0 collective-permute-start.2
  55.1 13.8 %all-to-all-done.1 = bf16[16,8,2048]{2,1,0:T(8,128)(2,1)S(1)} async-done(((bf16[16,8,2048]{2,1,0:T(8,128)(2,1)}), bf16[16,8,2048]{2,1,0:T(8,128)(2,1)S(1)}, u32[]{:S(2)}, u32[]{:S(2)}) %all-to-all-start.1) | async-done | bytes 524320 | tf_op jit(solution)/shard_map/all_to_all | solution.py:18
  70.1 3.6 %all-to-all-start.2 = ((bf16[16,8,2048]{2,1,0:T(8,128)(2,1)}), bf16[16,8,2048]{2,1,0:T(8,128)(2,1)S(1)}, u32[]{:S(2)}, u32[]{:S(2)}) async-start(bf16[16,8,2048]{2,1,0:T(8,128)(2,1)} %broadcast_in_dim.21), calls=%async_computation.2 | async-start | bytes 1048576 | tf_op jit(solution)/shard_map/all_to_all | solution.py:18
  73.7 1.9 collective-permute-start.3
  75.7 16.1 %all-to-all-done.2 = bf16[16,8,2048]{2,1,0:T(8,128)(2,1)S(1)} async-done(((bf16[16,8,2048]{2,1,0:T(8,128)(2,1)}), bf16[16,8,2048]{2,1,0:T(8,128)(2,1)S(1)}, u32[]{:S(2)}, u32[]{:S(2)}) %all-to-all-start.2) | async-done | bytes 524320 | tf_op jit(solution)/shard_map/all_to_all | solution.py:18
  91.8 2.1 fusion.42
  94.7 1.6 fusion.3
  96.3 20.6 %all_to_all.41 = bf16[16,8,2048]{2,1,0:T(8,128)(2,1)S(1)} all-to-all(bf16[16,8,2048]{2,1,0:T(8,128)(2,1)S(1)} %fusion.3), channel_id=1, replica_groups=mesh['layer'=32,'tp'=16] {'tp'}, dimensions={0} | all-to-all | bytes 1048576 | tf_op jit(solution)/shard_map/all_to_all | solution.py:18
  117.0 3.5 %collective-permute-start.4 = (bf16[8,2048]{1,0:T(8,128)(2,1)S(1)}, bf16[8,2048]{1,0:T(8,128)(2,1)S(1)}, u32[]{:S(2)}, u32[]{:S(2)}) collective-permute-start(bf16[8,2048]{1,0:T(8,128)(2,1)S(1)} %fusion.69), channel_id=1, source_target_pairs={{0,32},{16,48},{32,64},{48,80},{64,96},{80,112},{96,128},{112,144}... | collective-permute-start | bytes 98312 | tf_op jit(solution)/shard_map/ppermute | solution.py:14
  120.5 4.7 %collective-permute-done.4 = bf16[8,2048]{1,0:T(8,128)(2,1)S(1)} collective-permute-done((bf16[8,2048]{1,0:T(8,128)(2,1)S(1)}, bf16[8,2048]{1,0:T(8,128)(2,1)S(1)}, u32[]{:S(2)}, u32[]{:S(2)}) %collective-permute-start.4) | collective-permute-done | bytes 32800 | tf_op jit(solution)/shard_map/ppermute | solution.py:14
  125.6 18.8 %all_to_all.42 = bf16[16,8,2048]{2,1,0:T(8,128)(2,1)S(1)} all-to-all(bf16[16,8,2048]{2,1,0:T(8,128)(2,1)S(1)} %broadcast_in_dim.22), channel_id=1, replica_groups=mesh['layer'=32,'tp'=16] {'tp'}, dimensions={0} | all-to-all | bytes 1048576 | tf_op jit(solution)/shard_map/all_to_all | solution.py:18
  144.4 2.0 collective-permute-start.5
  146.8 1.5 collective-permute-done.5
  149.8 2.8 %fusion.33 = f32[256,2048]{1,0:T(8,128)} fusion(bf16[64,2048]{1,0:T(8,128)(2,1)S(1)} %copy-done.5, f32[1,64,256]{2,1,0:T(8,128)S(1)} %fusion.21, f32[256,256]{0,1:T(8,128)S(1)} %get-tuple-element.13, f32[256]{0:T(256)S(1)} %fusion.45, f32[256]{0:T(256)S(1)} %get-tuple-element.12, f32[]{:T(128)} %bitcast.12, bf16[256,1,192]{0,2,1:T(8,128)(2,1)} %copy-done.9), kind=kOutput, calls=%fused_computation.53 | convolution fusion | flops 75743232 | bytes 2722304 | tf_op jit(solution)/shard_map/dot_general | solution.py:100
  152.5 1.3 slice.194
  153.8 2.0 collective-permute-start.6
  155.9 1.8 collective-permute-done.6
  157.6 1.3 fusion.35
  159.0 22.8 %all_to_all.43 = bf16[16,8,2048]{2,1,0:T(8,128)(2,1)S(1)} all-to-all(bf16[16,8,2048]{2,1,0:T(8,128)(2,1)S(1)} %fusion.35), channel_id=1, replica_groups=mesh['layer'=32,'tp'=16] {'tp'}, dimensions={0} | all-to-all | bytes 1048576 | tf_op jit(solution)/shard_map/all_to_all | solution.py:18
  182.1 21.1 %all_to_all.44 = bf16[16,8,2048]{2,1,0:T(8,128)(2,1)S(1)} all-to-all(bf16[16,8,2048]{2,1,0:T(8,128)(2,1)S(1)} %broadcast_in_dim.23), channel_id=1, replica_groups=mesh['layer'=32,'tp'=16] {'tp'}, dimensions={0} | all-to-all | bytes 1048576 | tf_op jit(solution)/shard_map/all_to_all | solution.py:18
  204.4 2.4 %fusion.2 = bf16[16,8,2048]{2,1,0:T(8,128)(2,1)} fusion(f32[128,2048]{1,0:T(8,128)S(1)} %fusion.81, bf16[256,2048]{1,0:T(8,128)(2,1)} %collective-permute-done.3, f32[128,2,256]{2,0,1:T(8,128)S(1)} %fusion.36), kind=kOutput, calls=%fused_computation.4 | convolution fusion | flops 134938624 | bytes 2883584 | tf_op jit(solution)/shard_map/dot_general | solution.py:107
  206.8 3.6 %all-to-all-start.7 = ((bf16[16,8,2048]{2,1,0:T(8,128)(2,1)}), bf16[16,8,2048]{2,1,0:T(8,128)(2,1)S(1)}, u32[]{:S(2)}, u32[]{:S(2)}) async-start(bf16[16,8,2048]{2,1,0:T(8,128)(2,1)} %fusion.2), calls=%async_computation.7 | async-start | bytes 1048576 | tf_op jit(solution)/shard_map/all_to_all | solution.py:18
  211.9 16.8 %all-to-all-done.7 = bf16[16,8,2048]{2,1,0:T(8,128)(2,1)S(1)} async-done(((bf16[16,8,2048]{2,1,0:T(8,128)(2,1)}), bf16[16,8,2048]{2,1,0:T(8,128)(2,1)S(1)}, u32[]{:S(2)}, u32[]{:S(2)}) %all-to-all-start.7) | async-done | bytes 524320 | tf_op jit(solution)/shard_map/all_to_all | solution.py:18
  (84 shorter events, 12.6 us)
Async XLA Ops:
  0.6 37.3 %copy-start = (bf16[1,2048,192]{1,2,0:T(8,128)(2,1)S(1)}, bf16[1,2048,192]{1,2,0:T(8,128)(2,1)}, u32[]{:S(2)}) copy-start(bf16[1,2048,192]{1,2,0:T(8,128)(2,1)} %param.15) | copy-start | bytes 2359300
  3.4 35.3 %copy-start.13 = (f32[1,64]{1,0:T(1,128)S(1)}, f32[1,64]{1,0:T(1,128)}, u32[]{:S(2)}) copy-start(f32[1,64]{1,0:T(1,128)} %param.20) | copy-start | bytes 772
  3.4 35.6 %copy-start.15 = (f32[1,64,64]{2,1,0:T(8,128)S(1)}, f32[1,64,64]{2,1,0:T(8,128)}, u32[]{:S(2)}) copy-start(f32[1,64,64]{2,1,0:T(8,128)} %param.19) | copy-start | bytes 49156
  34.0 5.3 %copy-start.4 = (bf16[64,2048]{1,0:T(8,128)(2,1)S(1)}, bf16[64,2048]{1,0:T(8,128)(2,1)}, u32[]{:S(2)}) copy-start(bf16[64,2048]{1,0:T(8,128)(2,1)} %param.16) | copy-start | bytes 786436
  34.0 3.9 %collective-permute-start = (bf16[128,2048]{1,0:T(8,128)(2,1)S(1)}, bf16[128,2048]{1,0:T(8,128)(2,1)S(1)}, u32[]{:S(2)}, u32[]{:S(2)}) collective-permute-start(bf16[128,2048]{1,0:T(8,128)(2,1)S(1)} %bitcast.215), channel_id=1, source_target_pairs={{0,16},{16,0},{32,48},{48,32},{64,80},{80,64},{96,112},{112,96},{1... | collective-permute-start | bytes 1572872 | tf_op jit(solution)/shard_map/ppermute | solution.py:9
  38.4 0.8 copy-start.7
  40.7 3.8 %collective-permute-start.1 = (bf16[128,2048]{1,0:T(8,128)(2,1)S(1)}, bf16[128,2048]{1,0:T(8,128)(2,1)S(1)}, u32[]{:S(2)}, u32[]{:S(2)}) collective-permute-start(bf16[128,2048]{1,0:T(8,128)(2,1)S(1)} %slice.195), channel_id=1, source_target_pairs={{0,16},{16,0},{32,48},{48,32},{64,80},{80,64},{96,112},{112,96},{1... | collective-permute-start | bytes 1572872 | tf_op jit(solution)/shard_map/ppermute | solution.py:9
  45.4 23.5 %all-to-all-start.1 = ((bf16[16,8,2048]{2,1,0:T(8,128)(2,1)}), bf16[16,8,2048]{2,1,0:T(8,128)(2,1)S(1)}, u32[]{:S(2)}, u32[]{:S(2)}) async-start(bf16[16,8,2048]{2,1,0:T(8,128)(2,1)} %fusion.34), calls=%async_computation.1 | async-start | bytes 1048576 | tf_op jit(solution)/shard_map/all_to_all | solution.py:18
  49.0 20.0 %copy-start.6 = (bf16[8,2048]{1,0:T(8,128)(2,1)S(1)}, bf16[8,2048]{1,0:T(8,128)(2,1)}, u32[]{:S(2)}) copy-start(bf16[8,2048]{1,0:T(8,128)(2,1)} %param.11) | copy-start | bytes 98308
  52.3 42.0 %collective-permute-start.2 = (bf16[2048,2,256]{2,0,1:T(8,128)(2,1)}, bf16[2048,2,256]{2,0,1:T(8,128)(2,1)S(1)}, u32[]{:S(2)}, u32[]{:S(2)}) collective-permute-start(bf16[2048,2,256]{2,0,1:T(8,128)(2,1)} %copy.15), channel_id=1, source_target_pairs={{0,16},{16,0},{32,48},{48,32},{64,80},{80,64},{96,112},{112,96},{1... | collective-permute-start | bytes 6291464 | tf_op jit(solution)/shard_map/ppermute | solution.py:9
  70.1 21.6 %all-to-all-start.2 = ((bf16[16,8,2048]{2,1,0:T(8,128)(2,1)}), bf16[16,8,2048]{2,1,0:T(8,128)(2,1)S(1)}, u32[]{:S(2)}, u32[]{:S(2)}) async-start(bf16[16,8,2048]{2,1,0:T(8,128)(2,1)} %broadcast_in_dim.21), calls=%async_computation.2 | async-start | bytes 1048576 | tf_op jit(solution)/shard_map/all_to_all | solution.py:18
  73.7 21.0 %collective-permute-start.3 = (bf16[256,2048]{1,0:T(8,128)(2,1)}, bf16[256,2048]{1,0:T(8,128)(2,1)}, u32[]{:S(2)}, u32[]{:S(2)}) collective-permute-start(bf16[256,2048]{1,0:T(8,128)(2,1)} %param.18), channel_id=1, source_target_pairs={{0,16},{16,0},{32,48},{48,32},{64,80},{80,64},{96,112},{112,96},{1... | collective-permute-start | bytes 3145736 | tf_op jit(solution)/shard_map/ppermute | solution.py:9
  91.8 2.1 copy-start.1
  94.7 30.6 %copy-start.12 = (bf16[2,8,2048]{2,1,0:T(8,128)(2,1)S(1)}, bf16[2,8,2048]{2,1,0:T(8,128)(2,1)}, u32[]{:S(2)}) copy-start(bf16[2,8,2048]{2,1,0:T(8,128)(2,1)} %param.12) | copy-start | bytes 196612
  96.3 50.2 %copy-start.8 = (bf16[256,1,192]{0,2,1:T(8,128)(2,1)S(1)}, bf16[256,1,192]{0,2,1:T(8,128)(2,1)}, u32[]{:S(2)}) copy-start(bf16[256,1,192]{0,2,1:T(8,128)(2,1)} %copy-done.7) | copy-start | bytes 294916
  117.0 8.5 %copy-start.11 = (bf16[8,2048]{1,0:T(8,128)(2,1)}, bf16[8,2048]{1,0:T(8,128)(2,1)S(1)}, u32[]{:S(2)}) copy-start(bf16[8,2048]{1,0:T(8,128)(2,1)S(1)} %fusion.69) | copy-start | bytes 98308
  117.0 8.2 %collective-permute-start.4 = (bf16[8,2048]{1,0:T(8,128)(2,1)S(1)}, bf16[8,2048]{1,0:T(8,128)(2,1)S(1)}, u32[]{:S(2)}, u32[]{:S(2)}) collective-permute-start(bf16[8,2048]{1,0:T(8,128)(2,1)S(1)} %fusion.69), channel_id=1, source_target_pairs={{0,32},{16,48},{32,64},{48,80},{64,96},{80,112},{96,128},{112,144}... | collective-permute-start | bytes 98312 | tf_op jit(solution)/shard_map/ppermute | solution.py:14
  144.4 5.3 %copy-start.5 = (bf16[64,2048]{1,0:T(8,128)(2,1)S(1)}, bf16[64,2048]{1,0:T(8,128)(2,1)}, u32[]{:S(2)}) copy-start(bf16[64,2048]{1,0:T(8,128)(2,1)} %param.16) | copy-start | bytes 786436
  144.4 3.9 %collective-permute-start.5 = (bf16[128,2048]{1,0:T(8,128)(2,1)S(1)}, bf16[128,2048]{1,0:T(8,128)(2,1)S(1)}, u32[]{:S(2)}, u32[]{:S(2)}) collective-permute-start(bf16[128,2048]{1,0:T(8,128)(2,1)S(1)} %bitcast.217), channel_id=1, source_target_pairs={{0,16},{16,0},{32,48},{48,32},{64,80},{80,64},{96,112},{112,96},{1... | collective-permute-start | bytes 1572872 | tf_op jit(solution)/shard_map/ppermute | solution.py:9
  146.8 2.6 %copy-start.16 = (f32[1,64,64]{2,1,0:T(8,128)}, f32[1,64,64]{2,1,0:T(8,128)S(1)}, u32[]{:S(2)}) copy-start(f32[1,64,64]{2,1,0:T(8,128)S(1)} %fusion.18) | copy-start | bytes 49156
  148.9 0.6 copy-start.9
  153.8 3.8 %collective-permute-start.6 = (bf16[128,2048]{1,0:T(8,128)(2,1)S(1)}, bf16[128,2048]{1,0:T(8,128)(2,1)S(1)}, u32[]{:S(2)}, u32[]{:S(2)}) collective-permute-start(bf16[128,2048]{1,0:T(8,128)(2,1)S(1)} %slice.194), channel_id=1, source_target_pairs={{0,16},{16,0},{32,48},{48,32},{64,80},{80,64},{96,112},{112,96},{1... | collective-permute-start | bytes 1572872 | tf_op jit(solution)/shard_map/ppermute | solution.py:9
  159.0 44.2 %copy-start.3 = (bf16[2048,2,256]{2,1,0:T(2,128)(2,1)S(1)}, bf16[2048,2,256]{2,1,0:T(2,128)(2,1)}, u32[]{:S(2)}) copy-start(bf16[2048,2,256]{2,1,0:T(2,128)(2,1)} %param.17) | copy-start | bytes 6291460
  182.1 21.5 %copy-start.2 = (bf16[256,2048]{1,0:T(8,128)(2,1)S(1)}, bf16[256,2048]{1,0:T(8,128)(2,1)}, u32[]{:S(2)}) copy-start(bf16[256,2048]{1,0:T(8,128)(2,1)} %param.18) | copy-start | bytes 3145732
  204.4 6.0 %copy-start.10 = (bf16[256,1,192]{0,2,1:T(8,128)(2,1)S(1)}, bf16[256,1,192]{0,2,1:T(8,128)(2,1)}, u32[]{:S(2)}) copy-start(bf16[256,1,192]{0,2,1:T(8,128)(2,1)} %copy-done.9) | copy-start | bytes 294916
  204.4 6.1 %copy-start.14 = (f32[1,64]{1,0:T(1,128)S(1)}, f32[1,64]{1,0:T(1,128)}, u32[]{:S(2)}) copy-start(f32[1,64]{1,0:T(1,128)} %param.20) | copy-start | bytes 772
  204.4 6.7 %copy-start.17 = (f32[1,64,64]{2,1,0:T(8,128)S(1)}, f32[1,64,64]{2,1,0:T(8,128)}, u32[]{:S(2)}) copy-start(f32[1,64,64]{2,1,0:T(8,128)} %copy-done.16) | copy-start | bytes 49156
  206.8 21.8 %all-to-all-start.7 = ((bf16[16,8,2048]{2,1,0:T(8,128)(2,1)}), bf16[16,8,2048]{2,1,0:T(8,128)(2,1)S(1)}, u32[]{:S(2)}, u32[]{:S(2)}) async-start(bf16[16,8,2048]{2,1,0:T(8,128)(2,1)} %fusion.2), calls=%async_computation.7 | async-start | bytes 1048576 | tf_op jit(solution)/shard_map/all_to_all | solution.py:18

commit v2 on v1

v2 whole, which is shorter than its diff:
```python
import jax
import jax.numpy as jnp
from jax import lax
from jax.sharding import PartitionSpec as P


def swap_halves(value):
    pairs = [(source, source ^ 1) for source in range(lax.axis_size("layer"))]
    return lax.ppermute(value, "layer", pairs)


def next_layer(value):
    count = lax.axis_size("layer")
    return lax.ppermute(value, "layer", [(source, source + 2) for source in range(count - 2)])


def exchange(blocks):
    return lax.all_to_all(blocks, "tp", 0, 0, tiled=True)


def gather_rows(rows):
    members = lax.axis_size("tp")
    blocks = exchange(jnp.broadcast_to(rows[None], (members,) + rows.shape))
    return blocks.reshape((-1, rows.shape[1]))


def scatter_sum(partial):
    members = lax.axis_size("tp")
    blocks = exchange(partial.reshape((members, -1, partial.shape[1])))
    return jnp.sum(blocks.astype(jnp.float32), axis=0)


def rms_norm(values, weight):
    floats = values.astype(jnp.float32)
    scaled = floats * lax.rsqrt(jnp.mean(floats * floats, axis=-1, keepdims=True) + 1e-05)
    return (scaled * weight).astype(jnp.bfloat16)


def lifted(values):
    return jax.nn.elu(values.astype(jnp.float32)) + 1.0


def attend(queries, keyed, valued, memory, totals, logits, allowed):
    head_dim = memory.shape[-1]
    scores = jnp.einsum(
        "qhc,khc->hqk", queries, keyed, preferred_element_type=jnp.float32
    ) * head_dim ** (-0.5)
    probs = jax.nn.softmax(jnp.where(allowed[None], scores, -jnp.inf), axis=-1).astype(jnp.bfloat16)
    direct = jnp.einsum("hqk,khc->qhc", probs, valued, preferred_element_type=jnp.float32)
    lifted_q = lifted(queries)
    numer = jnp.einsum("qhc,hce->qhe", lifted_q, memory, precision=lax.Precision.HIGHEST)
    denom = jnp.einsum("qhc,hc->qh", lifted_q, totals, precision=lax.Precision.HIGHEST)[..., None]
    gate_open = jax.nn.sigmoid(logits)[None, :, None]
    return (gate_open * numer / denom + (1.0 - gate_open) * direct).astype(jnp.bfloat16)


def absorb(keyed, valued, memory, totals):
    lifted_k = lifted(keyed)
    new_memory = memory + jnp.einsum(
        "khc,khe->hce", lifted_k, valued.astype(jnp.float32), precision=lax.Precision.HIGHEST
    )
    return (new_memory, totals + jnp.sum(lifted_k, axis=0))


def body(
    acts,
    fresh,
    norm_first,
    norm_second,
    proj_qkv,
    proj_out,
    proj_gate_up,
    proj_down,
    memory_state,
    memory_norm,
    bias_gate,
):
    position = lax.axis_index("layer")
    half = position % 2
    depth = position // 2
    gain_one = lax.dynamic_index_in_dim(norm_first, depth, 0, keepdims=False)
    gain_two = lax.dynamic_index_in_dim(norm_second, depth, 0, keepdims=False)
    head_dim = memory_state.shape[-1]
    half_len = acts.shape[0] * lax.axis_size("tp")
    logit_row = jnp.broadcast_to(bias_gate[:, None, None], (1, 1, head_dim))
    state = jnp.concatenate([memory_state, memory_norm[:, None], logit_row], axis=1)
    other_state = swap_halves(state)
    wide = lax.optimization_barrier(jnp.transpose(proj_gate_up, (1, 0, 2)))
    qkv_pair, out_pair, wide_pair, down_pair = (
        lax.optimization_barrier(jnp.concatenate([weight, swap_halves(weight)], axis=axis))
        for weight, axis in ((proj_qkv, 0), (proj_out, 0), (wide, 2), (proj_down, 0))
    )
    memory_pair = jnp.concatenate([memory_state, other_state[:, :head_dim]], axis=0)
    totals_pair = jnp.concatenate([memory_norm, other_state[:, head_dim]], axis=0)
    logits = jnp.concatenate([bias_gate, other_state[:, head_dim + 1, 0]], axis=0)
    index = jnp.arange(half_len)
    causal = index[:, None] >= index[None, :]
    allowed = jnp.concatenate([causal, jnp.broadcast_to(half == 1, causal.shape)], axis=1)

    def expand(rows):
        gate, up = (
            jnp.dot(rows, weight, preferred_element_type=jnp.float32) for weight in wide_pair
        )
        return (jax.nn.silu(gate) * up).astype(jnp.bfloat16)

    def apply_layer(rows, memory, totals):
        normed = gather_rows(rms_norm(rows, gain_one))
        both = jnp.einsum(
            "sd,hdc->shc", normed, qkv_pair, preferred_element_type=jnp.float32
        ).astype(jnp.bfloat16)
        swapped = swap_halves(both[:, ::-1, head_dim:])
        queries = both[..., :head_dim]
        keyed = jnp.concatenate([both[..., head_dim : 2 * head_dim], swapped[..., :head_dim]], axis=0)
        valued = jnp.concatenate([both[..., 2 * head_dim :], swapped[..., head_dim:]], axis=0)
        blended = attend(queries, keyed, valued, memory, totals, logits, allowed)
        memory, totals = absorb(keyed, valued, memory, totals)
        attn = jnp.dot(
            blended.reshape(half_len, -1), out_pair, preferred_element_type=jnp.float32
        )
        attn = scatter_sum(attn.astype(jnp.bfloat16))
        hidden_one = (rows.astype(jnp.float32) + attn).astype(jnp.bfloat16)
        normed_two = gather_rows(rms_norm(hidden_one, gain_two))
        down = jnp.dot(expand(normed_two), down_pair, preferred_element_type=jnp.float32)
        ffn = scatter_sum(down.astype(jnp.bfloat16))
        output = (hidden_one.astype(jnp.float32) + ffn).astype(jnp.bfloat16)
        return (output, memory, totals)

    first_rows, memory_one, totals_one = apply_layer(acts, memory_pair, totals_pair)
    incoming = next_layer(first_rows)
    fresh_rows = lax.dynamic_index_in_dim(fresh, half, 0, keepdims=False)
    entering = jnp.where(depth == 0, fresh_rows, incoming)
    second_rows, memory_two, totals_two = apply_layer(entering, memory_one, totals_one)
    return (first_rows, second_rows, memory_two[:1], totals_two[:1])


def solution(mesh):
    in_specs = (
        P(("layer", "tp"), None),
        P(None, "tp", None),
        P(),
        P(),
        P(("layer", "tp"), None, None),
        P(("layer", "tp"), None),
        P(None, None, ("layer", "tp")),
        P(("layer", "tp"), None),
        P(("layer", "tp"), None, None),
        P(("layer", "tp"), None),
        P(("layer", "tp")),
    )
    out_specs = (
        P(("layer", "tp"), None),
        P(("layer", "tp"), None),
        P(("layer", "tp"), None, None),
        P(("layer", "tp"), None),
    )
    return jax.shard_map(body, mesh=mesh, in_specs=in_specs, out_specs=out_specs, check_vma=False)
```

time: 231 us -> 224 us (0.970)
  blocking collectives: 114 us -> 64.4 us
  starting transfers between devices: 26.3 us -> 44.3 us
  waiting for transfers between devices: 57.6 us -> 69.2 us
  other arithmetic: 6.58 us -> 15.3 us
  local copies, waits for them, and re-layouts: 7.48 us -> 11.1 us
    all_to_all x5 -> x3, blocking collectives: 114 us -> 64.4 us  [exchange(): return lax.all_to_all(blocks, 'tp', 0, 0, tiled=True)]
    all_to_all x3 -> x5, waiting for transfers between devices: 46.7 us -> 62.4 us  [exchange(): return lax.all_to_all(blocks, 'tp', 0, 0, tiled=True)]
    all_to_all x3 -> x5, starting transfers between devices: 10.7 us -> 26.3 us  [exchange(): return lax.all_to_all(blocks, 'tp', 0, 0, tiled=True)]
    concatenate x0 -> x6, other arithmetic: none -> 9.63 us  [the longest x4 8.89 us: body(): jnp.concatenate([weight, swap_halves(weight)], axis=axis)]
    ppermute x6 -> x7, waiting for transfers between devices: 6.16 us -> 2.15 us  [swap_halves(): return lax.ppermute(value, 'layer', pairs)]
    ppermute x6 -> x7, starting transfers between devices: 12.1 us -> 14.5 us  [swap_halves(): return lax.ppermute(value, 'layer', pairs)]
    dot_general x14 -> x10, matrix products: 14.3 us -> 12.7 us  [the longest x2 6.38 us: apply_layer(): jnp.dot(expand(normed_two), down_pair, preferred_element_type=jnp.float32)]
    unnamed x37 -> x45, local copies, waits for them, and re-layouts: 3.43 us -> 4.85 us
  transfers between devices with their start and end apart: 10 -> 13, of which waited for: 8 -> 8; matrix products, arithmetic and copies ran while one was open for 4% -> 11% of each run, Pallas kernels for 0% -> 0%
where the time goes in v2:
time: 224 us; the launch traced here: 222 us
  waiting for transfers between devices  69.2 us (31%)
  blocking collectives  64.4 us (29%)
  starting transfers between devices  44.3 us (20%)
  matrix products  16 us (7%)
  other arithmetic  15.3 us (7%)
  local copies, waits for them, and re-layouts  11.1 us (5%)
    all_to_all x3, blocking collectives, exchange(): return lax.all_to_all(blocks, 'tp', 0, 0, tiled=True)  64.4 us
    all_to_all x5, waiting for transfers between devices, exchange(): return lax.all_to_all(blocks, 'tp', 0, 0, tiled=True)  62.4 us
    all_to_all x5, starting transfers between devices, exchange(): return lax.all_to_all(blocks, 'tp', 0, 0, tiled=True)  26.3 us
    ppermute x7, starting transfers between devices, swap_halves(): return lax.ppermute(value, 'layer', pairs)  14.5 us
    concatenate x4, other arithmetic, body(): jnp.concatenate([weight, swap_halves(weight)], axis=axis)  8.89 us
    dot_general x2, matrix products, apply_layer(): jnp.dot(expand(normed_two), down_pair, preferred_element_type=jnp.float32)  6.38 us
    unnamed x45, local copies, waits for them, and re-layouts  4.85 us
    ppermute x1, waiting for transfers between devices, next_layer(): lax.ppermute(value, 'layer', [(source, source + 2) for source in range(co...  4.63 us
  transfers between devices with their start and end apart: 13, of which 8 were waited for; matrix products, arithmetic and copies ran while one was open for 11% of the time, Pallas kernels for 0%

profile of v2, /device:TPU:2, one launch (start us, length us, event | category | flops | bytes accessed | tf_op | source)
XLA Modules:
  0.0 222.4 jit_solution(1770242482941392278)
XLA Ops:
  0.7 2.1 collective-permute-start.1
  5.4 12.0 %all-to-all-start = ((bf16[16,8,2048]{2,1,0:T(8,128)(2,1)}), bf16[16,8,2048]{2,1,0:T(8,128)(2,1)S(1)}, u32[]{:S(2)}, u32[]{:S(2)}) async-start(bf16[16,8,2048]{2,1,0:T(8,128)(2,1)} %broadcast_in_dim.41), calls=%async_computation | async-start | bytes 1048576 | tf_op jit(solution)/shard_map/all_to_all | solution.py:18
  19.8 2.1 collective-permute-start
  21.9 2.2 collective-permute-start.3
  26.2 1.3 broadcast_subtract_fusion
  27.5 1.3 pad_maximum_fusion.2
  28.9 8.5 %all-to-all-done = bf16[16,8,2048]{2,1,0:T(8,128)(2,1)S(1)} async-done(((bf16[16,8,2048]{2,1,0:T(8,128)(2,1)}), bf16[16,8,2048]{2,1,0:T(8,128)(2,1)S(1)}, u32[]{:S(2)}, u32[]{:S(2)}) %all-to-all-start) | async-done | bytes 524320 | tf_op jit(solution)/shard_map/all_to_all | solution.py:18
  38.2 1.9 collective-permute-start.2
  42.6 1.1 fusion.2
  43.8 3.6 %all-to-all-start.1 = ((bf16[16,8,2048]{2,1,0:T(8,128)(2,1)}), bf16[16,8,2048]{2,1,0:T(8,128)(2,1)S(1)}, u32[]{:S(2)}, u32[]{:S(2)}) async-start(bf16[16,8,2048]{2,1,0:T(8,128)(2,1)} %fusion.2), calls=%async_computation.1 | async-start | bytes 1048576 | tf_op jit(solution)/shard_map/all_to_all | solution.py:18
  47.4 3.2 %copy.35 = bf16[2048,2,256]{2,0,1:T(8,128)(2,1)} copy(bf16[2048,2,256]{2,1,0:T(2,128)(2,1)} %param.17) | data formatting | bytes 4194304 | tf_op args[6]
  50.6 2.1 collective-permute-start.4
  52.6 2.3 %collective-permute-start.5 = (bf16[256,2048]{1,0:T(8,128)(2,1)}, bf16[256,2048]{1,0:T(8,128)(2,1)}, u32[]{:S(2)}, u32[]{:S(2)}) collective-permute-start(bf16[256,2048]{1,0:T(8,128)(2,1)} %param.18), channel_id=1, source_target_pairs={{0,16},{16,0},{32,48},{48,32},{64,80},{80,64},{96,112},{112,96},{1... | collective-permute-start | bytes 3145736 | tf_op jit(solution)/shard_map/ppermute | solution.py:9
  55.8 11.6 %all-to-all-done.1 = bf16[16,8,2048]{2,1,0:T(8,128)(2,1)S(1)} async-done(((bf16[16,8,2048]{2,1,0:T(8,128)(2,1)}), bf16[16,8,2048]{2,1,0:T(8,128)(2,1)S(1)}, u32[]{:S(2)}, u32[]{:S(2)}) %all-to-all-start.1) | async-done | bytes 524320 | tf_op jit(solution)/shard_map/all_to_all | solution.py:18
  68.5 3.6 %all-to-all-start.2 = ((bf16[16,8,2048]{2,1,0:T(8,128)(2,1)}), bf16[16,8,2048]{2,1,0:T(8,128)(2,1)S(1)}, u32[]{:S(2)}, u32[]{:S(2)}) async-start(bf16[16,8,2048]{2,1,0:T(8,128)(2,1)} %broadcast_in_dim.44), calls=%async_computation.2 | async-start | bytes 1048576 | tf_op jit(solution)/shard_map/all_to_all | solution.py:18
  72.1 3.1 %pad_maximum_fusion.1 = bf16[512,2048]{1,0:T(8,128)(2,1)} fusion(bf16[256,2048]{1,0:T(8,128)(2,1)} %collective-permute-done.5, bf16[256,2048]{1,0:T(8,128)(2,1)} %param.18), kind=kLoop, calls=%fused_computation.13 | loop fusion | flops 4194304 | bytes 4194304 | tf_op jit(solution)/shard_map/concatenate | solution.py:90
  75.2 4.4 %pad_maximum_fusion = bf16[2,2048,512]{2,1,0:T(8,128)(2,1)} fusion(bf16[2,2048,256]{2,1,0:T(8,128)(2,1)} %collective-permute-done.4, bf16[2,2048,256]{2,1,0:T(8,128)(2,1)} %bitcast.115), kind=kLoop, calls=%fused_computation.2 | loop fusion | flops 8388608 | bytes 8388608 | tf_op jit(solution)/shard_map/concatenate | solution.py:90
  79.7 10.4 %all-to-all-done.2 = bf16[16,8,2048]{2,1,0:T(8,128)(2,1)S(1)} async-done(((bf16[16,8,2048]{2,1,0:T(8,128)(2,1)}), bf16[16,8,2048]{2,1,0:T(8,128)(2,1)S(1)}, u32[]{:S(2)}, u32[]{:S(2)}) %all-to-all-start.2) | async-done | bytes 524320 | tf_op jit(solution)/shard_map/all_to_all | solution.py:18
  90.1 2.7 %fusion.7 = f32[128,512]{1,0:T(8,128)} fusion(bf16[2,2048,512]{2,1,0:T(8,128)(2,1)} %pad_maximum_fusion, bf16[16,8,2048]{2,1,0:T(8,128)(2,1)S(1)} %all-to-all-done.2), kind=kOutput, calls=%fused_computation.16 | convolution fusion | flops 268435456 | bytes 2883584 | tf_op jit(solution)/shard_map/dot_general | solution.py:102
  92.9 3.2 %fusion.3 = bf16[16,8,2048]{2,1,0:T(8,128)(2,1)S(1)} fusion(bf16[512,2048]{1,0:T(8,128)(2,1)} %pad_maximum_fusion.1, f32[128,512]{1,0:T(8,128)} %fusion.7, bf16[2,2048,512]{2,1,0:T(8,128)(2,1)} %pad_maximum_fusion, bf16[16,8,2048]{2,1,0:T(8,128)(2,1)S(1)} %all-to-all-done.2), kind=kOutput, calls=%fused_computation.8 | convolution fusion | flops 537526272 | bytes 5505024 | tf_op jit(solution)/shard_map/dot_general | solution.py:123
  96.1 20.5 %all_to_all.40 = bf16[16,8,2048]{2,1,0:T(8,128)(2,1)S(1)} all-to-all(bf16[16,8,2048]{2,1,0:T(8,128)(2,1)S(1)} %fusion.3), channel_id=1, replica_groups=mesh['layer'=32,'tp'=16] {'tp'}, dimensions={0} | all-to-all | bytes 1048576 | tf_op jit(solution)/shard_map/all_to_all | solution.py:18
  116.7 3.5 %collective-permute-start.6 = (bf16[8,2048]{1,0:T(8,128)(2,1)S(1)}, bf16[8,2048]{1,0:T(8,128)(2,1)S(1)}, u32[]{:S(2)}, u32[]{:S(2)}) collective-permute-start(bf16[8,2048]{1,0:T(8,128)(2,1)S(1)} %fusion.60), channel_id=1, source_target_pairs={{0,32},{16,48},{32,64},{48,80},{64,96},{80,112},{96,128},{112,144}... | collective-permute-start | bytes 98312 | tf_op jit(solution)/shard_map/ppermute | solution.py:14
  120.2 4.6 %collective-permute-done.6 = bf16[8,2048]{1,0:T(8,128)(2,1)S(1)} collective-permute-done((bf16[8,2048]{1,0:T(8,128)(2,1)S(1)}, bf16[8,2048]{1,0:T(8,128)(2,1)S(1)}, u32[]{:S(2)}, u32[]{:S(2)}) %collective-permute-start.6) | collective-permute-done | bytes 32800 | tf_op jit(solution)/shard_map/ppermute | solution.py:14
  126.6 3.6 %all-to-all-start.4 = ((bf16[16,8,2048]{2,1,0:T(8,128)(2,1)}), bf16[16,8,2048]{2,1,0:T(8,128)(2,1)S(1)}, u32[]{:S(2)}, u32[]{:S(2)}) async-start(bf16[16,8,2048]{2,1,0:T(8,128)(2,1)} %broadcast_in_dim.45), calls=%async_computation.4 | async-start | bytes 1048576 | tf_op jit(solution)/shard_map/all_to_all | solution.py:18
  130.7 15.1 %all-to-all-done.4 = bf16[16,8,2048]{2,1,0:T(8,128)(2,1)S(1)} async-done(((bf16[16,8,2048]{2,1,0:T(8,128)(2,1)}), bf16[16,8,2048]{2,1,0:T(8,128)(2,1)S(1)}, u32[]{:S(2)}, u32[]{:S(2)}) %all-to-all-start.4) | async-done | bytes 524320 | tf_op jit(solution)/shard_map/all_to_all | solution.py:18
  146.4 1.9 collective-permute-start.7
  148.4 1.2 collective-permute-done.7
  151.8 22.9 %all_to_all.41 = bf16[16,8,2048]{2,1,0:T(8,128)(2,1)S(1)} all-to-all(bf16[16,8,2048]{2,1,0:T(8,128)(2,1)S(1)} %fusion.4), channel_id=1, replica_groups=mesh['layer'=32,'tp'=16] {'tp'}, dimensions={0} | all-to-all | bytes 1048576 | tf_op jit(solution)/shard_map/all_to_all | solution.py:18
  175.1 21.1 %all_to_all.42 = bf16[16,8,2048]{2,1,0:T(8,128)(2,1)S(1)} all-to-all(bf16[16,8,2048]{2,1,0:T(8,128)(2,1)S(1)} %broadcast_in_dim.46), channel_id=1, replica_groups=mesh['layer'=32,'tp'=16] {'tp'}, dimensions={0} | all-to-all | bytes 1048576 | tf_op jit(solution)/shard_map/all_to_all | solution.py:18
  196.6 3.2 %fusion.5 = bf16[16,8,2048]{2,1,0:T(8,128)(2,1)} fusion(bf16[512,2048]{1,0:T(8,128)(2,1)S(1)} %copy-done.2, f32[128,512]{1,0:T(8,128)S(1)} %fusion.6, bf16[2,2048,512]{2,1,0:T(8,128)(2,1)} %pad_maximum_fusion, bf16[16,8,2048]{2,1,0:T(8,128)(2,1)S(1)} %all_to_all.42), kind=kOutput, calls=%fused_computation.10 | convolution fusion | flops 537526272 | bytes 5505024 | tf_op jit(solution)/shard_map/dot_general | solution.py:123
  199.8 3.6 %all-to-all-start.7 = ((bf16[16,8,2048]{2,1,0:T(8,128)(2,1)}), bf16[16,8,2048]{2,1,0:T(8,128)(2,1)S(1)}, u32[]{:S(2)}, u32[]{:S(2)}) async-start(bf16[16,8,2048]{2,1,0:T(8,128)(2,1)} %fusion.5), calls=%async_computation.7 | async-start | bytes 1048576 | tf_op jit(solution)/shard_map/all_to_all | solution.py:18
  204.9 16.8 %all-to-all-done.7 = bf16[16,8,2048]{2,1,0:T(8,128)(2,1)S(1)} async-done(((bf16[16,8,2048]{2,1,0:T(8,128)(2,1)}), bf16[16,8,2048]{2,1,0:T(8,128)(2,1)S(1)}, u32[]{:S(2)}, u32[]{:S(2)}) %all-to-all-start.7) | async-done | bytes 524320 | tf_op jit(solution)/shard_map/all_to_all | solution.py:18
  (114 shorter events, 19.9 us)
Async XLA Ops:
  0.6 3.0 %copy-start = (f32[16,2048]{1,0:T(8,128)S(1)}, f32[16,2048]{1,0:T(8,128)}, u32[]{:S(2)}) copy-start(f32[16,2048]{1,0:T(8,128)} %param.13) | copy-start | bytes 393220
  0.6 26.9 %copy-start.3 = (bf16[1,2048,192]{1,2,0:T(8,128)(2,1)S(1)}, bf16[1,2048,192]{1,2,0:T(8,128)(2,1)}, u32[]{:S(2)}) copy-start(bf16[1,2048,192]{1,2,0:T(8,128)(2,1)} %param.15) | copy-start | bytes 2359300
  0.7 26.8 %copy-start.6 = (bf16[64,2048]{1,0:T(8,128)(2,1)S(1)}, bf16[64,2048]{1,0:T(8,128)(2,1)}, u32[]{:S(2)}) copy-start(bf16[64,2048]{1,0:T(8,128)(2,1)} %param.16) | copy-start | bytes 786436
  0.7 26.9 %collective-permute-start.1 = (bf16[1,2048,192]{1,2,0:T(8,128)(2,1)}, bf16[1,2048,192]{1,2,0:T(8,128)(2,1)}, u32[]{:S(2)}, u32[]{:S(2)}) collective-permute-start(bf16[1,2048,192]{1,2,0:T(8,128)(2,1)} %param.15), channel_id=1, source_target_pairs={{0,16},{16,0},{32,48},{48,32},{64,80},{80,64},{96,112},{112,96},{1... | collective-permute-start | bytes 2359304 | tf_op jit(solution)/shard_map/ppermute | solution.py:9
  5.4 32.0 %all-to-all-start = ((bf16[16,8,2048]{2,1,0:T(8,128)(2,1)}), bf16[16,8,2048]{2,1,0:T(8,128)(2,1)S(1)}, u32[]{:S(2)}, u32[]{:S(2)}) async-start(bf16[16,8,2048]{2,1,0:T(8,128)(2,1)} %broadcast_in_dim.41), calls=%async_computation | async-start | bytes 1048576 | tf_op jit(solution)/shard_map/all_to_all | solution.py:18
  18.9 8.5 %copy-start.7 = (f32[1,64,64]{1,2,0:T(8,128)}, f32[1,64,64]{1,2,0:T(8,128)S(1)}, u32[]{:S(2)}) copy-start(f32[1,64,64]{1,2,0:T(8,128)S(1)} %copy.21) | copy-start | bytes 49156
  19.8 5.0 %collective-permute-start = (f32[1,66,64]{1,2,0:T(8,128)S(1)}, f32[1,66,64]{1,2,0:T(8,128)S(1)}, u32[]{:S(2)}, u32[]{:S(2)}) collective-permute-start(f32[1,66,64]{1,2,0:T(8,128)S(1)} %maximum_maximum_fusion), channel_id=1, source_target_pairs={{0,16},{16,0},{32,48},{48,32},{64,80},{80,64},{96,112},{112,96},{1... | collective-permute-start | bytes 50696 | tf_op jit(solution)/shard_map/ppermute | solution.py:9
  21.9 5.6 %collective-permute-start.3 = (bf16[64,2048]{1,0:T(8,128)(2,1)}, bf16[64,2048]{1,0:T(8,128)(2,1)S(1)}, u32[]{:S(2)}, u32[]{:S(2)}) collective-permute-start(bf16[64,2048]{1,0:T(8,128)(2,1)} %param.16), channel_id=1, source_target_pairs={{0,16},{16,0},{32,48},{48,32},{64,80},{80,64},{96,112},{112,96},{1... | collective-permute-start | bytes 786440 | tf_op jit(solution)/shard_map/ppermute | solution.py:9
  28.8 11.3 %copy-start.8 = (f32[1,64,64]{1,2,0:T(8,128)S(1)}, f32[1,64,64]{1,2,0:T(8,128)}, u32[]{:S(2)}) copy-start(f32[1,64,64]{1,2,0:T(8,128)} %copy-done.7) | copy-start | bytes 49156
  28.8 11.3 %copy-start.10 = (f32[1,66,64]{1,2,0:T(8,128)S(1)}, f32[1,66,64]{1,2,0:T(8,128)}, u32[]{:S(2)}) copy-start(f32[1,66,64]{1,2,0:T(8,128)} %copy-done.9) | copy-start | bytes 50692
  28.9 11.3 %copy-start.19 = (f32[2]{0:T(128)S(1)}, f32[2]{0:T(128)}, u32[]{:S(2)}) copy-start(f32[2]{0:T(128)} %get-tuple-element.21) | copy-start | bytes 28
  28.9 12.5 %copy-start.4 = (pred[128,256]{1,0:T(8,128)(4,1)S(1)}, pred[128,256]{1,0:T(8,128)(4,1)}, u32[]{:S(2)}) copy-start(pred[128,256]{1,0:T(8,128)(4,1)} %concatenate.55) | copy-start | bytes 98308
  37.4 4.7 %copy-start.17 = (f32[2]{0:T(128)S(1)}, f32[2]{0:T(128)}, u32[]{:S(2)}) copy-start(f32[2]{0:T(128)} %get-tuple-element.20) | copy-start | bytes 28
  38.2 3.1 %collective-permute-start.2 = (bf16[128,2,128]{0,2,1:T(8,128)(2,1)S(1)}, bf16[128,2,128]{0,2,1:T(8,128)(2,1)S(1)}, u32[]{:S(2)}, u32[]{:S(2)}) collective-permute-start(bf16[128,2,128]{0,2,1:T(8,128)(2,1)S(1)} %rev.6), channel_id=1, source_target_pairs={{0,16},{16,0},{32,48},{48,32},{64,80},{80,64},{96,112},{112,96},{1... | collective-permute-start | bytes 196616 | tf_op jit(solution)/shard_map/ppermute | solution.py:9
  40.4 3.4 %copy-start.12 = (bf16[128,2,64]{0,2,1:T(8,128)(2,1)}, bf16[128,2,64]{0,2,1:T(8,128)(2,1)S(1)}, u32[]{:S(2)}) copy-start(bf16[128,2,64]{0,2,1:T(8,128)(2,1)S(1)} %get-tuple-element.24) | copy-start | bytes 98308
  43.8 23.6 %all-to-all-start.1 = ((bf16[16,8,2048]{2,1,0:T(8,128)(2,1)}), bf16[16,8,2048]{2,1,0:T(8,128)(2,1)S(1)}, u32[]{:S(2)}, u32[]{:S(2)}) async-start(bf16[16,8,2048]{2,1,0:T(8,128)(2,1)} %fusion.2), calls=%async_computation.1 | async-start | bytes 1048576 | tf_op jit(solution)/shard_map/all_to_all | solution.py:18
  47.4 20.1 %copy-start.5 = (bf16[8,2048]{1,0:T(8,128)(2,1)S(1)}, bf16[8,2048]{1,0:T(8,128)(2,1)}, u32[]{:S(2)}) copy-start(bf16[8,2048]{1,0:T(8,128)(2,1)} %param.11) | copy-start | bytes 98308
  50.6 24.7 %collective-permute-start.4 = (bf16[2,2048,256]{2,1,0:T(8,128)(2,1)}, bf16[2,2048,256]{2,1,0:T(8,128)(2,1)}, u32[]{:S(2)}, u32[]{:S(2)}) collective-permute-start(bf16[2,2048,256]{2,1,0:T(8,128)(2,1)} %bitcast.115), channel_id=1, source_target_pairs={{0,16},{16,0},{32,48},{48,32},{64,80},{80,64},{96,112},{112,96},{1... | collective-permute-start | bytes 6291464 | tf_op jit(solution)/shard_map/ppermute | solution.py:9
  52.6 19.5 %collective-permute-start.5 = (bf16[256,2048]{1,0:T(8,128)(2,1)}, bf16[256,2048]{1,0:T(8,128)(2,1)}, u32[]{:S(2)}, u32[]{:S(2)}) collective-permute-start(bf16[256,2048]{1,0:T(8,128)(2,1)} %param.18), channel_id=1, source_target_pairs={{0,16},{16,0},{32,48},{48,32},{64,80},{80,64},{96,112},{112,96},{1... | collective-permute-start | bytes 3145736 | tf_op jit(solution)/shard_map/ppermute | solution.py:9
  68.5 21.6 %all-to-all-start.2 = ((bf16[16,8,2048]{2,1,0:T(8,128)(2,1)}), bf16[16,8,2048]{2,1,0:T(8,128)(2,1)S(1)}, u32[]{:S(2)}, u32[]{:S(2)}) async-start(bf16[16,8,2048]{2,1,0:T(8,128)(2,1)} %broadcast_in_dim.44), calls=%async_computation.2 | async-start | bytes 1048576 | tf_op jit(solution)/shard_map/all_to_all | solution.py:18
  116.5 13.8 %copy-start.13 = (bf16[128,2,64]{0,2,1:T(8,128)(2,1)S(1)}, bf16[128,2,64]{0,2,1:T(8,128)(2,1)}, u32[]{:S(2)}) copy-start(bf16[128,2,64]{0,2,1:T(8,128)(2,1)} %copy-done.12) | copy-start | bytes 98308
  116.5 13.8 %copy-start.15 = (bf16[128,2,64]{0,2,1:T(8,128)(2,1)S(1)}, bf16[128,2,64]{0,2,1:T(8,128)(2,1)}, u32[]{:S(2)}) copy-start(bf16[128,2,64]{0,2,1:T(8,128)(2,1)} %copy-done.14) | copy-start | bytes 98308
  116.6 29.7 %copy-start.11 = (bf16[8,2048]{1,0:T(8,128)(2,1)}, bf16[8,2048]{1,0:T(8,128)(2,1)S(1)}, u32[]{:S(2)}) copy-start(bf16[8,2048]{1,0:T(8,128)(2,1)S(1)} %fusion.60) | copy-start | bytes 98308
  116.7 8.1 %collective-permute-start.6 = (bf16[8,2048]{1,0:T(8,128)(2,1)S(1)}, bf16[8,2048]{1,0:T(8,128)(2,1)S(1)}, u32[]{:S(2)}, u32[]{:S(2)}) collective-permute-start(bf16[8,2048]{1,0:T(8,128)(2,1)S(1)} %fusion.60), channel_id=1, source_target_pairs={{0,32},{16,48},{32,64},{48,80},{64,96},{80,112},{96,128},{112,144}... | collective-permute-start | bytes 98312 | tf_op jit(solution)/shard_map/ppermute | solution.py:14
  126.6 19.2 %all-to-all-start.4 = ((bf16[16,8,2048]{2,1,0:T(8,128)(2,1)}), bf16[16,8,2048]{2,1,0:T(8,128)(2,1)S(1)}, u32[]{:S(2)}, u32[]{:S(2)}) async-start(bf16[16,8,2048]{2,1,0:T(8,128)(2,1)} %broadcast_in_dim.45), calls=%async_computation.4 | async-start | bytes 1048576 | tf_op jit(solution)/shard_map/all_to_all | solution.py:18
  130.6 19.8 %copy-start.16 = (f32[1,64]{1,0:T(1,128)S(1)}, f32[1,64]{1,0:T(1,128)}, u32[]{:S(2)}) copy-start(f32[1,64]{1,0:T(1,128)} %param.20) | copy-start | bytes 772
  130.7 20.0 %copy-start.20 = (f32[2]{0:T(128)S(1)}, f32[2]{0:T(128)}, u32[]{:S(2)}) copy-start(f32[2]{0:T(128)} %get-tuple-element.21) | copy-start | bytes 28
  130.7 20.2 %copy-start.18 = (f32[2]{0:T(128)S(1)}, f32[2]{0:T(128)}, u32[]{:S(2)}) copy-start(f32[2]{0:T(128)} %get-tuple-element.20) | copy-start | bytes 28
  146.4 3.1 %collective-permute-start.7 = (bf16[128,2,128]{0,2,1:T(8,128)(2,1)S(1)}, bf16[128,2,128]{0,2,1:T(8,128)(2,1)S(1)}, u32[]{:S(2)}, u32[]{:S(2)}) collective-permute-start(bf16[128,2,128]{0,2,1:T(8,128)(2,1)S(1)} %rev.7), channel_id=1, source_target_pairs={{0,16},{16,0},{32,48},{48,32},{64,80},{80,64},{96,112},{112,96},{1... | collective-permute-start | bytes 196616 | tf_op jit(solution)/shard_map/ppermute | solution.py:9
  151.5 44.7 %copy-start.1 = (bf16[2,2048,512]{2,1,0:T(8,128)(2,1)S(1)}, bf16[2,2048,512]{2,1,0:T(8,128)(2,1)}, u32[]{:S(2)}) copy-start(bf16[2,2048,512]{2,1,0:T(8,128)(2,1)} %pad_maximum_fusion) | copy-start | bytes 12582916
  175.1 21.5 %copy-start.2 = (bf16[512,2048]{1,0:T(8,128)(2,1)S(1)}, bf16[512,2048]{1,0:T(8,128)(2,1)}, u32[]{:S(2)}) copy-start(bf16[512,2048]{1,0:T(8,128)(2,1)} %pad_maximum_fusion.1) | copy-start | bytes 6291460
  199.8 21.8 %all-to-all-start.7 = ((bf16[16,8,2048]{2,1,0:T(8,128)(2,1)}), bf16[16,8,2048]{2,1,0:T(8,128)(2,1)S(1)}, u32[]{:S(2)}, u32[]{:S(2)}) async-start(bf16[16,8,2048]{2,1,0:T(8,128)(2,1)} %fusion.5), calls=%async_computation.7 | async-start | bytes 1048576 | tf_op jit(solution)/shard_map/all_to_all | solution.py:18
  (2 other events, 5.1 us)

commit v3 on v2

--- a/solution.py
+++ b/solution.py
@@ -1,6 +1,8 @@
 import jax
 import jax.numpy as jnp
 from jax import lax
+from jax.experimental import pallas as pl
+from jax.experimental.pallas import tpu as pltpu
 from jax.sharding import PartitionSpec as P
 
 
@@ -24,10 +26,53 @@
     return blocks.reshape((-1, rows.shape[1]))
 
 
-def scatter_sum(partial):
+def scatter_sum(partial, *beside):
     members = lax.axis_size("tp")
     blocks = exchange(partial.reshape((members, -1, partial.shape[1])))
-    return jnp.sum(blocks.astype(jnp.float32), axis=0)
+    if beside:
+        blocks, *beside = lax.optimization_barrier((blocks, *beside))
+    return (jnp.sum(blocks.astype(jnp.float32), axis=0), *beside)
+
+
+def feed_kernel(rows_ref, wide_ref, down_ref, out_ref, total_ref):
+    step = pl.program_id(0)
+    gate, up = (
+        jnp.dot(rows_ref[...], wide_ref[0, part], preferred_element_type=jnp.float32)
+        for part in range(2)
+    )
+    hidden = (jax.nn.silu(gate) * up).astype(jnp.bfloat16)
+    term = jnp.dot(hidden, down_ref[0], preferred_element_type=jnp.float32)
+
+    @pl.when(step == 0)
+    def _():
+        total_ref[...] = term
+
+    @pl.when(step > 0)
+    def _():
+        total_ref[...] += term
+
+    @pl.when(step == pl.num_programs(0) - 1)
+    def _():
+        out_ref[...] = total_ref[...].astype(out_ref.dtype)
+
+
+def feed_forward(rows, wide_pair, down_pair, cut=2):
+    count, width = rows.shape
+    sources, _, _, units = wide_pair.shape
+    block = units // cut
+    return pl.pallas_call(
+        feed_kernel,
+        grid=(sources * cut,),
+        out_shape=jax.ShapeDtypeStruct((count, width), rows.dtype),
+        in_specs=[
+            pl.BlockSpec((count, width), lambda i: (0, 0)),
+            pl.BlockSpec((1, 2, width, block), lambda i: (i // cut, 0, 0, i % cut)),
+            pl.BlockSpec((1, block, width), lambda i: (i // cut, i % cut, 0)),
+        ],
+        out_specs=pl.BlockSpec((count, width), lambda i: (0, 0)),
+        scratch_shapes=[pltpu.VMEM((count, width), jnp.float32)],
+        name="feed_forward",
+    )(rows, wide_pair, down_pair)
 
 
 def rms_norm(values, weight):
@@ -85,11 +130,16 @@
     logit_row = jnp.broadcast_to(bias_gate[:, None, None], (1, 1, head_dim))
     state = jnp.concatenate([memory_state, memory_norm[:, None], logit_row], axis=1)
     other_state = swap_halves(state)
+    other_qkv = swap_halves(proj_qkv)
+    out_pair = lax.optimization_barrier(
+        jnp.concatenate([proj_out, swap_halves(proj_out)], axis=0)
+    )
     wide = lax.optimization_barrier(jnp.transpose(proj_gate_up, (1, 0, 2)))
-    qkv_pair, out_pair, wide_pair, down_pair = (
-        lax.optimization_barrier(jnp.concatenate([weight, swap_halves(weight)], axis=axis))
-        for weight, axis in ((proj_qkv, 0), (proj_out, 0), (wide, 2), (proj_down, 0))
-    )
+    wide_pair, down_pair = (
+        lax.optimization_barrier(jnp.stack([weight, swap_halves(weight)], axis=0))
+        for weight in (wide, proj_down)
+    )
+    fresh_rows = lax.dynamic_index_in_dim(fresh, half, 0, keepdims=False)
     memory_pair = jnp.concatenate([memory_state, other_state[:, :head_dim]], axis=0)
     totals_pair = jnp.concatenate([memory_norm, other_state[:, head_dim]], axis=0)
     logits = jnp.concatenate([bias_gate, other_state[:, head_dim + 1, 0]], axis=0)
@@ -97,18 +147,15 @@
     causal = index[:, None] >= index[None, :]
     allowed = jnp.concatenate([causal, jnp.broadcast_to(half == 1, causal.shape)], axis=1)
 
-    def expand(rows):
-        gate, up = (
-            jnp.dot(rows, weight, preferred_element_type=jnp.float32) for weight in wide_pair
-        )
-        return (jax.nn.silu(gate) * up).astype(jnp.bfloat16)
-
-    def apply_layer(rows, memory, totals):
+    def project(rows, weight):
+        return jnp.dot(rows, weight[0], preferred_element_type=jnp.float32).astype(jnp.bfloat16)
+
+    def apply_layer(rows, memory, totals, *beside):
         normed = gather_rows(rms_norm(rows, gain_one))
-        both = jnp.einsum(
-            "sd,hdc->shc", normed, qkv_pair, preferred_element_type=jnp.float32
-        ).astype(jnp.bfloat16)
-        swapped = swap_halves(both[:, ::-1, head_dim:])
+        own = project(normed, proj_qkv)
+        other = project(normed, other_qkv)
+        swapped = swap_halves(jnp.stack([other[:, head_dim:], own[:, head_dim:]], axis=1))
+        both = jnp.stack([own, other], axis=1)
         queries = both[..., :head_dim]
         keyed = jnp.concatenate([both[..., head_dim : 2 * head_dim], swapped[..., :head_dim]], axis=0)
         valued = jnp.concatenate([both[..., 2 * head_dim :], swapped[..., head_dim:]], axis=0)
@@ -117,17 +164,19 @@
         attn = jnp.dot(
             blended.reshape(half_len, -1), out_pair, preferred_element_type=jnp.float32
         )
-        attn = scatter_sum(attn.astype(jnp.bfloat16))
+        attn, memory, totals, *beside = scatter_sum(
+            attn.astype(jnp.bfloat16), memory, totals, *beside
+        )
         hidden_one = (rows.astype(jnp.float32) + attn).astype(jnp.bfloat16)
         normed_two = gather_rows(rms_norm(hidden_one, gain_two))
-        down = jnp.dot(expand(normed_two), down_pair, preferred_element_type=jnp.float32)
-        ffn = scatter_sum(down.astype(jnp.bfloat16))
+        (ffn,) = scatter_sum(feed_forward(normed_two, wide_pair, down_pair))
         output = (hidden_one.astype(jnp.float32) + ffn).astype(jnp.bfloat16)
-        return (output, memory, totals)
-
-    first_rows, memory_one, totals_one = apply_layer(acts, memory_pair, totals_pair)
+        return (output, memory, totals, *beside)
+
+    first_rows, memory_one, totals_one, fresh_rows = apply_layer(
+        acts, memory_pair, totals_pair, fresh_rows
+    )
     incoming = next_layer(first_rows)
-    fresh_rows = lax.dynamic_index_in_dim(fresh, half, 0, keepdims=False)
     entering = jnp.where(depth == 0, fresh_rows, incoming)
     second_rows, memory_two, totals_two = apply_layer(entering, memory_one, totals_one)
     return (first_rows, second_rows, memory_two[:1], totals_two[:1])

time: 224 us -> 225 us (level)
  Pallas kernels: 0 us -> 12.3 us
  matrix products: 16 us -> 9.07 us
  blocking collectives: 64.4 us -> 59.6 us
  waiting for transfers between devices: 69.2 us -> 72.2 us
    pallas_call x0 -> x2, Pallas kernels: none -> 12.3 us  [feed_forward(): pl.pallas_call(feed_kernel, grid=(sources * cut,), out_shape=jax.ShapeDty...]
    concatenate x5 -> x1, other arithmetic: 9.56 us -> 0.04 us  [body(): jnp.concatenate([proj_out, swap_halves(proj_out)], axis=0)]
    dot_general x4, matrix products: 9.57 us -> 1.46 us  [project(): jnp.dot(rows, weight[0], preferred_element_type=jnp.float32)]
    another operation x0 -> x6, other arithmetic: none -> 7 us  [the longest x2 6.96 us: body(): jnp.stack([weight, swap_halves(weight)], axis=0)]
    all_to_all x3, blocking collectives: 64.4 us -> 59.6 us  [exchange(): return lax.all_to_all(blocks, 'tp', 0, 0, tiled=True)]
    all_to_all x5, waiting for transfers between devices: 62.4 us -> 65.4 us  [exchange(): return lax.all_to_all(blocks, 'tp', 0, 0, tiled=True)]
    unnamed x45 -> x47, local copies, waits for them, and re-layouts: 4.85 us -> 4.11 us
  transfers between devices with their start and end apart: 13 -> 13, of which waited for: 8 -> 9; matrix products, arithmetic and copies ran while one was open for 11% -> 8% of each run, Pallas kernels for 0% -> 0%
where the time goes in v3:
time: 225 us; the launch traced here: 223 us
  waiting for transfers between devices  72.2 us (32%)
  blocking collectives  59.6 us (26%)
  starting transfers between devices  45.5 us (20%)
  other arithmetic  13.2 us (6%)
  Pallas kernels  12.3 us (5%)
  local copies, waits for them, and re-layouts  9.54 us (4%)
  matrix products  9.07 us (4%)
    all_to_all x5, waiting for transfers between devices, exchange(): return lax.all_to_all(blocks, 'tp', 0, 0, tiled=True)  65.4 us
    all_to_all x3, blocking collectives, exchange(): return lax.all_to_all(blocks, 'tp', 0, 0, tiled=True)  59.6 us
    all_to_all x5, starting transfers between devices, exchange(): return lax.all_to_all(blocks, 'tp', 0, 0, tiled=True)  27.6 us
    ppermute x7, starting transfers between devices, swap_halves(): return lax.ppermute(value, 'layer', pairs)  14.4 us
    pallas_call x2, Pallas kernels, feed_forward(): pl.pallas_call(feed_kernel, grid=(sources * cut,), out_shape=jax.ShapeDty...  12.3 us
    another operation x2, other arithmetic, body(): jnp.stack([weight, swap_halves(weight)], axis=0)  6.96 us
    ppermute x1, waiting for transfers between devices, next_layer(): lax.ppermute(value, 'layer', [(source, source + 2) for source in range(co...  4.63 us
  transfers between devices with their start and end apart: 13, of which 9 were waited for; matrix products, arithmetic and copies ran while one was open for 8% of the time, Pallas kernels for 0%

profile of v3, /device:TPU:2, one launch (start us, length us, event | category | flops | bytes accessed | tf_op | source)
XLA Modules:
  0.0 223.3 jit_solution(11102592952944459861)
XLA Ops:
  4.2 12.0 %all-to-all-start = ((bf16[16,8,2048]{2,1,0:T(8,128)(2,1)}), bf16[16,8,2048]{2,1,0:T(8,128)(2,1)S(1)}, u32[]{:S(2)}, u32[]{:S(2)}) async-start(bf16[16,8,2048]{2,1,0:T(8,128)(2,1)} %broadcast_in_dim.41), calls=%async_computation | async-start | bytes 1048576 | tf_op jit(solution)/shard_map/all_to_all | solution.py:20
  16.2 1.9 collective-permute-start.1
  20.5 2.4 %collective-permute-start = (f32[1,66,64]{1,2,0:T(8,128)S(1)}, f32[1,66,64]{1,2,0:T(8,128)S(1)}, u32[]{:S(2)}, u32[]{:S(2)}) collective-permute-start(f32[1,66,64]{1,2,0:T(8,128)S(1)} %maximum_maximum_fusion), channel_id=1, source_target_pairs={{0,16},{16,0},{32,48},{48,32},{64,80},{80,64},{96,112},{112,96},{1... | collective-permute-start | bytes 50696 | tf_op jit(solution)/shard_map/ppermute | solution.py:11
  22.9 1.9 collective-permute-start.3
  26.7 8.3 %all-to-all-done = bf16[16,8,2048]{2,1,0:T(8,128)(2,1)S(1)} async-done(((bf16[16,8,2048]{2,1,0:T(8,128)(2,1)}), bf16[16,8,2048]{2,1,0:T(8,128)(2,1)S(1)}, u32[]{:S(2)}, u32[]{:S(2)}) %all-to-all-start) | async-done | bytes 524320 | tf_op jit(solution)/shard_map/all_to_all | solution.py:20
  35.8 1.9 collective-permute-start.2
  37.7 1.2 collective-permute-done.2
  41.4 1.1 fusion.2
  42.6 4.2 %all-to-all-start.1 = ((bf16[16,8,2048]{2,1,0:T(8,128)(2,1)}), bf16[16,8,2048]{2,1,0:T(8,128)(2,1)}, u32[]{:S(2)}, u32[]{:S(2)}) async-start(bf16[16,8,2048]{2,1,0:T(8,128)(2,1)} %fusion.2), calls=%async_computation.1 | async-start | bytes 1048576 | tf_op jit(solution)/shard_map/all_to_all | solution.py:20
  46.8 1.9 copy.36
  48.7 2.1 collective-permute-start.4
  50.8 2.3 %collective-permute-start.5 = (bf16[256,2048]{1,0:T(8,128)(2,1)}, bf16[256,2048]{1,0:T(8,128)(2,1)}, u32[]{:S(2)}, u32[]{:S(2)}) collective-permute-start(bf16[256,2048]{1,0:T(8,128)(2,1)} %param.18), channel_id=1, source_target_pairs={{0,16},{16,0},{32,48},{48,32},{64,80},{80,64},{96,112},{112,96},{1... | collective-permute-start | bytes 3145736 | tf_op jit(solution)/shard_map/ppermute | solution.py:11
  53.7 1.8 convolution_add_fusion.1
  55.5 11.4 %all-to-all-done.1 = bf16[16,8,2048]{2,1,0:T(8,128)(2,1)} async-done(((bf16[16,8,2048]{2,1,0:T(8,128)(2,1)}), bf16[16,8,2048]{2,1,0:T(8,128)(2,1)}, u32[]{:S(2)}, u32[]{:S(2)}) %all-to-all-start.1) | async-done | bytes 524320 | tf_op jit(solution)/shard_map/all_to_all | solution.py:20
  66.8 1.1 convert_reduce_fusion.3
  69.7 4.2 %all-to-all-start.2 = ((bf16[16,8,2048]{2,1,0:T(8,128)(2,1)}), bf16[16,8,2048]{2,1,0:T(8,128)(2,1)}, u32[]{:S(2)}, u32[]{:S(2)}) async-start(bf16[16,8,2048]{2,1,0:T(8,128)(2,1)} %broadcast_in_dim.44), calls=%async_computation.2 | async-start | bytes 1048576 | tf_op jit(solution)/shard_map/all_to_all | solution.py:20
  73.9 3.1 %pad_maximum_fusion.1.down_ref = bf16[2,256,2048]{2,1,0:T(8,128)(2,1)} fusion(bf16[1,256,2048]{2,1,0:T(8,128)(2,1)} %bitcast.27, bf16[1,256,2048]{2,1,0:T(8,128)(2,1)} %bitcast.26), kind=kLoop, calls=%fused_computation.7 | loop fusion | flops 1048576 | bytes 4194304 | tf_op jit(solution)/shard_map/stack | solution.py:139
  77.0 3.9 %pad_maximum_fusion.wide_ref = bf16[2,2,2048,256]{3,2,1,0:T(8,128)(2,1)} fusion(bf16[1,2,2048,256]{3,2,1,0:T(8,128)(2,1)} %bitcast.25, bf16[1,2,2048,256]{3,2,1,0:T(8,128)(2,1)S(1)} %bitcast.110), kind=kLoop, calls=%fused_computation.2 | loop fusion | flops 2097152 | bytes 8388608 | tf_op jit(solution)/shard_map/stack | solution.py:139
  80.9 10.3 %all-to-all-done.2 = bf16[16,8,2048]{2,1,0:T(8,128)(2,1)} async-done(((bf16[16,8,2048]{2,1,0:T(8,128)(2,1)}), bf16[16,8,2048]{2,1,0:T(8,128)(2,1)}, u32[]{:S(2)}, u32[]{:S(2)}) %all-to-all-start.2) | async-done | bytes 524320 | tf_op jit(solution)/shard_map/all_to_all | solution.py:20
  91.2 6.2 %feed_forward.2 = bf16[128,2048]{1,0:T(8,128)(2,1)} custom-call(bf16[128,2048]{1,0:T(8,128)(2,1)} %bitcast.22.rows_ref, bf16[2,2,2048,256]{3,2,1,0:T(8,128)(2,1)} %pad_maximum_fusion.wide_ref, bf16[2,256,2048]{2,1,0:T(8,128)(2,1)} %pad_maximum_fusion.1.down_ref), custom_call_target="tpu_custom_call" | custom-call | tf_op jit(solution)/shard_map/feed_forward/pallas_call | solution.py:63
  97.3 20.0 %all_to_all.40 = bf16[16,8,2048]{2,1,0:T(8,128)(2,1)S(1)} all-to-all(bf16[16,8,2048]{2,1,0:T(8,128)(2,1)} %bitcast.113), channel_id=1, replica_groups=mesh['layer'=32,'tp'=16] {'tp'}, dimensions={0} | all-to-all | bytes 1048576 | tf_op jit(solution)/shard_map/all_to_all | solution.py:20
  117.4 3.5 %collective-permute-start.6 = (bf16[8,2048]{1,0:T(8,128)(2,1)S(1)}, bf16[8,2048]{1,0:T(8,128)(2,1)S(1)}, u32[]{:S(2)}, u32[]{:S(2)}) collective-permute-start(bf16[8,2048]{1,0:T(8,128)(2,1)S(1)} %fusion.43), channel_id=1, source_target_pairs={{0,32},{16,48},{32,64},{48,80},{64,96},{80,112},{96,128},{112,144}... | collective-permute-start | bytes 98312 | tf_op jit(solution)/shard_map/ppermute | solution.py:16
  120.9 4.6 %collective-permute-done.6 = bf16[8,2048]{1,0:T(8,128)(2,1)S(1)} collective-permute-done((bf16[8,2048]{1,0:T(8,128)(2,1)S(1)}, bf16[8,2048]{1,0:T(8,128)(2,1)S(1)}, u32[]{:S(2)}, u32[]{:S(2)}) %collective-permute-start.6) | collective-permute-done | bytes 32800 | tf_op jit(solution)/shard_map/ppermute | solution.py:16
  125.8 18.3 %all_to_all.41 = bf16[16,8,2048]{2,1,0:T(8,128)(2,1)S(1)} all-to-all(bf16[16,8,2048]{2,1,0:T(8,128)(2,1)S(1)} %broadcast_in_dim.45), channel_id=1, replica_groups=mesh['layer'=32,'tp'=16] {'tp'}, dimensions={0} | all-to-all | bytes 1048576 | tf_op jit(solution)/shard_map/all_to_all | solution.py:20
  144.9 1.9 collective-permute-start.7
  149.5 1.1 fusion.3
  150.6 3.6 %all-to-all-start.5 = ((bf16[16,8,2048]{2,1,0:T(8,128)(2,1)}), bf16[16,8,2048]{2,1,0:T(8,128)(2,1)S(1)}, u32[]{:S(2)}, u32[]{:S(2)}) async-start(bf16[16,8,2048]{2,1,0:T(8,128)(2,1)} %fusion.3), calls=%async_computation.5 | async-start | bytes 1048576 | tf_op jit(solution)/shard_map/all_to_all | solution.py:20
  154.5 19.7 %all-to-all-done.5 = bf16[16,8,2048]{2,1,0:T(8,128)(2,1)S(1)} async-done(((bf16[16,8,2048]{2,1,0:T(8,128)(2,1)}), bf16[16,8,2048]{2,1,0:T(8,128)(2,1)S(1)}, u32[]{:S(2)}, u32[]{:S(2)}) %all-to-all-start.5) | async-done | bytes 524320 | tf_op jit(solution)/shard_map/all_to_all | solution.py:20
  174.5 21.3 %all_to_all.42 = bf16[16,8,2048]{2,1,0:T(8,128)(2,1)} all-to-all(bf16[16,8,2048]{2,1,0:T(8,128)(2,1)S(1)} %broadcast_in_dim.46), channel_id=1, replica_groups=mesh['layer'=32,'tp'=16] {'tp'}, dimensions={0} | all-to-all | bytes 1048576 | tf_op jit(solution)/shard_map/all_to_all | solution.py:20
  195.9 6.2 %feed_forward.3 = bf16[128,2048]{1,0:T(8,128)(2,1)} custom-call(bf16[128,2048]{1,0:T(8,128)(2,1)} %bitcast.112, bf16[2,2,2048,256]{3,2,1,0:T(8,128)(2,1)} %pad_maximum_fusion.wide_ref, bf16[2,256,2048]{2,1,0:T(8,128)(2,1)} %pad_maximum_fusion.1.down_ref), custom_call_target="tpu_custom_call" | custom-call | tf_op jit(solution)/shard_map/feed_forward/pallas_call | solution.py:63
  202.0 3.6 %all-to-all-start.7 = ((bf16[16,8,2048]{2,1,0:T(8,128)(2,1)}), bf16[16,8,2048]{2,1,0:T(8,128)(2,1)S(1)}, u32[]{:S(2)}, u32[]{:S(2)}) async-start(bf16[16,8,2048]{2,1,0:T(8,128)(2,1)} %bitcast.111), calls=%async_computation.7 | async-start | bytes 1048576 | tf_op jit(solution)/shard_map/all_to_all | solution.py:20
  206.8 15.8 %all-to-all-done.7 = bf16[16,8,2048]{2,1,0:T(8,128)(2,1)S(1)} async-done(((bf16[16,8,2048]{2,1,0:T(8,128)(2,1)}), bf16[16,8,2048]{2,1,0:T(8,128)(2,1)S(1)}, u32[]{:S(2)}, u32[]{:S(2)}) %all-to-all-start.7) | async-done | bytes 524320 | tf_op jit(solution)/shard_map/all_to_all | solution.py:20
  (115 shorter events, 18.7 us)
Async XLA Ops:
  0.6 52.4 %copy-start = (bf16[2,8,2048]{2,1,0:T(8,128)(2,1)S(1)}, bf16[2,8,2048]{2,1,0:T(8,128)(2,1)}, u32[]{:S(2)}) copy-start(bf16[2,8,2048]{2,1,0:T(8,128)(2,1)} %param.12) | copy-start | bytes 196612
  0.6 25.9 %copy-start.8 = (bf16[64,2048]{1,0:T(8,128)(2,1)S(1)}, bf16[64,2048]{1,0:T(8,128)(2,1)}, u32[]{:S(2)}) copy-start(bf16[64,2048]{1,0:T(8,128)(2,1)} %param.16) | copy-start | bytes 786436
  3.4 32.0 %copy-start.1 = (bf16[1,2048,192]{1,2,0:T(8,128)(2,1)S(1)}, bf16[1,2048,192]{1,2,0:T(8,128)(2,1)}, u32[]{:S(2)}) copy-start(bf16[1,2048,192]{1,2,0:T(8,128)(2,1)} %param.15) | copy-start | bytes 2359300
  4.2 30.8 %all-to-all-start = ((bf16[16,8,2048]{2,1,0:T(8,128)(2,1)}), bf16[16,8,2048]{2,1,0:T(8,128)(2,1)S(1)}, u32[]{:S(2)}, u32[]{:S(2)}) async-start(bf16[16,8,2048]{2,1,0:T(8,128)(2,1)} %broadcast_in_dim.41), calls=%async_computation | async-start | bytes 1048576 | tf_op jit(solution)/shard_map/all_to_all | solution.py:20
  16.2 10.5 %collective-permute-start.1 = (bf16[1,2048,192]{1,2,0:T(8,128)(2,1)}, bf16[1,2048,192]{1,2,0:T(8,128)(2,1)S(1)}, u32[]{:S(2)}, u32[]{:S(2)}) collective-permute-start(bf16[1,2048,192]{1,2,0:T(8,128)(2,1)} %param.15), channel_id=1, source_target_pairs={{0,16},{16,0},{32,48},{48,32},{64,80},{80,64},{96,112},{112,96},{1... | collective-permute-start | bytes 2359304 | tf_op jit(solution)/shard_map/ppermute | solution.py:11
  18.9 21.6 %copy-start.9 = (f32[1,64,64]{1,2,0:T(8,128)}, f32[1,64,64]{1,2,0:T(8,128)S(1)}, u32[]{:S(2)}) copy-start(f32[1,64,64]{1,2,0:T(8,128)S(1)} %copy.22) | copy-start | bytes 49156
  20.5 4.4 %collective-permute-start = (f32[1,66,64]{1,2,0:T(8,128)S(1)}, f32[1,66,64]{1,2,0:T(8,128)S(1)}, u32[]{:S(2)}, u32[]{:S(2)}) collective-permute-start(f32[1,66,64]{1,2,0:T(8,128)S(1)} %maximum_maximum_fusion), channel_id=1, source_target_pairs={{0,16},{16,0},{32,48},{48,32},{64,80},{80,64},{96,112},{112,96},{1... | collective-permute-start | bytes 50696 | tf_op jit(solution)/shard_map/ppermute | solution.py:11
  22.9 3.6 %collective-permute-start.3 = (bf16[64,2048]{1,0:T(8,128)(2,1)}, bf16[64,2048]{1,0:T(8,128)(2,1)S(1)}, u32[]{:S(2)}, u32[]{:S(2)}) collective-permute-start(bf16[64,2048]{1,0:T(8,128)(2,1)} %param.16), channel_id=1, source_target_pairs={{0,16},{16,0},{32,48},{48,32},{64,80},{80,64},{96,112},{112,96},{1... | collective-permute-start | bytes 786440 | tf_op jit(solution)/shard_map/ppermute | solution.py:11
  24.9 15.7 %copy-start.12 = (f32[1,66,64]{1,2,0:T(8,128)}, f32[1,66,64]{1,2,0:T(8,128)S(1)}, u32[]{:S(2)}) copy-start(f32[1,66,64]{1,2,0:T(8,128)S(1)} %collective-permute-done) | copy-start | bytes 50692
  26.2 14.3 %copy-start.19 = (f32[2]{0:T(128)}, f32[2]{0:T(128)S(1)}, u32[]{:S(2)}) copy-start(f32[2]{0:T(128)S(1)} %get-tuple-element.37) | copy-start | bytes 28
  26.2 14.6 %copy-start.17 = (f32[2]{0:T(128)}, f32[2]{0:T(128)S(1)}, u32[]{:S(2)}) copy-start(f32[2]{0:T(128)S(1)} %get-tuple-element.36) | copy-start | bytes 28
  26.6 13.1 %copy-start.16 = (f32[1,64]{1,0:T(1,128)S(1)}, f32[1,64]{1,0:T(1,128)}, u32[]{:S(2)}) copy-start(f32[1,64]{1,0:T(1,128)} %param.20) | copy-start | bytes 772
  26.6 13.1 %copy-start.2 = (bf16[1,2048,192]{1,2,0:T(8,128)(2,1)}, bf16[1,2048,192]{1,2,0:T(8,128)(2,1)S(1)}, u32[]{:S(2)}) copy-start(bf16[1,2048,192]{1,2,0:T(8,128)(2,1)S(1)} %collective-permute-done.1) | copy-start | bytes 2359300
  35.8 3.1 %collective-permute-start.2 = (bf16[128,2,128]{0,2,1:T(8,128)(2,1)S(1)}, bf16[128,2,128]{0,2,1:T(8,128)(2,1)S(1)}, u32[]{:S(2)}, u32[]{:S(2)}) collective-permute-start(bf16[128,2,128]{0,2,1:T(8,128)(2,1)S(1)} %pad_maximum_fusion.6), channel_id=1, source_target_pairs={{0,16},{16,0},{32,48},{48,32},{64,80},{80,64},{96,112},{112,96},{1... | collective-permute-start | bytes 196616 | tf_op jit(solution)/shard_map/ppermute | solution.py:11
  37.7 4.8 %copy-start.11 = (bf16[128,2,64]{0,2,1:T(8,128)(2,1)}, bf16[128,2,64]{0,2,1:T(8,128)(2,1)S(1)}, u32[]{:S(2)}) copy-start(bf16[128,2,64]{0,2,1:T(8,128)(2,1)S(1)} %get-tuple-element.40) | copy-start | bytes 98308
  42.6 24.3 %all-to-all-start.1 = ((bf16[16,8,2048]{2,1,0:T(8,128)(2,1)}), bf16[16,8,2048]{2,1,0:T(8,128)(2,1)}, u32[]{:S(2)}, u32[]{:S(2)}) async-start(bf16[16,8,2048]{2,1,0:T(8,128)(2,1)} %fusion.2), calls=%async_computation.1 | async-start | bytes 1048576 | tf_op jit(solution)/shard_map/all_to_all | solution.py:20
  46.8 21.2 %copy-start.4 = (bf16[8,2048]{1,0:T(8,128)(2,1)S(1)}, bf16[8,2048]{1,0:T(8,128)(2,1)}, u32[]{:S(2)}) copy-start(bf16[8,2048]{1,0:T(8,128)(2,1)} %param.11) | copy-start | bytes 98308
  48.7 28.3 %collective-permute-start.4 = (bf16[2,2048,256]{2,1,0:T(8,128)(2,1)S(1)}, bf16[2,2048,256]{2,1,0:T(8,128)(2,1)}, u32[]{:S(2)}, u32[]{:S(2)}) collective-permute-start(bf16[2,2048,256]{2,1,0:T(8,128)(2,1)S(1)} %bitcast.109), channel_id=1, source_target_pairs={{0,16},{16,0},{32,48},{48,32},{64,80},{80,64},{96,112},{112,96},{1... | collective-permute-start | bytes 6291464 | tf_op jit(solution)/shard_map/ppermute | solution.py:11
  50.8 23.1 %collective-permute-start.5 = (bf16[256,2048]{1,0:T(8,128)(2,1)}, bf16[256,2048]{1,0:T(8,128)(2,1)}, u32[]{:S(2)}, u32[]{:S(2)}) collective-permute-start(bf16[256,2048]{1,0:T(8,128)(2,1)} %param.18), channel_id=1, source_target_pairs={{0,16},{16,0},{32,48},{48,32},{64,80},{80,64},{96,112},{112,96},{1... | collective-permute-start | bytes 3145736 | tf_op jit(solution)/shard_map/ppermute | solution.py:11
  69.7 21.5 %all-to-all-start.2 = ((bf16[16,8,2048]{2,1,0:T(8,128)(2,1)}), bf16[16,8,2048]{2,1,0:T(8,128)(2,1)}, u32[]{:S(2)}, u32[]{:S(2)}) async-start(bf16[16,8,2048]{2,1,0:T(8,128)(2,1)} %broadcast_in_dim.44), calls=%async_computation.2 | async-start | bytes 1048576 | tf_op jit(solution)/shard_map/all_to_all | solution.py:20
  91.2 26.2 %copy-start.6 = (bf16[8,2048]{1,0:T(8,128)(2,1)S(1)}, bf16[8,2048]{1,0:T(8,128)(2,1)}, u32[]{:S(2)}) copy-start(bf16[8,2048]{1,0:T(8,128)(2,1)} %copy-done.5) | copy-start | bytes 98308
  91.2 34.4 %copy-start.10 = (bf16[8,2048]{1,0:T(8,128)(2,1)S(1)}, bf16[8,2048]{1,0:T(8,128)(2,1)}, u32[]{:S(2)}) copy-start(bf16[8,2048]{1,0:T(8,128)(2,1)} %dynamic-slice_bitcast_fusion) | copy-start | bytes 98308
  97.3 46.8 %copy-start.3 = (bf16[1,2048,192]{1,2,0:T(8,128)(2,1)S(1)}, bf16[1,2048,192]{1,2,0:T(8,128)(2,1)}, u32[]{:S(2)}) copy-start(bf16[1,2048,192]{1,2,0:T(8,128)(2,1)} %copy-done.2) | copy-start | bytes 2359300
  117.4 27.5 %copy-start.13 = (bf16[8,2048]{1,0:T(8,128)(2,1)}, bf16[8,2048]{1,0:T(8,128)(2,1)S(1)}, u32[]{:S(2)}) copy-start(bf16[8,2048]{1,0:T(8,128)(2,1)S(1)} %fusion.43) | copy-start | bytes 98308
  117.4 8.1 %collective-permute-start.6 = (bf16[8,2048]{1,0:T(8,128)(2,1)S(1)}, bf16[8,2048]{1,0:T(8,128)(2,1)S(1)}, u32[]{:S(2)}, u32[]{:S(2)}) collective-permute-start(bf16[8,2048]{1,0:T(8,128)(2,1)S(1)} %fusion.43), channel_id=1, source_target_pairs={{0,32},{16,48},{32,64},{48,80},{64,96},{80,112},{96,128},{112,144}... | collective-permute-start | bytes 98312 | tf_op jit(solution)/shard_map/ppermute | solution.py:16
  125.8 21.1 %copy-start.15 = (f32[2,64]{1,0:T(2,128)S(1)}, f32[2,64]{1,0:T(2,128)}, u32[]{:S(2)}) copy-start(f32[2,64]{1,0:T(2,128)} %get-tuple-element.14) | copy-start | bytes 1540
  125.8 21.3 %copy-start.20 = (f32[2]{0:T(128)S(1)}, f32[2]{0:T(128)}, u32[]{:S(2)}) copy-start(f32[2]{0:T(128)} %copy-done.19) | copy-start | bytes 28
  125.8 21.2 %copy-start.21 = (f32[2,64,64]{1,2,0:T(8,128)S(1)}, f32[2,64,64]{1,2,0:T(8,128)}, u32[]{:S(2)}) copy-start(f32[2,64,64]{1,2,0:T(8,128)} %convolution_add_fusion.1) | copy-start | bytes 98308
  144.5 4.4 %copy-start.18 = (f32[2]{0:T(128)S(1)}, f32[2]{0:T(128)}, u32[]{:S(2)}) copy-start(f32[2]{0:T(128)} %copy-done.17) | copy-start | bytes 28
  144.9 3.1 %collective-permute-start.7 = (bf16[128,2,128]{0,2,1:T(8,128)(2,1)S(1)}, bf16[128,2,128]{0,2,1:T(8,128)(2,1)S(1)}, u32[]{:S(2)}, u32[]{:S(2)}) collective-permute-start(bf16[128,2,128]{0,2,1:T(8,128)(2,1)S(1)} %pad_maximum_fusion.8), channel_id=1, source_target_pairs={{0,16},{16,0},{32,48},{48,32},{64,80},{80,64},{96,112},{112,96},{1... | collective-permute-start | bytes 196616 | tf_op jit(solution)/shard_map/ppermute | solution.py:11
  150.6 23.6 %all-to-all-start.5 = ((bf16[16,8,2048]{2,1,0:T(8,128)(2,1)}), bf16[16,8,2048]{2,1,0:T(8,128)(2,1)S(1)}, u32[]{:S(2)}, u32[]{:S(2)}) async-start(bf16[16,8,2048]{2,1,0:T(8,128)(2,1)} %fusion.3), calls=%async_computation.5 | async-start | bytes 1048576 | tf_op jit(solution)/shard_map/all_to_all | solution.py:20
  202.0 20.6 %all-to-all-start.7 = ((bf16[16,8,2048]{2,1,0:T(8,128)(2,1)}), bf16[16,8,2048]{2,1,0:T(8,128)(2,1)S(1)}, u32[]{:S(2)}, u32[]{:S(2)}) async-start(bf16[16,8,2048]{2,1,0:T(8,128)(2,1)} %bitcast.111), calls=%async_computation.7 | async-start | bytes 1048576 | tf_op jit(solution)/shard_map/all_to_all | solution.py:20
  (3 other events, 7.7 us)

commit v4 on v2

--- a/solution.py
+++ b/solution.py
@@ -24,10 +24,21 @@
     return blocks.reshape((-1, rows.shape[1]))
 
 
-def scatter_sum(partial):
+def scatter_sum(partial, *beside):
     members = lax.axis_size("tp")
     blocks = exchange(partial.reshape((members, -1, partial.shape[1])))
-    return jnp.sum(blocks.astype(jnp.float32), axis=0)
+    if beside:
+        blocks, *beside = lax.optimization_barrier((blocks, *beside))
+    return (jnp.sum(blocks.astype(jnp.float32), axis=0), *beside)
+
+
+def feed_forward(rows, wide, other_wide, down_pair):
+    hidden = []
+    for weight in (wide, other_wide):
+        gate_up = jnp.einsum("sd,tdf->stf", rows, weight, preferred_element_type=jnp.float32)
+        hidden.append((jax.nn.silu(gate_up[:, 0]) * gate_up[:, 1]).astype(jnp.bfloat16))
+    hidden = jnp.concatenate(hidden, axis=1)
+    return jnp.dot(hidden, down_pair, preferred_element_type=jnp.float32).astype(jnp.bfloat16)
 
 
 def rms_norm(values, weight):
@@ -85,11 +96,15 @@
     logit_row = jnp.broadcast_to(bias_gate[:, None, None], (1, 1, head_dim))
     state = jnp.concatenate([memory_state, memory_norm[:, None], logit_row], axis=1)
     other_state = swap_halves(state)
+    other_qkv = swap_halves(proj_qkv)
+    out_pair = lax.optimization_barrier(
+        jnp.concatenate([proj_out, swap_halves(proj_out)], axis=0)
+    )
     wide = lax.optimization_barrier(jnp.transpose(proj_gate_up, (1, 0, 2)))
-    qkv_pair, out_pair, wide_pair, down_pair = (
-        lax.optimization_barrier(jnp.concatenate([weight, swap_halves(weight)], axis=axis))
-        for weight, axis in ((proj_qkv, 0), (proj_out, 0), (wide, 2), (proj_down, 0))
-    )
+    other_wide = swap_halves(wide)
+    down_pair = jnp.concatenate([proj_down, swap_halves(proj_down)], axis=0)
+    feed_weights = lax.optimization_barrier((wide, other_wide, down_pair))
+    fresh_rows = lax.dynamic_index_in_dim(fresh, half, 0, keepdims=False)
     memory_pair = jnp.concatenate([memory_state, other_state[:, :head_dim]], axis=0)
     totals_pair = jnp.concatenate([memory_norm, other_state[:, head_dim]], axis=0)
     logits = jnp.concatenate([bias_gate, other_state[:, head_dim + 1, 0]], axis=0)
@@ -97,18 +112,15 @@
     causal = index[:, None] >= index[None, :]
     allowed = jnp.concatenate([causal, jnp.broadcast_to(half == 1, causal.shape)], axis=1)
 
-    def expand(rows):
-        gate, up = (
-            jnp.dot(rows, weight, preferred_element_type=jnp.float32) for weight in wide_pair
-        )
-        return (jax.nn.silu(gate) * up).astype(jnp.bfloat16)
+    def project(rows, weight):
+        return jnp.dot(rows, weight[0], preferred_element_type=jnp.float32).astype(jnp.bfloat16)
 
-    def apply_layer(rows, memory, totals):
+    def apply_layer(rows, memory, totals, wide, other_wide, down_pair, *beside):
         normed = gather_rows(rms_norm(rows, gain_one))
-        both = jnp.einsum(
-            "sd,hdc->shc", normed, qkv_pair, preferred_element_type=jnp.float32
-        ).astype(jnp.bfloat16)
-        swapped = swap_halves(both[:, ::-1, head_dim:])
+        own = project(normed, proj_qkv)
+        other = project(normed, other_qkv)
+        swapped = swap_halves(jnp.stack([other[:, head_dim:], own[:, head_dim:]], axis=1))
+        both = jnp.stack([own, other], axis=1)
         queries = both[..., :head_dim]
         keyed = jnp.concatenate([both[..., head_dim : 2 * head_dim], swapped[..., :head_dim]], axis=0)
         valued = jnp.concatenate([both[..., 2 * head_dim :], swapped[..., head_dim:]], axis=0)
@@ -117,19 +129,23 @@
         attn = jnp.dot(
             blended.reshape(half_len, -1), out_pair, preferred_element_type=jnp.float32
         )
-        attn = scatter_sum(attn.astype(jnp.bfloat16))
+        attn, memory, totals, wide, other_wide, down_pair, *beside = scatter_sum(
+            attn.astype(jnp.bfloat16), memory, totals, wide, other_wide, down_pair, *beside
+        )
         hidden_one = (rows.astype(jnp.float32) + attn).astype(jnp.bfloat16)
         normed_two = gather_rows(rms_norm(hidden_one, gain_two))
-        down = jnp.dot(expand(normed_two), down_pair, preferred_element_type=jnp.float32)
-        ffn = scatter_sum(down.astype(jnp.bfloat16))
+        (ffn,) = scatter_sum(feed_forward(normed_two, wide, other_wide, down_pair))
         output = (hidden_one.astype(jnp.float32) + ffn).astype(jnp.bfloat16)
-        return (output, memory, totals)
+        return (output, memory, totals, wide, other_wide, down_pair, *beside)
 
-    first_rows, memory_one, totals_one = apply_layer(acts, memory_pair, totals_pair)
+    first_rows, memory_one, totals_one, *feed_weights, fresh_rows = apply_layer(
+        acts, memory_pair, totals_pair, *feed_weights, fresh_rows
+    )
     incoming = next_layer(first_rows)
-    fresh_rows = lax.dynamic_index_in_dim(fresh, half, 0, keepdims=False)
     entering = jnp.where(depth == 0, fresh_rows, incoming)
-    second_rows, memory_two, totals_two = apply_layer(entering, memory_one, totals_one)
+    second_rows, memory_two, totals_two, *_ = apply_layer(
+        entering, memory_one, totals_one, *feed_weights
+    )
     return (first_rows, second_rows, memory_two[:1], totals_two[:1])
 
 

time: 224 us -> 226 us (level)
  blocking collectives: 64.4 us -> 85.3 us
  other arithmetic: 15.3 us -> 9.2 us
  waiting for transfers between devices: 69.2 us -> 63.9 us
  local copies, waits for them, and re-layouts: 11.1 us -> 6.3 us
    all_to_all x3 -> x4, blocking collectives: 64.4 us -> 85.3 us  [exchange(): return lax.all_to_all(blocks, 'tp', 0, 0, tiled=True)]
    concatenate x5 -> x2, other arithmetic: 9.56 us -> 1.88 us  [the longest x1 1.84 us: body(): down_pair = jnp.concatenate([proj_down, swap_halves(proj_down)], axis=0)]
    all_to_all x5 -> x4, waiting for transfers between devices: 62.4 us -> 57.2 us  [exchange(): return lax.all_to_all(blocks, 'tp', 0, 0, tiled=True)]
    unnamed x45 -> x56, local copies, waits for them, and re-layouts: 4.85 us -> 1.66 us
    all_to_all x5 -> x4, starting transfers between devices: 26.3 us -> 24.8 us  [exchange(): return lax.all_to_all(blocks, 'tp', 0, 0, tiled=True)]
    dot_general x4 -> x10, matrix products: 9.57 us -> 8.17 us  [the longest x4 4.97 us: feed_forward(): jnp.einsum('sd,tdf->stf', rows, weight, preferred_element_type=jnp.float32)]
  transfers between devices with their start and end apart: 13 -> 12, of which waited for: 8 -> 7; matrix products, arithmetic and copies ran while one was open for 11% -> 6% of each run, Pallas kernels for 0% -> 0%
where the time goes in v4:
time: 226 us; the launch traced here: 224 us
  blocking collectives  85.3 us (38%)
  waiting for transfers between devices  63.9 us (28%)
  starting transfers between devices  42.7 us (19%)
  matrix products  14.9 us (7%)
  other arithmetic  9.2 us (4%)
  local copies, waits for them, and re-layouts  6.3 us (3%)
    all_to_all x4, blocking collectives, exchange(): return lax.all_to_all(blocks, 'tp', 0, 0, tiled=True)  85.3 us
    all_to_all x4, waiting for transfers between devices, exchange(): return lax.all_to_all(blocks, 'tp', 0, 0, tiled=True)  57.2 us
    all_to_all x4, starting transfers between devices, exchange(): return lax.all_to_all(blocks, 'tp', 0, 0, tiled=True)  24.8 us
    ppermute x7, starting transfers between devices, swap_halves(): return lax.ppermute(value, 'layer', pairs)  14.4 us
    dot_general x4, matrix products, feed_forward(): jnp.einsum('sd,tdf->stf', rows, weight, preferred_element_type=jnp.float32)  4.97 us
    ppermute x1, waiting for transfers between devices, next_layer(): lax.ppermute(value, 'layer', [(source, source + 2) for source in range(co...  4.73 us
  transfers between devices with their start and end apart: 12, of which 7 were waited for; matrix products, arithmetic and copies ran while one was open for 6% of the time, Pallas kernels for 0%

profile of v4, /device:TPU:2, one launch (start us, length us, event | category | flops | bytes accessed | tf_op | source)
XLA Modules:
  0.0 224.4 jit_solution(170064513635245718)
XLA Ops:
  0.7 1.0 fusion.64
  1.7 0.9 constant_dynamic-slice_fusion
  4.2 12.0 %all-to-all-start = ((bf16[16,8,2048]{2,1,0:T(8,128)(2,1)}), bf16[16,8,2048]{2,1,0:T(8,128)(2,1)S(1)}, u32[]{:S(2)}, u32[]{:S(2)}) async-start(bf16[16,8,2048]{2,1,0:T(8,128)(2,1)} %broadcast_in_dim.41), calls=%async_computation | async-start | bytes 1048576 | tf_op jit(solution)/shard_map/all_to_all | solution.py:18
  18.6 1.9 collective-permute-start
  20.6 2.4 %collective-permute-start.3 = (bf16[64,2048]{1,0:T(8,128)(2,1)}, bf16[64,2048]{1,0:T(8,128)(2,1)S(1)}, u32[]{:S(2)}, u32[]{:S(2)}) collective-permute-start(bf16[64,2048]{1,0:T(8,128)(2,1)} %param.16), channel_id=1, source_target_pairs={{0,16},{16,0},{32,48},{48,32},{64,80},{80,64},{96,112},{112,96},{1... | collective-permute-start | bytes 786440 | tf_op jit(solution)/shard_map/ppermute | solution.py:9
  23.0 1.9 collective-permute-start.1
  24.9 2.4 %collective-permute-start.5 = (bf16[256,2048]{1,0:T(8,128)(2,1)}, bf16[256,2048]{1,0:T(8,128)(2,1)}, u32[]{:S(2)}, u32[]{:S(2)}) collective-permute-start(bf16[256,2048]{1,0:T(8,128)(2,1)} %param.18), channel_id=1, source_target_pairs={{0,16},{16,0},{32,48},{48,32},{64,80},{80,64},{96,112},{112,96},{1... | collective-permute-start | bytes 3145736 | tf_op jit(solution)/shard_map/ppermute | solution.py:9
  27.3 1.9 collective-permute-start.4
  30.9 4.2 %all-to-all-done = bf16[16,8,2048]{2,1,0:T(8,128)(2,1)S(1)} async-done(((bf16[16,8,2048]{2,1,0:T(8,128)(2,1)}), bf16[16,8,2048]{2,1,0:T(8,128)(2,1)S(1)}, u32[]{:S(2)}, u32[]{:S(2)}) %all-to-all-start) | async-done | bytes 524320 | tf_op jit(solution)/shard_map/all_to_all | solution.py:18
  35.9 1.9 collective-permute-start.2
  37.9 1.2 collective-permute-done.2
  41.5 1.1 fusion.2
  42.7 5.7 %all-to-all-start.1 = ((bf16[16,8,2048]{2,1,0:T(8,128)(2,1)}), bf16[16,8,2048]{2,1,0:T(8,128)(2,1)}, u32[]{:S(2)}, u32[]{:S(2)}) async-start(bf16[16,8,2048]{2,1,0:T(8,128)(2,1)} %fusion.2), calls=%async_computation.1 | async-start | bytes 1048576 | tf_op jit(solution)/shard_map/all_to_all | solution.py:18
  49.1 1.8 pad_maximum_fusion
  51.0 0.9 convolution_add_fusion.1
  51.9 16.3 %all-to-all-done.1 = bf16[16,8,2048]{2,1,0:T(8,128)(2,1)} async-done(((bf16[16,8,2048]{2,1,0:T(8,128)(2,1)}), bf16[16,8,2048]{2,1,0:T(8,128)(2,1)}, u32[]{:S(2)}, u32[]{:S(2)}) %all-to-all-start.1) | async-done | bytes 524320 | tf_op jit(solution)/shard_map/all_to_all | solution.py:18
  68.2 1.3 convert_reduce_fusion.3
  69.7 21.3 %all_to_all.40 = bf16[16,8,2048]{2,1,0:T(8,128)(2,1)S(1)} all-to-all(bf16[16,8,2048]{2,1,0:T(8,128)(2,1)S(1)} %broadcast_in_dim.44), channel_id=1, replica_groups=mesh['layer'=32,'tp'=16] {'tp'}, dimensions={0} | all-to-all | bytes 1048576 | tf_op jit(solution)/shard_map/all_to_all | solution.py:18
  91.5 2.0 fusion.10
  94.1 22.1 %all_to_all.41 = bf16[16,8,2048]{2,1,0:T(8,128)(2,1)S(1)} all-to-all(bf16[16,8,2048]{2,1,0:T(8,128)(2,1)S(1)} %fusion.3), channel_id=1, replica_groups=mesh['layer'=32,'tp'=16] {'tp'}, dimensions={0} | all-to-all | bytes 1048576 | tf_op jit(solution)/shard_map/all_to_all | solution.py:18
  116.3 3.5 %collective-permute-start.6 = (bf16[8,2048]{1,0:T(8,128)(2,1)S(1)}, bf16[8,2048]{1,0:T(8,128)(2,1)}, u32[]{:S(2)}, u32[]{:S(2)}) collective-permute-start(bf16[8,2048]{1,0:T(8,128)(2,1)S(1)} %fusion.71), channel_id=1, source_target_pairs={{0,32},{16,48},{32,64},{48,80},{64,96},{80,112},{96,128},{112,144}... | collective-permute-start | bytes 98312 | tf_op jit(solution)/shard_map/ppermute | solution.py:14
  119.8 4.7 %collective-permute-done.6 = bf16[8,2048]{1,0:T(8,128)(2,1)} collective-permute-done((bf16[8,2048]{1,0:T(8,128)(2,1)S(1)}, bf16[8,2048]{1,0:T(8,128)(2,1)}, u32[]{:S(2)}, u32[]{:S(2)}) %collective-permute-start.6) | collective-permute-done | bytes 32800 | tf_op jit(solution)/shard_map/ppermute | solution.py:14
  125.6 20.9 %all_to_all.42 = bf16[16,8,2048]{2,1,0:T(8,128)(2,1)S(1)} all-to-all(bf16[16,8,2048]{2,1,0:T(8,128)(2,1)S(1)} %broadcast_in_dim.45), channel_id=1, replica_groups=mesh['layer'=32,'tp'=16] {'tp'}, dimensions={0} | all-to-all | bytes 1048576 | tf_op jit(solution)/shard_map/all_to_all | solution.py:18
  147.3 1.9 collective-permute-start.7
  151.8 1.1 fusion.4
  153.0 3.6 %all-to-all-start.5 = ((bf16[16,8,2048]{2,1,0:T(8,128)(2,1)}), bf16[16,8,2048]{2,1,0:T(8,128)(2,1)S(1)}, u32[]{:S(2)}, u32[]{:S(2)}) async-start(bf16[16,8,2048]{2,1,0:T(8,128)(2,1)} %fusion.4), calls=%async_computation.5 | async-start | bytes 1048576 | tf_op jit(solution)/shard_map/all_to_all | solution.py:18
  156.8 19.7 %all-to-all-done.5 = bf16[16,8,2048]{2,1,0:T(8,128)(2,1)S(1)} async-done(((bf16[16,8,2048]{2,1,0:T(8,128)(2,1)}), bf16[16,8,2048]{2,1,0:T(8,128)(2,1)S(1)}, u32[]{:S(2)}, u32[]{:S(2)}) %all-to-all-start.5) | async-done | bytes 524320 | tf_op jit(solution)/shard_map/all_to_all | solution.py:18
  176.9 21.1 %all_to_all.43 = bf16[16,8,2048]{2,1,0:T(8,128)(2,1)S(1)} all-to-all(bf16[16,8,2048]{2,1,0:T(8,128)(2,1)S(1)} %broadcast_in_dim.46), channel_id=1, replica_groups=mesh['layer'=32,'tp'=16] {'tp'}, dimensions={0} | all-to-all | bytes 1048576 | tf_op jit(solution)/shard_map/all_to_all | solution.py:18
  198.5 2.0 fusion.6
  200.6 1.3 fusion.5
  201.8 3.6 %all-to-all-start.7 = ((bf16[16,8,2048]{2,1,0:T(8,128)(2,1)}), bf16[16,8,2048]{2,1,0:T(8,128)(2,1)S(1)}, u32[]{:S(2)}, u32[]{:S(2)}) async-start(bf16[16,8,2048]{2,1,0:T(8,128)(2,1)} %fusion.5), calls=%async_computation.7 | async-start | bytes 1048576 | tf_op jit(solution)/shard_map/all_to_all | solution.py:18
  206.6 17.0 %all-to-all-done.7 = bf16[16,8,2048]{2,1,0:T(8,128)(2,1)S(1)} async-done(((bf16[16,8,2048]{2,1,0:T(8,128)(2,1)}), bf16[16,8,2048]{2,1,0:T(8,128)(2,1)S(1)}, u32[]{:S(2)}, u32[]{:S(2)}) %all-to-all-start.7) | async-done | bytes 524320 | tf_op jit(solution)/shard_map/all_to_all | solution.py:18
  (130 shorter events, 17.7 us)
Async XLA Ops:
  0.6 47.8 %copy-start = (bf16[2,8,2048]{2,1,0:T(8,128)(2,1)S(1)}, bf16[2,8,2048]{2,1,0:T(8,128)(2,1)}, u32[]{:S(2)}) copy-start(bf16[2,8,2048]{2,1,0:T(8,128)(2,1)} %param.12) | copy-start | bytes 196612
  0.6 30.2 %copy-start.7 = (bf16[64,2048]{1,0:T(8,128)(2,1)S(1)}, bf16[64,2048]{1,0:T(8,128)(2,1)}, u32[]{:S(2)}) copy-start(bf16[64,2048]{1,0:T(8,128)(2,1)} %param.16) | copy-start | bytes 786436
  0.7 34.4 %copy-start.1 = (bf16[1,2048,192]{1,2,0:T(8,128)(2,1)S(1)}, bf16[1,2048,192]{1,2,0:T(8,128)(2,1)}, u32[]{:S(2)}) copy-start(bf16[1,2048,192]{1,2,0:T(8,128)(2,1)} %param.15) | copy-start | bytes 2359300
  4.2 30.8 %all-to-all-start = ((bf16[16,8,2048]{2,1,0:T(8,128)(2,1)}), bf16[16,8,2048]{2,1,0:T(8,128)(2,1)S(1)}, u32[]{:S(2)}, u32[]{:S(2)}) async-start(bf16[16,8,2048]{2,1,0:T(8,128)(2,1)} %broadcast_in_dim.41), calls=%async_computation | async-start | bytes 1048576 | tf_op jit(solution)/shard_map/all_to_all | solution.py:18
  17.7 23.0 %copy-start.8 = (f32[1,64,64]{1,2,0:T(8,128)}, f32[1,64,64]{1,2,0:T(8,128)S(1)}, u32[]{:S(2)}) copy-start(f32[1,64,64]{1,2,0:T(8,128)S(1)} %copy.25) | copy-start | bytes 49156
  18.6 10.7 %collective-permute-start = (f32[1,66,64]{1,2,0:T(8,128)S(1)}, f32[1,66,64]{1,2,0:T(8,128)S(1)}, u32[]{:S(2)}, u32[]{:S(2)}) collective-permute-start(f32[1,66,64]{1,2,0:T(8,128)S(1)} %maximum_maximum_fusion), channel_id=1, source_target_pairs={{0,16},{16,0},{32,48},{48,32},{64,80},{80,64},{96,112},{112,96},{1... | collective-permute-start | bytes 50696 | tf_op jit(solution)/shard_map/ppermute | solution.py:9
  20.6 10.3 %collective-permute-start.3 = (bf16[64,2048]{1,0:T(8,128)(2,1)}, bf16[64,2048]{1,0:T(8,128)(2,1)S(1)}, u32[]{:S(2)}, u32[]{:S(2)}) collective-permute-start(bf16[64,2048]{1,0:T(8,128)(2,1)} %param.16), channel_id=1, source_target_pairs={{0,16},{16,0},{32,48},{48,32},{64,80},{80,64},{96,112},{112,96},{1... | collective-permute-start | bytes 786440 | tf_op jit(solution)/shard_map/ppermute | solution.py:9
  23.0 12.5 %collective-permute-start.1 = (bf16[1,2048,192]{1,2,0:T(8,128)(2,1)}, bf16[1,2048,192]{1,2,0:T(8,128)(2,1)S(1)}, u32[]{:S(2)}, u32[]{:S(2)}) collective-permute-start(bf16[1,2048,192]{1,2,0:T(8,128)(2,1)} %param.15), channel_id=1, source_target_pairs={{0,16},{16,0},{32,48},{48,32},{64,80},{80,64},{96,112},{112,96},{1... | collective-permute-start | bytes 2359304 | tf_op jit(solution)/shard_map/ppermute | solution.py:9
  24.9 24.2 %collective-permute-start.5 = (bf16[256,2048]{1,0:T(8,128)(2,1)}, bf16[256,2048]{1,0:T(8,128)(2,1)}, u32[]{:S(2)}, u32[]{:S(2)}) collective-permute-start(bf16[256,2048]{1,0:T(8,128)(2,1)} %param.18), channel_id=1, source_target_pairs={{0,16},{16,0},{32,48},{48,32},{64,80},{80,64},{96,112},{112,96},{1... | collective-permute-start | bytes 3145736 | tf_op jit(solution)/shard_map/ppermute | solution.py:9
  27.3 24.5 %collective-permute-start.4 = (bf16[2,2048,256]{2,0,1:T(2,128)(2,1)}, bf16[2,2048,256]{2,0,1:T(2,128)(2,1)}, u32[]{:S(2)}, u32[]{:S(2)}) collective-permute-start(bf16[2,2048,256]{2,0,1:T(2,128)(2,1)} %bitcast.179), channel_id=1, source_target_pairs={{0,16},{16,0},{32,48},{48,32},{64,80},{80,64},{96,112},{112,96},{1... | collective-permute-start | bytes 6291464 | tf_op jit(solution)/shard_map/ppermute | solution.py:9
  29.3 11.4 %copy-start.12 = (f32[1,66,64]{1,2,0:T(8,128)}, f32[1,66,64]{1,2,0:T(8,128)S(1)}, u32[]{:S(2)}) copy-start(f32[1,66,64]{1,2,0:T(8,128)S(1)} %collective-permute-done) | copy-start | bytes 50692
  30.8 9.9 %copy-start.21 = (f32[2]{0:T(128)}, f32[2]{0:T(128)S(1)}, u32[]{:S(2)}) copy-start(f32[2]{0:T(128)S(1)} %get-tuple-element.55) | copy-start | bytes 28
  30.8 10.1 %copy-start.19 = (f32[2]{0:T(128)}, f32[2]{0:T(128)S(1)}, u32[]{:S(2)}) copy-start(f32[2]{0:T(128)S(1)} %get-tuple-element.54) | copy-start | bytes 28
  30.8 8.4 %copy-start.18 = (f32[1,64]{1,0:T(1,128)S(1)}, f32[1,64]{1,0:T(1,128)}, u32[]{:S(2)}) copy-start(f32[1,64]{1,0:T(1,128)} %param.20) | copy-start | bytes 772
  35.5 6.1 %copy-start.2 = (bf16[1,2048,192]{1,2,0:T(8,128)(2,1)}, bf16[1,2048,192]{1,2,0:T(8,128)(2,1)S(1)}, u32[]{:S(2)}) copy-start(bf16[1,2048,192]{1,2,0:T(8,128)(2,1)S(1)} %collective-permute-done.1) | copy-start | bytes 2359300
  35.9 3.1 %collective-permute-start.2 = (bf16[128,2,128]{0,2,1:T(8,128)(2,1)S(1)}, bf16[128,2,128]{0,2,1:T(8,128)(2,1)S(1)}, u32[]{:S(2)}, u32[]{:S(2)}) collective-permute-start(bf16[128,2,128]{0,2,1:T(8,128)(2,1)S(1)} %pad_maximum_fusion.5), channel_id=1, source_target_pairs={{0,16},{16,0},{32,48},{48,32},{64,80},{80,64},{96,112},{112,96},{1... | collective-permute-start | bytes 196616 | tf_op jit(solution)/shard_map/ppermute | solution.py:9
  37.8 4.8 %copy-start.10 = (bf16[128,2,64]{0,2,1:T(8,128)(2,1)}, bf16[128,2,64]{0,2,1:T(8,128)(2,1)S(1)}, u32[]{:S(2)}) copy-start(bf16[128,2,64]{0,2,1:T(8,128)(2,1)S(1)} %get-tuple-element.58) | copy-start | bytes 98308
  39.0 3.6 %copy-start.15 = (bf16[128,2,64]{0,2,1:T(8,128)(2,1)}, bf16[128,2,64]{0,2,1:T(8,128)(2,1)S(1)}, u32[]{:S(2)}) copy-start(bf16[128,2,64]{0,2,1:T(8,128)(2,1)S(1)} %get-tuple-element.62) | copy-start | bytes 98308
  42.7 25.5 %all-to-all-start.1 = ((bf16[16,8,2048]{2,1,0:T(8,128)(2,1)}), bf16[16,8,2048]{2,1,0:T(8,128)(2,1)}, u32[]{:S(2)}, u32[]{:S(2)}) async-start(bf16[16,8,2048]{2,1,0:T(8,128)(2,1)} %fusion.2), calls=%async_computation.1 | async-start | bytes 1048576 | tf_op jit(solution)/shard_map/all_to_all | solution.py:18
  49.0 20.4 %copy-start.4 = (bf16[8,2048]{1,0:T(8,128)(2,1)S(1)}, bf16[8,2048]{1,0:T(8,128)(2,1)}, u32[]{:S(2)}) copy-start(bf16[8,2048]{1,0:T(8,128)(2,1)} %param.11) | copy-start | bytes 98308
  68.2 22.8 %copy-start.23 = (bf16[2048,2,256]{2,1,0:T(2,128)(2,1)S(1)}, bf16[2048,2,256]{2,1,0:T(2,128)(2,1)}, u32[]{:S(2)}) copy-start(bf16[2048,2,256]{2,1,0:T(2,128)(2,1)} %param.17) | copy-start | bytes 6291460
  116.3 8.3 %collective-permute-start.6 = (bf16[8,2048]{1,0:T(8,128)(2,1)S(1)}, bf16[8,2048]{1,0:T(8,128)(2,1)}, u32[]{:S(2)}, u32[]{:S(2)}) collective-permute-start(bf16[8,2048]{1,0:T(8,128)(2,1)S(1)} %fusion.71), channel_id=1, source_target_pairs={{0,32},{16,48},{32,64},{48,80},{64,96},{80,112},{96,128},{112,144}... | collective-permute-start | bytes 98312 | tf_op jit(solution)/shard_map/ppermute | solution.py:14
  119.8 27.1 %copy-start.3 = (bf16[1,2048,192]{1,2,0:T(8,128)(2,1)S(1)}, bf16[1,2048,192]{1,2,0:T(8,128)(2,1)}, u32[]{:S(2)}) copy-start(bf16[1,2048,192]{1,2,0:T(8,128)(2,1)} %copy-done.2) | copy-start | bytes 2359300
  125.6 23.6 %copy-start.17 = (f32[2,64]{1,0:T(2,128)S(1)}, f32[2,64]{1,0:T(2,128)}, u32[]{:S(2)}) copy-start(f32[2,64]{1,0:T(2,128)} %get-tuple-element.29) | copy-start | bytes 1540
  125.6 23.8 %copy-start.22 = (f32[2]{0:T(128)S(1)}, f32[2]{0:T(128)}, u32[]{:S(2)}) copy-start(f32[2]{0:T(128)} %copy-done.21) | copy-start | bytes 28
  125.6 23.8 %copy-start.25 = (f32[2,64,64]{1,2,0:T(8,128)S(1)}, f32[2,64,64]{1,2,0:T(8,128)}, u32[]{:S(2)}) copy-start(f32[2,64,64]{1,2,0:T(8,128)} %convolution_add_fusion.1) | copy-start | bytes 98308
  146.8 4.4 %copy-start.20 = (f32[2]{0:T(128)S(1)}, f32[2]{0:T(128)}, u32[]{:S(2)}) copy-start(f32[2]{0:T(128)} %copy-done.19) | copy-start | bytes 28
  147.3 3.1 %collective-permute-start.7 = (bf16[128,2,128]{0,2,1:T(8,128)(2,1)S(1)}, bf16[128,2,128]{0,2,1:T(8,128)(2,1)S(1)}, u32[]{:S(2)}, u32[]{:S(2)}) collective-permute-start(bf16[128,2,128]{0,2,1:T(8,128)(2,1)S(1)} %pad_maximum_fusion.7), channel_id=1, source_target_pairs={{0,16},{16,0},{32,48},{48,32},{64,80},{80,64},{96,112},{112,96},{1... | collective-permute-start | bytes 196616 | tf_op jit(solution)/shard_map/ppermute | solution.py:9
  150.6 6.0 %copy-start.26 = (f32[2,64,64]{1,2,0:T(8,128)S(1)}, f32[2,64,64]{1,2,0:T(8,128)}, u32[]{:S(2)}) copy-start(f32[2,64,64]{1,2,0:T(8,128)} %convolution_add_fusion.1) | copy-start | bytes 98308
  153.0 23.6 %all-to-all-start.5 = ((bf16[16,8,2048]{2,1,0:T(8,128)(2,1)}), bf16[16,8,2048]{2,1,0:T(8,128)(2,1)S(1)}, u32[]{:S(2)}, u32[]{:S(2)}) async-start(bf16[16,8,2048]{2,1,0:T(8,128)(2,1)} %fusion.4), calls=%async_computation.5 | async-start | bytes 1048576 | tf_op jit(solution)/shard_map/all_to_all | solution.py:18
  176.5 21.4 %copy-start.24 = (bf16[2048,2,256]{2,1,0:T(2,128)(2,1)S(1)}, bf16[2048,2,256]{2,1,0:T(2,128)(2,1)}, u32[]{:S(2)}) copy-start(bf16[2048,2,256]{2,1,0:T(2,128)(2,1)} %param.17) | copy-start | bytes 6291460
  201.8 21.8 %all-to-all-start.7 = ((bf16[16,8,2048]{2,1,0:T(8,128)(2,1)}), bf16[16,8,2048]{2,1,0:T(8,128)(2,1)S(1)}, u32[]{:S(2)}, u32[]{:S(2)}) async-start(bf16[16,8,2048]{2,1,0:T(8,128)(2,1)} %fusion.5), calls=%async_computation.7 | async-start | bytes 1048576 | tf_op jit(solution)/shard_map/all_to_all | solution.py:18
  (7 other events, 16.5 us)

commit v5 on v4

--- a/solution.py
+++ b/solution.py
@@ -1,6 +1,8 @@
 import jax
 import jax.numpy as jnp
 from jax import lax
+from jax.experimental import pallas as pl
+from jax.experimental.pallas import tpu as pltpu
 from jax.sharding import PartitionSpec as P
 
 
@@ -18,10 +20,12 @@
     return lax.all_to_all(blocks, "tp", 0, 0, tiled=True)
 
 
-def gather_rows(rows):
-    members = lax.axis_size("tp")
-    blocks = exchange(jnp.broadcast_to(rows[None], (members,) + rows.shape))
-    return blocks.reshape((-1, rows.shape[1]))
+def spread(rows):
+    return jnp.broadcast_to(rows[None], (lax.axis_size("tp"),) + rows.shape)
+
+
+def gather_rows(blocks):
+    return exchange(blocks).reshape((-1, blocks.shape[2]))
 
 
 def scatter_sum(partial, *beside):
@@ -32,19 +36,38 @@
     return (jnp.sum(blocks.astype(jnp.float32), axis=0), *beside)
 
 
-def feed_forward(rows, wide, other_wide, down_pair):
-    hidden = []
-    for weight in (wide, other_wide):
-        gate_up = jnp.einsum("sd,tdf->stf", rows, weight, preferred_element_type=jnp.float32)
-        hidden.append((jax.nn.silu(gate_up[:, 0]) * gate_up[:, 1]).astype(jnp.bfloat16))
-    hidden = jnp.concatenate(hidden, axis=1)
-    return jnp.dot(hidden, down_pair, preferred_element_type=jnp.float32).astype(jnp.bfloat16)
+def feed_forward(rows, wide, other_wide, down, other_down):
+    total = None
+    for weight, narrow in ((wide, down), (other_wide, other_down)):
+        gate_up = jnp.einsum("sd,dtf->stf", rows, weight, preferred_element_type=jnp.float32)
+        hidden = (jax.nn.silu(gate_up[:, 0]) * gate_up[:, 1]).astype(jnp.bfloat16)
+        term = jnp.dot(hidden, narrow, preferred_element_type=jnp.float32)
+        total = term if total is None else total + term
+    return total.astype(jnp.bfloat16)
 
 
 def rms_norm(values, weight):
     floats = values.astype(jnp.float32)
     scaled = floats * lax.rsqrt(jnp.mean(floats * floats, axis=-1, keepdims=True) + 1e-05)
     return (scaled * weight).astype(jnp.bfloat16)
+
+
+def first_kernel(rows_ref, gains_ref, out_ref):
+    depth = lax.axis_index("layer") // 2
+    normed = rms_norm(rows_ref[...], gains_ref[pl.ds(depth, 1), :])
+    for member in range(out_ref.shape[0]):
+        out_ref[member] = normed
+
+
+def first_blocks(rows, gains):
+    members = lax.axis_size("tp")
+    return pl.pallas_call(
+        first_kernel,
+        out_shape=jax.ShapeDtypeStruct((members,) + rows.shape, rows.dtype),
+        in_specs=[pl.BlockSpec(memory_space=pltpu.VMEM)] * 2,
+        out_specs=pl.BlockSpec(memory_space=pltpu.VMEM),
+        name="first_blocks",
+    )(rows, gains)
 
 
 def lifted(values):
@@ -100,10 +123,8 @@
     out_pair = lax.optimization_barrier(
         jnp.concatenate([proj_out, swap_halves(proj_out)], axis=0)
     )
-    wide = lax.optimization_barrier(jnp.transpose(proj_gate_up, (1, 0, 2)))
-    other_wide = swap_halves(wide)
-    down_pair = jnp.concatenate([proj_down, swap_halves(proj_down)], axis=0)
-    feed_weights = lax.optimization_barrier((wide, other_wide, down_pair))
+    other_wide = swap_halves(proj_gate_up)
+    other_down = swap_halves(proj_down)
     fresh_rows = lax.dynamic_index_in_dim(fresh, half, 0, keepdims=False)
     memory_pair = jnp.concatenate([memory_state, other_state[:, :head_dim]], axis=0)
     totals_pair = jnp.concatenate([memory_norm, other_state[:, head_dim]], axis=0)
@@ -115,8 +136,8 @@
     def project(rows, weight):
         return jnp.dot(rows, weight[0], preferred_element_type=jnp.float32).astype(jnp.bfloat16)
 
-    def apply_layer(rows, memory, totals, wide, other_wide, down_pair, *beside):
-        normed = gather_rows(rms_norm(rows, gain_one))
+    def apply_layer(rows, blocks, memory, totals, other_wide, other_down, *beside):
+        normed = gather_rows(blocks)
         own = project(normed, proj_qkv)
         other = project(normed, other_qkv)
         swapped = swap_halves(jnp.stack([other[:, head_dim:], own[:, head_dim:]], axis=1))
@@ -129,22 +150,24 @@
         attn = jnp.dot(
             blended.reshape(half_len, -1), out_pair, preferred_element_type=jnp.float32
         )
-        attn, memory, totals, wide, other_wide, down_pair, *beside = scatter_sum(
-            attn.astype(jnp.bfloat16), memory, totals, wide, other_wide, down_pair, *beside
+        attn, memory, totals, other_down, *beside = scatter_sum(
+            attn.astype(jnp.bfloat16), memory, totals, other_down, *beside
         )
         hidden_one = (rows.astype(jnp.float32) + attn).astype(jnp.bfloat16)
-        normed_two = gather_rows(rms_norm(hidden_one, gain_two))
-        (ffn,) = scatter_sum(feed_forward(normed_two, wide, other_wide, down_pair))
+        normed_two = gather_rows(spread(rms_norm(hidden_one, gain_two)))
+        (ffn,) = scatter_sum(
+            feed_forward(normed_two, proj_gate_up, other_wide, proj_down, other_down)
+        )
         output = (hidden_one.astype(jnp.float32) + ffn).astype(jnp.bfloat16)
-        return (output, memory, totals, wide, other_wide, down_pair, *beside)
+        return (output, memory, totals, other_wide, other_down, *beside)
 
-    first_rows, memory_one, totals_one, *feed_weights, fresh_rows = apply_layer(
-        acts, memory_pair, totals_pair, *feed_weights, fresh_rows
+    first_rows, memory_one, totals_one, other_wide, other_down, fresh_rows = apply_layer(
+        acts, first_blocks(acts, norm_first), memory_pair, totals_pair, other_wide, other_down, fresh_rows
     )
     incoming = next_layer(first_rows)
     entering = jnp.where(depth == 0, fresh_rows, incoming)
     second_rows, memory_two, totals_two, *_ = apply_layer(
-        entering, memory_one, totals_one, *feed_weights
+        entering, spread(rms_norm(entering, gain_one)), memory_one, totals_one, other_wide, other_down
     )
     return (first_rows, second_rows, memory_two[:1], totals_two[:1])
 

time: 226 us -> 233 us (1.031)
  matrix products: 14.9 us -> 24.1 us
  waiting for transfers between devices: 63.9 us -> 59.9 us
  local copies, waits for them, and re-layouts: 6.3 us -> 8.98 us
    all_to_all x4, waiting for transfers between devices: 57.2 us -> 54.5 us  [exchange(): return lax.all_to_all(blocks, 'tp', 0, 0, tiled=True)]
    dot_general x6 -> x8, matrix products: 6.67 us -> 6.35 us  [the longest x4 4.58 us: feed_forward(): term = jnp.dot(hidden, narrow, preferred_element_type=jnp.float32)]
  transfers between devices with their start and end apart: 12 -> 12, of which waited for: 7 -> 7; matrix products, arithmetic and copies ran while one was open for 6% -> 12% of each run, Pallas kernels for 0% -> 0%
where the time goes in v5:
time: 233 us; the launch traced here: 231 us
  blocking collectives  84.7 us (36%)
  waiting for transfers between devices  59.9 us (26%)
  starting transfers between devices  41.5 us (18%)
  matrix products  24.1 us (10%)
  local copies, waits for them, and re-layouts  8.98 us (4%)
  other arithmetic  7.87 us (3%)
    all_to_all x4, blocking collectives, exchange(): return lax.all_to_all(blocks, 'tp', 0, 0, tiled=True)  84.7 us
    all_to_all x4, waiting for transfers between devices, exchange(): return lax.all_to_all(blocks, 'tp', 0, 0, tiled=True)  54.5 us
    all_to_all x4, starting transfers between devices, exchange(): return lax.all_to_all(blocks, 'tp', 0, 0, tiled=True)  23.5 us
    ppermute x7, starting transfers between devices, swap_halves(): return lax.ppermute(value, 'layer', pairs)  14.5 us
  transfers between devices with their start and end apart: 12, of which 7 were waited for; matrix products, arithmetic and copies ran while one was open for 12% of the time, Pallas kernels for 0%

profile of v5, /device:TPU:2, one launch (start us, length us, event | category | flops | bytes accessed | tf_op | source)
XLA Modules:
  0.0 231.0 jit_solution(93270416448236455)
XLA Ops:
  0.7 1.9 first_blocks.1
  2.6 12.1 %all-to-all-start = ((bf16[16,8,2048]{2,1,0:T(8,128)(2,1)}), bf16[16,8,2048]{2,1,0:T(8,128)(2,1)S(1)}, u32[]{:S(2)}, u32[]{:S(2)}) async-start(bf16[16,8,2048]{2,1,0:T(8,128)(2,1)} %first_blocks.1), calls=%async_computation | async-start | bytes 1048576 | tf_op jit(solution)/shard_map/all_to_all | solution.py:20
  14.7 1.9 collective-permute-start.1
  19.0 2.4 %collective-permute-start = (f32[1,66,64]{1,2,0:T(8,128)S(1)}, f32[1,66,64]{1,2,0:T(8,128)S(1)}, u32[]{:S(2)}, u32[]{:S(2)}) collective-permute-start(f32[1,66,64]{1,2,0:T(8,128)S(1)} %maximum_maximum_fusion), channel_id=1, source_target_pairs={{0,16},{16,0},{32,48},{48,32},{64,80},{80,64},{96,112},{112,96},{1... | collective-permute-start | bytes 50696 | tf_op jit(solution)/shard_map/ppermute | solution.py:11
  21.4 1.9 collective-permute-start.3
  23.4 2.4 %collective-permute-start.4 = (bf16[256,2048]{1,0:T(8,128)(2,1)}, bf16[256,2048]{1,0:T(8,128)(2,1)}, u32[]{:S(2)}, u32[]{:S(2)}) collective-permute-start(bf16[256,2048]{1,0:T(8,128)(2,1)} %param.18), channel_id=1, source_target_pairs={{0,16},{16,0},{32,48},{48,32},{64,80},{80,64},{96,112},{112,96},{1... | collective-permute-start | bytes 3145736 | tf_op jit(solution)/shard_map/ppermute | solution.py:11
  26.5 1.3 broadcast_subtract_fusion
  28.0 5.5 %all-to-all-done = bf16[16,8,2048]{2,1,0:T(8,128)(2,1)S(1)} async-done(((bf16[16,8,2048]{2,1,0:T(8,128)(2,1)}), bf16[16,8,2048]{2,1,0:T(8,128)(2,1)S(1)}, u32[]{:S(2)}, u32[]{:S(2)}) %all-to-all-start) | async-done | bytes 524320 | tf_op jit(solution)/shard_map/all_to_all | solution.py:20
  34.3 1.9 collective-permute-start.2
  41.8 1.6 fusion.21
  43.4 2.3 fusion.22
  45.7 1.9 fusion.4
  47.6 4.2 %all-to-all-start.1 = ((bf16[16,8,2048]{2,1,0:T(8,128)(2,1)}), bf16[16,8,2048]{2,1,0:T(8,128)(2,1)}, u32[]{:S(2)}, u32[]{:S(2)}) async-start(bf16[16,8,2048]{2,1,0:T(8,128)(2,1)} %fusion.4), calls=%async_computation.1 | async-start | bytes 1048576 | tf_op jit(solution)/shard_map/all_to_all | solution.py:20
  51.8 1.6 copy.28
  53.4 2.1 collective-permute-start.5
  55.5 1.4 dynamic-slice_bitcast_fusion
  56.9 1.8 convolution_add_fusion.3
  58.7 13.1 %all-to-all-done.1 = bf16[16,8,2048]{2,1,0:T(8,128)(2,1)} async-done(((bf16[16,8,2048]{2,1,0:T(8,128)(2,1)}), bf16[16,8,2048]{2,1,0:T(8,128)(2,1)}, u32[]{:S(2)}, u32[]{:S(2)}) %all-to-all-start.1) | async-done | bytes 524320 | tf_op jit(solution)/shard_map/all_to_all | solution.py:20
  74.2 21.1 %all_to_all.40 = bf16[16,8,2048]{2,1,0:T(8,128)(2,1)S(1)} all-to-all(bf16[16,8,2048]{2,1,0:T(8,128)(2,1)S(1)} %broadcast_in_dim.41), channel_id=1, replica_groups=mesh['layer'=32,'tp'=16] {'tp'}, dimensions={0} | all-to-all | bytes 1048576 | tf_op jit(solution)/shard_map/all_to_all | solution.py:20
  96.5 1.6 fusion.7
  98.0 21.7 %all_to_all.41 = bf16[16,8,2048]{2,1,0:T(8,128)(2,1)S(1)} all-to-all(bf16[16,8,2048]{2,1,0:T(8,128)(2,1)S(1)} %fusion.7), channel_id=1, replica_groups=mesh['layer'=32,'tp'=16] {'tp'}, dimensions={0} | all-to-all | bytes 1048576 | tf_op jit(solution)/shard_map/all_to_all | solution.py:20
  120.4 3.5 %collective-permute-start.6 = (bf16[8,2048]{1,0:T(8,128)(2,1)}, bf16[8,2048]{1,0:T(8,128)(2,1)}, u32[]{:S(2)}, u32[]{:S(2)}) collective-permute-start(bf16[8,2048]{1,0:T(8,128)(2,1)} %fusion.59), channel_id=1, source_target_pairs={{0,32},{16,48},{32,64},{48,80},{64,96},{80,112},{96,128},{112,144}... | collective-permute-start | bytes 98312 | tf_op jit(solution)/shard_map/ppermute | solution.py:16
  124.8 4.1 %collective-permute-done.6 = bf16[8,2048]{1,0:T(8,128)(2,1)} collective-permute-done((bf16[8,2048]{1,0:T(8,128)(2,1)}, bf16[8,2048]{1,0:T(8,128)(2,1)}, u32[]{:S(2)}, u32[]{:S(2)}) %collective-permute-start.6) | collective-permute-done | bytes 32800 | tf_op jit(solution)/shard_map/ppermute | solution.py:16
  130.5 20.9 %all_to_all.42 = bf16[16,8,2048]{2,1,0:T(8,128)(2,1)S(1)} all-to-all(bf16[16,8,2048]{2,1,0:T(8,128)(2,1)S(1)} %broadcast_in_dim.42), channel_id=1, replica_groups=mesh['layer'=32,'tp'=16] {'tp'}, dimensions={0} | all-to-all | bytes 1048576 | tf_op jit(solution)/shard_map/all_to_all | solution.py:20
  151.5 1.5 convolution_convert_fusion.2
  153.4 1.9 collective-permute-start.7
  159.9 3.6 %all-to-all-start.5 = ((bf16[16,8,2048]{2,1,0:T(8,128)(2,1)}), bf16[16,8,2048]{2,1,0:T(8,128)(2,1)S(1)}, u32[]{:S(2)}, u32[]{:S(2)}) async-start(bf16[16,8,2048]{2,1,0:T(8,128)(2,1)} %fusion.5), calls=%async_computation.5 | async-start | bytes 1048576 | tf_op jit(solution)/shard_map/all_to_all | solution.py:20
  164.6 18.8 %all-to-all-done.5 = bf16[16,8,2048]{2,1,0:T(8,128)(2,1)S(1)} async-done(((bf16[16,8,2048]{2,1,0:T(8,128)(2,1)}), bf16[16,8,2048]{2,1,0:T(8,128)(2,1)S(1)}, u32[]{:S(2)}, u32[]{:S(2)}) %all-to-all-start.5) | async-done | bytes 524320 | tf_op jit(solution)/shard_map/all_to_all | solution.py:20
  183.8 21.1 %all_to_all.43 = bf16[16,8,2048]{2,1,0:T(8,128)(2,1)S(1)} all-to-all(bf16[16,8,2048]{2,1,0:T(8,128)(2,1)S(1)} %broadcast_in_dim.43), channel_id=1, replica_groups=mesh['layer'=32,'tp'=16] {'tp'}, dimensions={0} | all-to-all | bytes 1048576 | tf_op jit(solution)/shard_map/all_to_all | solution.py:20
  206.1 2.4 %fusion.6 = bf16[16,8,2048]{2,1,0:T(8,128)(2,1)} fusion(f32[128,2048]{1,0:T(8,128)S(1)} %fusion.71, bf16[256,2048]{1,0:T(8,128)(2,1)} %collective-permute-done.4, f32[128,2,256]{2,0,1:T(8,128)S(1)} %fusion.28), kind=kOutput, calls=%fused_computation.10 | convolution fusion | flops 134938624 | bytes 2883584 | tf_op jit(solution)/shard_map/dot_general | solution.py:44
  208.5 3.6 %all-to-all-start.7 = ((bf16[16,8,2048]{2,1,0:T(8,128)(2,1)}), bf16[16,8,2048]{2,1,0:T(8,128)(2,1)S(1)}, u32[]{:S(2)}, u32[]{:S(2)}) async-start(bf16[16,8,2048]{2,1,0:T(8,128)(2,1)} %fusion.6), calls=%async_computation.7 | async-start | bytes 1048576 | tf_op jit(solution)/shard_map/all_to_all | solution.py:20
  213.3 17.0 %all-to-all-done.7 = bf16[16,8,2048]{2,1,0:T(8,128)(2,1)S(1)} async-done(((bf16[16,8,2048]{2,1,0:T(8,128)(2,1)}), bf16[16,8,2048]{2,1,0:T(8,128)(2,1)S(1)}, u32[]{:S(2)}, u32[]{:S(2)}) %all-to-all-start.7) | async-done | bytes 524320 | tf_op jit(solution)/shard_map/all_to_all | solution.py:20
  (119 shorter events, 25.1 us)
Async XLA Ops:
  0.6 54.9 %copy-start = (f32[16,2048]{1,0:T(8,128)S(1)}, f32[16,2048]{1,0:T(8,128)}, u32[]{:S(2)}) copy-start(f32[16,2048]{1,0:T(8,128)} %param.14) | copy-start | bytes 393220
  0.6 27.3 %copy-start.13 = (bf16[64,2048]{1,0:T(8,128)(2,1)S(1)}, bf16[64,2048]{1,0:T(8,128)(2,1)}, u32[]{:S(2)}) copy-start(bf16[64,2048]{1,0:T(8,128)(2,1)} %param.16) | copy-start | bytes 786436
  2.6 31.3 %copy-start.3 = (bf16[1,2048,192]{1,2,0:T(8,128)(2,1)S(1)}, bf16[1,2048,192]{1,2,0:T(8,128)(2,1)}, u32[]{:S(2)}) copy-start(bf16[1,2048,192]{1,2,0:T(8,128)(2,1)} %param.15) | copy-start | bytes 2359300
  2.6 30.9 %all-to-all-start = ((bf16[16,8,2048]{2,1,0:T(8,128)(2,1)}), bf16[16,8,2048]{2,1,0:T(8,128)(2,1)S(1)}, u32[]{:S(2)}, u32[]{:S(2)}) async-start(bf16[16,8,2048]{2,1,0:T(8,128)(2,1)} %first_blocks.1), calls=%async_computation | async-start | bytes 1048576 | tf_op jit(solution)/shard_map/all_to_all | solution.py:20
  14.7 13.3 %collective-permute-start.1 = (bf16[1,2048,192]{1,2,0:T(8,128)(2,1)}, bf16[1,2048,192]{1,2,0:T(8,128)(2,1)S(1)}, u32[]{:S(2)}, u32[]{:S(2)}) collective-permute-start(bf16[1,2048,192]{1,2,0:T(8,128)(2,1)} %param.15), channel_id=1, source_target_pairs={{0,16},{16,0},{32,48},{48,32},{64,80},{80,64},{96,112},{112,96},{1... | collective-permute-start | bytes 2359304 | tf_op jit(solution)/shard_map/ppermute | solution.py:11
  17.5 8.4 %copy-start.15 = (f32[1,64,64]{1,2,0:T(8,128)}, f32[1,64,64]{1,2,0:T(8,128)S(1)}, u32[]{:S(2)}) copy-start(f32[1,64,64]{1,2,0:T(8,128)S(1)} %copy.24) | copy-start | bytes 49156
  19.0 6.8 %collective-permute-start = (f32[1,66,64]{1,2,0:T(8,128)S(1)}, f32[1,66,64]{1,2,0:T(8,128)S(1)}, u32[]{:S(2)}, u32[]{:S(2)}) collective-permute-start(f32[1,66,64]{1,2,0:T(8,128)S(1)} %maximum_maximum_fusion), channel_id=1, source_target_pairs={{0,16},{16,0},{32,48},{48,32},{64,80},{80,64},{96,112},{112,96},{1... | collective-permute-start | bytes 50696 | tf_op jit(solution)/shard_map/ppermute | solution.py:11
  21.4 6.5 %collective-permute-start.3 = (bf16[64,2048]{1,0:T(8,128)(2,1)}, bf16[64,2048]{1,0:T(8,128)(2,1)S(1)}, u32[]{:S(2)}, u32[]{:S(2)}) collective-permute-start(bf16[64,2048]{1,0:T(8,128)(2,1)} %param.16), channel_id=1, source_target_pairs={{0,16},{16,0},{32,48},{48,32},{64,80},{80,64},{96,112},{112,96},{1... | collective-permute-start | bytes 786440 | tf_op jit(solution)/shard_map/ppermute | solution.py:11
  23.4 35.3 %collective-permute-start.4 = (bf16[256,2048]{1,0:T(8,128)(2,1)}, bf16[256,2048]{1,0:T(8,128)(2,1)}, u32[]{:S(2)}, u32[]{:S(2)}) collective-permute-start(bf16[256,2048]{1,0:T(8,128)(2,1)} %param.18), channel_id=1, source_target_pairs={{0,16},{16,0},{32,48},{48,32},{64,80},{80,64},{96,112},{112,96},{1... | collective-permute-start | bytes 3145736 | tf_op jit(solution)/shard_map/ppermute | solution.py:11
  25.9 13.3 %copy-start.8 = (pred[128,256]{1,0:T(8,128)(4,1)}, pred[128,256]{1,0:T(8,128)(4,1)S(1)}, u32[]{:S(2)}) copy-start(pred[128,256]{1,0:T(8,128)(4,1)S(1)} %concatenate.45) | copy-start | bytes 98308
  27.7 15.7 %copy-start.20 = (f32[2]{0:T(128)}, f32[2]{0:T(128)S(1)}, u32[]{:S(2)}) copy-start(f32[2]{0:T(128)S(1)} %get-tuple-element.40) | copy-start | bytes 28
  28.0 12.2 %copy-start.19 = (f32[1,64]{1,0:T(1,128)S(1)}, f32[1,64]{1,0:T(1,128)}, u32[]{:S(2)}) copy-start(f32[1,64]{1,0:T(1,128)} %param.20) | copy-start | bytes 772
  28.0 12.1 %copy-start.4 = (bf16[1,2048,192]{1,2,0:T(8,128)(2,1)}, bf16[1,2048,192]{1,2,0:T(8,128)(2,1)S(1)}, u32[]{:S(2)}) copy-start(bf16[1,2048,192]{1,2,0:T(8,128)(2,1)S(1)} %collective-permute-done.1) | copy-start | bytes 2359300
  34.3 3.1 %collective-permute-start.2 = (bf16[128,2,128]{0,2,1:T(8,128)(2,1)S(1)}, bf16[128,2,128]{0,2,1:T(8,128)(2,1)S(1)}, u32[]{:S(2)}, u32[]{:S(2)}) collective-permute-start(bf16[128,2,128]{0,2,1:T(8,128)(2,1)S(1)} %pad_maximum_fusion.4), channel_id=1, source_target_pairs={{0,16},{16,0},{32,48},{48,32},{64,80},{80,64},{96,112},{112,96},{1... | collective-permute-start | bytes 196616 | tf_op jit(solution)/shard_map/ppermute | solution.py:11
  40.2 11.7 %copy-start.5 = (bf16[2048,2,256]{2,1,0:T(2,128)(2,1)S(1)}, bf16[2048,2,256]{2,1,0:T(2,128)(2,1)}, u32[]{:S(2)}) copy-start(bf16[2048,2,256]{2,1,0:T(2,128)(2,1)} %param.17) | copy-start | bytes 6291460
  47.6 24.3 %all-to-all-start.1 = ((bf16[16,8,2048]{2,1,0:T(8,128)(2,1)}), bf16[16,8,2048]{2,1,0:T(8,128)(2,1)}, u32[]{:S(2)}, u32[]{:S(2)}) async-start(bf16[16,8,2048]{2,1,0:T(8,128)(2,1)} %fusion.4), calls=%async_computation.1 | async-start | bytes 1048576 | tf_op jit(solution)/shard_map/all_to_all | solution.py:20
  53.4 42.6 %collective-permute-start.5 = (bf16[2048,2,256]{2,0,1:T(8,128)(2,1)}, bf16[2048,2,256]{2,0,1:T(8,128)(2,1)S(1)}, u32[]{:S(2)}, u32[]{:S(2)}) collective-permute-start(bf16[2048,2,256]{2,0,1:T(8,128)(2,1)} %copy.28), channel_id=1, source_target_pairs={{0,16},{16,0},{32,48},{48,32},{64,80},{80,64},{96,112},{112,96},{1... | collective-permute-start | bytes 6291464 | tf_op jit(solution)/shard_map/ppermute | solution.py:11
  71.8 23.4 %copy-start.6 = (bf16[2048,2,256]{2,1,0:T(2,128)(2,1)S(1)}, bf16[2048,2,256]{2,1,0:T(2,128)(2,1)}, u32[]{:S(2)}) copy-start(bf16[2048,2,256]{2,1,0:T(2,128)(2,1)} %param.17) | copy-start | bytes 6291460
  74.2 21.5 %copy-start.1 = (bf16[256,2048]{1,0:T(8,128)(2,1)S(1)}, bf16[256,2048]{1,0:T(8,128)(2,1)}, u32[]{:S(2)}) copy-start(bf16[256,2048]{1,0:T(8,128)(2,1)} %param.18) | copy-start | bytes 3145732
  120.4 8.4 %collective-permute-start.6 = (bf16[8,2048]{1,0:T(8,128)(2,1)}, bf16[8,2048]{1,0:T(8,128)(2,1)}, u32[]{:S(2)}, u32[]{:S(2)}) collective-permute-start(bf16[8,2048]{1,0:T(8,128)(2,1)} %fusion.59), channel_id=1, source_target_pairs={{0,32},{16,48},{32,64},{48,80},{64,96},{80,112},{96,128},{112,144}... | collective-permute-start | bytes 98312 | tf_op jit(solution)/shard_map/ppermute | solution.py:16
  130.5 24.8 %copy-start.18 = (f32[2,64]{1,0:T(2,128)S(1)}, f32[2,64]{1,0:T(2,128)}, u32[]{:S(2)}) copy-start(f32[2,64]{1,0:T(2,128)} %get-tuple-element.17) | copy-start | bytes 1540
  130.5 25.0 %copy-start.22 = (f32[2]{0:T(128)S(1)}, f32[2]{0:T(128)}, u32[]{:S(2)}) copy-start(f32[2]{0:T(128)} %get-tuple-element.41) | copy-start | bytes 28
  130.5 25.0 %copy-start.23 = (f32[2,64,64]{1,2,0:T(8,128)S(1)}, f32[2,64,64]{1,2,0:T(8,128)}, u32[]{:S(2)}) copy-start(f32[2,64,64]{1,2,0:T(8,128)} %convolution_add_fusion.3) | copy-start | bytes 98308
  151.5 5.2 %copy-start.9 = (pred[128,256]{1,0:T(8,128)(4,1)S(1)}, pred[128,256]{1,0:T(8,128)(4,1)}, u32[]{:S(2)}) copy-start(pred[128,256]{1,0:T(8,128)(4,1)} %copy-done.8) | copy-start | bytes 98308
  153.0 5.1 %copy-start.21 = (f32[2]{0:T(128)S(1)}, f32[2]{0:T(128)}, u32[]{:S(2)}) copy-start(f32[2]{0:T(128)} %copy-done.20) | copy-start | bytes 28
  153.4 3.1 %collective-permute-start.7 = (bf16[128,2,128]{0,2,1:T(8,128)(2,1)S(1)}, bf16[128,2,128]{0,2,1:T(8,128)(2,1)S(1)}, u32[]{:S(2)}, u32[]{:S(2)}) collective-permute-start(bf16[128,2,128]{0,2,1:T(8,128)(2,1)S(1)} %pad_maximum_fusion.6), channel_id=1, source_target_pairs={{0,16},{16,0},{32,48},{48,32},{64,80},{80,64},{96,112},{112,96},{1... | collective-permute-start | bytes 196616 | tf_op jit(solution)/shard_map/ppermute | solution.py:11
  156.5 3.3 %copy-start.17 = (bf16[128,2,64]{0,2,1:T(8,128)(2,1)}, bf16[128,2,64]{0,2,1:T(8,128)(2,1)S(1)}, u32[]{:S(2)}) copy-start(bf16[128,2,64]{0,2,1:T(8,128)(2,1)S(1)} %get-tuple-element.46) | copy-start | bytes 98308
  158.1 25.4 %copy-start.11 = (bf16[8,2048]{1,0:T(8,128)(2,1)S(1)}, bf16[8,2048]{1,0:T(8,128)(2,1)}, u32[]{:S(2)}) copy-start(bf16[8,2048]{1,0:T(8,128)(2,1)} %copy-done.10) | copy-start | bytes 98308
  159.9 23.6 %all-to-all-start.5 = ((bf16[16,8,2048]{2,1,0:T(8,128)(2,1)}), bf16[16,8,2048]{2,1,0:T(8,128)(2,1)S(1)}, u32[]{:S(2)}, u32[]{:S(2)}) async-start(bf16[16,8,2048]{2,1,0:T(8,128)(2,1)} %fusion.5), calls=%async_computation.5 | async-start | bytes 1048576 | tf_op jit(solution)/shard_map/all_to_all | solution.py:20
  183.4 21.4 %copy-start.7 = (bf16[2048,2,256]{2,1,0:T(2,128)(2,1)S(1)}, bf16[2048,2,256]{2,1,0:T(2,128)(2,1)}, u32[]{:S(2)}) copy-start(bf16[2048,2,256]{2,1,0:T(2,128)(2,1)} %param.17) | copy-start | bytes 6291460
  183.8 21.5 %copy-start.2 = (bf16[256,2048]{1,0:T(8,128)(2,1)S(1)}, bf16[256,2048]{1,0:T(8,128)(2,1)}, u32[]{:S(2)}) copy-start(bf16[256,2048]{1,0:T(8,128)(2,1)} %param.18) | copy-start | bytes 3145732
  208.5 21.8 %all-to-all-start.7 = ((bf16[16,8,2048]{2,1,0:T(8,128)(2,1)}), bf16[16,8,2048]{2,1,0:T(8,128)(2,1)S(1)}, u32[]{:S(2)}, u32[]{:S(2)}) async-start(bf16[16,8,2048]{2,1,0:T(8,128)(2,1)} %fusion.6), calls=%async_computation.7 | async-start | bytes 1048576 | tf_op jit(solution)/shard_map/all_to_all | solution.py:20
  (4 other events, 7.9 us)

commit v6 on v2

--- a/solution.py
+++ b/solution.py
@@ -1,6 +1,8 @@
 import jax
 import jax.numpy as jnp
 from jax import lax
+from jax.experimental import pallas as pl
+from jax.experimental.pallas import tpu as pltpu
 from jax.sharding import PartitionSpec as P
 
 
@@ -18,10 +20,12 @@
     return lax.all_to_all(blocks, "tp", 0, 0, tiled=True)
 
 
-def gather_rows(rows):
-    members = lax.axis_size("tp")
-    blocks = exchange(jnp.broadcast_to(rows[None], (members,) + rows.shape))
-    return blocks.reshape((-1, rows.shape[1]))
+def spread(rows):
+    return jnp.broadcast_to(rows[None], (lax.axis_size("tp"),) + rows.shape)
+
+
+def gather_rows(blocks):
+    return exchange(blocks).reshape((-1, blocks.shape[2]))
 
 
 def scatter_sum(partial):
@@ -34,6 +38,24 @@
     floats = values.astype(jnp.float32)
     scaled = floats * lax.rsqrt(jnp.mean(floats * floats, axis=-1, keepdims=True) + 1e-05)
     return (scaled * weight).astype(jnp.bfloat16)
+
+
+def first_kernel(rows_ref, gains_ref, out_ref):
+    depth = lax.axis_index("layer") // 2
+    normed = rms_norm(rows_ref[...], gains_ref[pl.ds(depth, 1), :])
+    for member in range(out_ref.shape[0]):
+        out_ref[member] = normed
+
+
+def first_blocks(rows, gains):
+    members = lax.axis_size("tp")
+    return pl.pallas_call(
+        first_kernel,
+        out_shape=jax.ShapeDtypeStruct((members,) + rows.shape, rows.dtype),
+        in_specs=[pl.BlockSpec(memory_space=pltpu.VMEM)] * 2,
+        out_specs=pl.BlockSpec(memory_space=pltpu.VMEM),
+        name="first_blocks",
+    )(rows, gains)
 
 
 def lifted(values):
@@ -86,9 +108,10 @@
     state = jnp.concatenate([memory_state, memory_norm[:, None], logit_row], axis=1)
     other_state = swap_halves(state)
     wide = lax.optimization_barrier(jnp.transpose(proj_gate_up, (1, 0, 2)))
-    qkv_pair, out_pair, wide_pair, down_pair = (
+    other_qkv = swap_halves(proj_qkv)
+    out_pair, wide_pair, down_pair = (
         lax.optimization_barrier(jnp.concatenate([weight, swap_halves(weight)], axis=axis))
-        for weight, axis in ((proj_qkv, 0), (proj_out, 0), (wide, 2), (proj_down, 0))
+        for weight, axis in ((proj_out, 0), (wide, 2), (proj_down, 0))
     )
     memory_pair = jnp.concatenate([memory_state, other_state[:, :head_dim]], axis=0)
     totals_pair = jnp.concatenate([memory_norm, other_state[:, head_dim]], axis=0)
@@ -97,18 +120,21 @@
     causal = index[:, None] >= index[None, :]
     allowed = jnp.concatenate([causal, jnp.broadcast_to(half == 1, causal.shape)], axis=1)
 
+    def project(rows, weight):
+        return jnp.dot(rows, weight[0], preferred_element_type=jnp.float32).astype(jnp.bfloat16)
+
     def expand(rows):
         gate, up = (
             jnp.dot(rows, weight, preferred_element_type=jnp.float32) for weight in wide_pair
         )
         return (jax.nn.silu(gate) * up).astype(jnp.bfloat16)
 
-    def apply_layer(rows, memory, totals):
-        normed = gather_rows(rms_norm(rows, gain_one))
-        both = jnp.einsum(
-            "sd,hdc->shc", normed, qkv_pair, preferred_element_type=jnp.float32
-        ).astype(jnp.bfloat16)
-        swapped = swap_halves(both[:, ::-1, head_dim:])
+    def apply_layer(rows, blocks, memory, totals):
+        normed = gather_rows(blocks)
+        own = project(normed, proj_qkv)
+        other = project(normed, other_qkv)
+        swapped = swap_halves(jnp.stack([other[:, head_dim:], own[:, head_dim:]], axis=1))
+        both = jnp.stack([own, other], axis=1)
         queries = both[..., :head_dim]
         keyed = jnp.concatenate([both[..., head_dim : 2 * head_dim], swapped[..., :head_dim]], axis=0)
         valued = jnp.concatenate([both[..., 2 * head_dim :], swapped[..., head_dim:]], axis=0)
@@ -119,17 +145,17 @@
         )
         attn = scatter_sum(attn.astype(jnp.bfloat16))
         hidden_one = (rows.astype(jnp.float32) + attn).astype(jnp.bfloat16)
-        normed_two = gather_rows(rms_norm(hidden_one, gain_two))
+        normed_two = gather_rows(spread(rms_norm(hidden_one, gain_two)))
         down = jnp.dot(expand(normed_two), down_pair, preferred_element_type=jnp.float32)
         ffn = scatter_sum(down.astype(jnp.bfloat16))
         output = (hidden_one.astype(jnp.float32) + ffn).astype(jnp.bfloat16)
         return (output, memory, totals)
 
-    first_rows, memory_one, totals_one = apply_layer(acts, memory_pair, totals_pair)
+    first_rows, memory_one, totals_one = apply_layer(acts, first_blocks(acts, norm_first), memory_pair, totals_pair)
     incoming = next_layer(first_rows)
     fresh_rows = lax.dynamic_index_in_dim(fresh, half, 0, keepdims=False)
     entering = jnp.where(depth == 0, fresh_rows, incoming)
-    second_rows, memory_two, totals_two = apply_layer(entering, memory_one, totals_one)
+    second_rows, memory_two, totals_two = apply_layer(entering, spread(rms_norm(entering, gain_one)), memory_one, totals_one)
     return (first_rows, second_rows, memory_two[:1], totals_two[:1])
 
 

time: 224 us -> 224 us (level)
    concatenate x4 -> x3, other arithmetic: 8.89 us -> 7.04 us  [body(): jnp.concatenate([weight, swap_halves(weight)], axis=axis)]
    unnamed x45 -> x75, local copies, waits for them, and re-layouts: 4.85 us -> 4.16 us
  transfers between devices with their start and end apart: 13 -> 13, of which waited for: 8 -> 8; matrix products, arithmetic and copies ran while one was open for 11% -> 9% of each run, Pallas kernels for 0% -> 0%
where the time goes in v6:
time: 224 us; the launch traced here: 222 us
  waiting for transfers between devices  68.6 us (31%)
  blocking collectives  63.9 us (29%)
  starting transfers between devices  45.5 us (20%)
  matrix products  16.8 us (8%)
  other arithmetic  14.4 us (6%)
  local copies, waits for them, and re-layouts  8.89 us (4%)
    all_to_all x3, blocking collectives, exchange(): return lax.all_to_all(blocks, 'tp', 0, 0, tiled=True)  63.9 us
    all_to_all x5, waiting for transfers between devices, exchange(): return lax.all_to_all(blocks, 'tp', 0, 0, tiled=True)  62.9 us
    all_to_all x5, starting transfers between devices, exchange(): return lax.all_to_all(blocks, 'tp', 0, 0, tiled=True)  27.6 us
    ppermute x7, starting transfers between devices, swap_halves(): return lax.ppermute(value, 'layer', pairs)  14.4 us
    concatenate x3, other arithmetic, body(): jnp.concatenate([weight, swap_halves(weight)], axis=axis)  7.04 us
    dot_general x2, matrix products, apply_layer(): jnp.dot(expand(normed_two), down_pair, preferred_element_type=jnp.float32)  6.63 us
  transfers between devices with their start and end apart: 13, of which 8 were waited for; matrix products, arithmetic and copies ran while one was open for 9% of the time, Pallas kernels for 0%

profile of v6, /device:TPU:2, one launch (start us, length us, event | category | flops | bytes accessed | tf_op | source)
XLA Modules:
  0.0 222.2 jit_solution(8388758743350620255)
XLA Ops:
  0.7 2.0 first_blocks.1
  2.6 12.0 %all-to-all-start = ((bf16[16,8,2048]{2,1,0:T(8,128)(2,1)}), bf16[16,8,2048]{2,1,0:T(8,128)(2,1)S(1)}, u32[]{:S(2)}, u32[]{:S(2)}) async-start(bf16[16,8,2048]{2,1,0:T(8,128)(2,1)} %first_blocks.1), calls=%async_computation | async-start | bytes 1048576 | tf_op jit(solution)/shard_map/all_to_all | solution.py:20
  14.6 1.9 collective-permute-start.1
  19.0 2.4 %collective-permute-start = (f32[1,66,64]{1,2,0:T(8,128)S(1)}, f32[1,66,64]{1,2,0:T(8,128)S(1)}, u32[]{:S(2)}, u32[]{:S(2)}) collective-permute-start(f32[1,66,64]{1,2,0:T(8,128)S(1)} %maximum_maximum_fusion), channel_id=1, source_target_pairs={{0,16},{16,0},{32,48},{48,32},{64,80},{80,64},{96,112},{112,96},{1... | collective-permute-start | bytes 50696 | tf_op jit(solution)/shard_map/ppermute | solution.py:11
  21.4 1.9 collective-permute-start.3
  25.6 7.8 %all-to-all-done = bf16[16,8,2048]{2,1,0:T(8,128)(2,1)S(1)} async-done(((bf16[16,8,2048]{2,1,0:T(8,128)(2,1)}), bf16[16,8,2048]{2,1,0:T(8,128)(2,1)S(1)}, u32[]{:S(2)}, u32[]{:S(2)}) %all-to-all-start) | async-done | bytes 524320 | tf_op jit(solution)/shard_map/all_to_all | solution.py:20
  34.2 1.9 collective-permute-start.2
  38.8 1.1 fusion.2
  40.0 4.3 %all-to-all-start.1 = ((bf16[16,8,2048]{2,1,0:T(8,128)(2,1)}), bf16[16,8,2048]{2,1,0:T(8,128)(2,1)}, u32[]{:S(2)}, u32[]{:S(2)}) async-start(bf16[16,8,2048]{2,1,0:T(8,128)(2,1)} %fusion.2), calls=%async_computation.1 | async-start | bytes 1048576 | tf_op jit(solution)/shard_map/all_to_all | solution.py:20
  44.2 1.9 copy.35
  46.1 2.1 collective-permute-start.4
  48.2 2.3 %collective-permute-start.5 = (bf16[256,2048]{1,0:T(8,128)(2,1)}, bf16[256,2048]{1,0:T(8,128)(2,1)}, u32[]{:S(2)}, u32[]{:S(2)}) collective-permute-start(bf16[256,2048]{1,0:T(8,128)(2,1)} %param.18), channel_id=1, source_target_pairs={{0,16},{16,0},{32,48},{48,32},{64,80},{80,64},{96,112},{112,96},{1... | collective-permute-start | bytes 3145736 | tf_op jit(solution)/shard_map/ppermute | solution.py:11
  50.5 13.8 %all-to-all-done.1 = bf16[16,8,2048]{2,1,0:T(8,128)(2,1)} async-done(((bf16[16,8,2048]{2,1,0:T(8,128)(2,1)}), bf16[16,8,2048]{2,1,0:T(8,128)(2,1)}, u32[]{:S(2)}, u32[]{:S(2)}) %all-to-all-start.1) | async-done | bytes 524320 | tf_op jit(solution)/shard_map/all_to_all | solution.py:20
  64.3 1.1 convert_reduce_fusion.3
  67.8 4.2 %all-to-all-start.2 = ((bf16[16,8,2048]{2,1,0:T(8,128)(2,1)}), bf16[16,8,2048]{2,1,0:T(8,128)(2,1)}, u32[]{:S(2)}, u32[]{:S(2)}) async-start(bf16[16,8,2048]{2,1,0:T(8,128)(2,1)} %broadcast_in_dim.41), calls=%async_computation.2 | async-start | bytes 1048576 | tf_op jit(solution)/shard_map/all_to_all | solution.py:20
  72.1 3.2 %pad_maximum_fusion.1 = bf16[512,2048]{1,0:T(8,128)(2,1)} fusion(bf16[256,2048]{1,0:T(8,128)(2,1)} %collective-permute-done.5, bf16[256,2048]{1,0:T(8,128)(2,1)} %param.18), kind=kLoop, calls=%fused_computation.13 | loop fusion | flops 4194304 | bytes 4194304 | tf_op jit(solution)/shard_map/concatenate | solution.py:113
  75.2 3.9 %pad_maximum_fusion = bf16[2,2048,512]{2,1,0:T(8,128)(2,1)} fusion(bf16[2,2048,256]{2,1,0:T(8,128)(2,1)} %collective-permute-done.4, bf16[2,2048,256]{2,1,0:T(8,128)(2,1)S(1)} %bitcast.143), kind=kLoop, calls=%fused_computation.2 | loop fusion | flops 8388608 | bytes 8388608 | tf_op jit(solution)/shard_map/concatenate | solution.py:113
  79.1 10.2 %all-to-all-done.2 = bf16[16,8,2048]{2,1,0:T(8,128)(2,1)} async-done(((bf16[16,8,2048]{2,1,0:T(8,128)(2,1)}), bf16[16,8,2048]{2,1,0:T(8,128)(2,1)}, u32[]{:S(2)}, u32[]{:S(2)}) %all-to-all-start.2) | async-done | bytes 524320 | tf_op jit(solution)/shard_map/all_to_all | solution.py:20
  89.3 2.9 %fusion.7 = f32[128,512]{1,0:T(8,128)} fusion(bf16[2,2048,512]{2,1,0:T(8,128)(2,1)} %pad_maximum_fusion, bf16[16,8,2048]{2,1,0:T(8,128)(2,1)} %all-to-all-done.2), kind=kOutput, calls=%fused_computation.16 | convolution fusion | flops 268435456 | bytes 2883584 | tf_op jit(solution)/shard_map/dot_general | solution.py:128
  92.2 3.4 %fusion.3 = bf16[16,8,2048]{2,1,0:T(8,128)(2,1)} fusion(bf16[512,2048]{1,0:T(8,128)(2,1)S(1)} %copy-done.5, f32[128,512]{1,0:T(8,128)} %fusion.7, bf16[2,2048,512]{2,1,0:T(8,128)(2,1)} %pad_maximum_fusion, bf16[16,8,2048]{2,1,0:T(8,128)(2,1)} %all-to-all-done.2), kind=kOutput, calls=%fused_computation.8 | convolution fusion | flops 537526272 | bytes 5505024 | tf_op jit(solution)/shard_map/dot_general | solution.py:149
  95.6 20.0 %all_to_all.40 = bf16[16,8,2048]{2,1,0:T(8,128)(2,1)S(1)} all-to-all(bf16[16,8,2048]{2,1,0:T(8,128)(2,1)} %fusion.3), channel_id=1, replica_groups=mesh['layer'=32,'tp'=16] {'tp'}, dimensions={0} | all-to-all | bytes 1048576 | tf_op jit(solution)/shard_map/all_to_all | solution.py:20
  116.5 3.5 %collective-permute-start.6 = (bf16[8,2048]{1,0:T(8,128)(2,1)S(1)}, bf16[8,2048]{1,0:T(8,128)(2,1)S(1)}, u32[]{:S(2)}, u32[]{:S(2)}) collective-permute-start(bf16[8,2048]{1,0:T(8,128)(2,1)S(1)} %fusion.60), channel_id=1, source_target_pairs={{0,32},{16,48},{32,64},{48,80},{64,96},{80,112},{96,128},{112,144}... | collective-permute-start | bytes 98312 | tf_op jit(solution)/shard_map/ppermute | solution.py:16
  120.9 3.8 %collective-permute-done.6 = bf16[8,2048]{1,0:T(8,128)(2,1)S(1)} collective-permute-done((bf16[8,2048]{1,0:T(8,128)(2,1)S(1)}, bf16[8,2048]{1,0:T(8,128)(2,1)S(1)}, u32[]{:S(2)}, u32[]{:S(2)}) %collective-permute-start.6) | collective-permute-done | bytes 32800 | tf_op jit(solution)/shard_map/ppermute | solution.py:16
  126.5 3.6 %all-to-all-start.4 = ((bf16[16,8,2048]{2,1,0:T(8,128)(2,1)}), bf16[16,8,2048]{2,1,0:T(8,128)(2,1)S(1)}, u32[]{:S(2)}, u32[]{:S(2)}) async-start(bf16[16,8,2048]{2,1,0:T(8,128)(2,1)} %broadcast_in_dim.42), calls=%async_computation.4 | async-start | bytes 1048576 | tf_op jit(solution)/shard_map/all_to_all | solution.py:20
  130.4 14.4 %all-to-all-done.4 = bf16[16,8,2048]{2,1,0:T(8,128)(2,1)S(1)} async-done(((bf16[16,8,2048]{2,1,0:T(8,128)(2,1)}), bf16[16,8,2048]{2,1,0:T(8,128)(2,1)S(1)}, u32[]{:S(2)}, u32[]{:S(2)}) %all-to-all-start.4) | async-done | bytes 524320 | tf_op jit(solution)/shard_map/all_to_all | solution.py:20
  145.6 1.9 collective-permute-start.7
  147.6 1.2 collective-permute-done.7
  151.6 22.9 %all_to_all.41 = bf16[16,8,2048]{2,1,0:T(8,128)(2,1)S(1)} all-to-all(bf16[16,8,2048]{2,1,0:T(8,128)(2,1)S(1)} %fusion.4), channel_id=1, replica_groups=mesh['layer'=32,'tp'=16] {'tp'}, dimensions={0} | all-to-all | bytes 1048576 | tf_op jit(solution)/shard_map/all_to_all | solution.py:20
  174.9 21.1 %all_to_all.42 = bf16[16,8,2048]{2,1,0:T(8,128)(2,1)S(1)} all-to-all(bf16[16,8,2048]{2,1,0:T(8,128)(2,1)S(1)} %broadcast_in_dim.43), channel_id=1, replica_groups=mesh['layer'=32,'tp'=16] {'tp'}, dimensions={0} | all-to-all | bytes 1048576 | tf_op jit(solution)/shard_map/all_to_all | solution.py:20
  196.4 3.3 %fusion.5 = bf16[16,8,2048]{2,1,0:T(8,128)(2,1)} fusion(bf16[512,2048]{1,0:T(8,128)(2,1)S(1)} %copy-done.6, f32[128,512]{1,0:T(8,128)S(1)} %fusion.6, bf16[2,2048,512]{2,1,0:T(8,128)(2,1)} %pad_maximum_fusion, bf16[16,8,2048]{2,1,0:T(8,128)(2,1)S(1)} %all_to_all.42), kind=kOutput, calls=%fused_computation.10 | convolution fusion | flops 537526272 | bytes 5505024 | tf_op jit(solution)/shard_map/dot_general | solution.py:149
  199.7 3.6 %all-to-all-start.7 = ((bf16[16,8,2048]{2,1,0:T(8,128)(2,1)}), bf16[16,8,2048]{2,1,0:T(8,128)(2,1)S(1)}, u32[]{:S(2)}, u32[]{:S(2)}) async-start(bf16[16,8,2048]{2,1,0:T(8,128)(2,1)} %fusion.5), calls=%async_computation.7 | async-start | bytes 1048576 | tf_op jit(solution)/shard_map/all_to_all | solution.py:20
  204.8 16.7 %all-to-all-done.7 = bf16[16,8,2048]{2,1,0:T(8,128)(2,1)S(1)} async-done(((bf16[16,8,2048]{2,1,0:T(8,128)(2,1)}), bf16[16,8,2048]{2,1,0:T(8,128)(2,1)S(1)}, u32[]{:S(2)}, u32[]{:S(2)}) %all-to-all-start.7) | async-done | bytes 524320 | tf_op jit(solution)/shard_map/all_to_all | solution.py:20
  (141 shorter events, 20.1 us)
Async XLA Ops:
  0.6 49.9 %copy-start = (f32[16,2048]{1,0:T(8,128)S(1)}, f32[16,2048]{1,0:T(8,128)}, u32[]{:S(2)}) copy-start(f32[16,2048]{1,0:T(8,128)} %param.14) | copy-start | bytes 393220
  0.6 32.8 %copy-start.2 = (bf16[1,2048,192]{1,2,0:T(8,128)(2,1)S(1)}, bf16[1,2048,192]{1,2,0:T(8,128)(2,1)}, u32[]{:S(2)}) copy-start(bf16[1,2048,192]{1,2,0:T(8,128)(2,1)} %param.15) | copy-start | bytes 2359300
  0.7 24.9 %copy-start.14 = (bf16[64,2048]{1,0:T(8,128)(2,1)S(1)}, bf16[64,2048]{1,0:T(8,128)(2,1)}, u32[]{:S(2)}) copy-start(bf16[64,2048]{1,0:T(8,128)(2,1)} %param.16) | copy-start | bytes 786436
  2.6 30.8 %all-to-all-start = ((bf16[16,8,2048]{2,1,0:T(8,128)(2,1)}), bf16[16,8,2048]{2,1,0:T(8,128)(2,1)S(1)}, u32[]{:S(2)}, u32[]{:S(2)}) async-start(bf16[16,8,2048]{2,1,0:T(8,128)(2,1)} %first_blocks.1), calls=%async_computation | async-start | bytes 1048576 | tf_op jit(solution)/shard_map/all_to_all | solution.py:20
  14.6 19.2 %collective-permute-start.1 = (bf16[1,2048,192]{1,2,0:T(8,128)(2,1)}, bf16[1,2048,192]{1,2,0:T(8,128)(2,1)S(1)}, u32[]{:S(2)}, u32[]{:S(2)}) collective-permute-start(bf16[1,2048,192]{1,2,0:T(8,128)(2,1)} %param.15), channel_id=1, source_target_pairs={{0,16},{16,0},{32,48},{48,32},{64,80},{80,64},{96,112},{112,96},{1... | collective-permute-start | bytes 2359304 | tf_op jit(solution)/shard_map/ppermute | solution.py:11
  18.1 18.3 %copy-start.15 = (f32[1,64,64]{1,2,0:T(8,128)}, f32[1,64,64]{1,2,0:T(8,128)S(1)}, u32[]{:S(2)}) copy-start(f32[1,64,64]{1,2,0:T(8,128)S(1)} %copy.21) | copy-start | bytes 49156
  19.0 4.4 %collective-permute-start = (f32[1,66,64]{1,2,0:T(8,128)S(1)}, f32[1,66,64]{1,2,0:T(8,128)S(1)}, u32[]{:S(2)}, u32[]{:S(2)}) collective-permute-start(f32[1,66,64]{1,2,0:T(8,128)S(1)} %maximum_maximum_fusion), channel_id=1, source_target_pairs={{0,16},{16,0},{32,48},{48,32},{64,80},{80,64},{96,112},{112,96},{1... | collective-permute-start | bytes 50696 | tf_op jit(solution)/shard_map/ppermute | solution.py:11
  21.4 4.2 %collective-permute-start.3 = (bf16[64,2048]{1,0:T(8,128)(2,1)}, bf16[64,2048]{1,0:T(8,128)(2,1)S(1)}, u32[]{:S(2)}, u32[]{:S(2)}) collective-permute-start(bf16[64,2048]{1,0:T(8,128)(2,1)} %param.16), channel_id=1, source_target_pairs={{0,16},{16,0},{32,48},{48,32},{64,80},{80,64},{96,112},{112,96},{1... | collective-permute-start | bytes 786440 | tf_op jit(solution)/shard_map/ppermute | solution.py:11
  23.4 14.6 %copy-start.7 = (pred[128,256]{1,0:T(8,128)(4,1)}, pred[128,256]{1,0:T(8,128)(4,1)S(1)}, u32[]{:S(2)}) copy-start(pred[128,256]{1,0:T(8,128)(4,1)S(1)} %concatenate.51) | copy-start | bytes 98308
  23.4 13.0 %copy-start.21 = (f32[1,66,64]{1,2,0:T(8,128)}, f32[1,66,64]{1,2,0:T(8,128)S(1)}, u32[]{:S(2)}) copy-start(f32[1,66,64]{1,2,0:T(8,128)S(1)} %collective-permute-done) | copy-start | bytes 50692
  34.2 3.1 %collective-permute-start.2 = (bf16[128,2,128]{0,2,1:T(8,128)(2,1)S(1)}, bf16[128,2,128]{0,2,1:T(8,128)(2,1)S(1)}, u32[]{:S(2)}, u32[]{:S(2)}) collective-permute-start(bf16[128,2,128]{0,2,1:T(8,128)(2,1)S(1)} %pad_maximum_fusion.6), channel_id=1, source_target_pairs={{0,16},{16,0},{32,48},{48,32},{64,80},{80,64},{96,112},{112,96},{1... | collective-permute-start | bytes 196616 | tf_op jit(solution)/shard_map/ppermute | solution.py:11
  40.0 24.3 %all-to-all-start.1 = ((bf16[16,8,2048]{2,1,0:T(8,128)(2,1)}), bf16[16,8,2048]{2,1,0:T(8,128)(2,1)}, u32[]{:S(2)}, u32[]{:S(2)}) async-start(bf16[16,8,2048]{2,1,0:T(8,128)(2,1)} %fusion.2), calls=%async_computation.1 | async-start | bytes 1048576 | tf_op jit(solution)/shard_map/all_to_all | solution.py:20
  46.1 29.1 %collective-permute-start.4 = (bf16[2,2048,256]{2,1,0:T(8,128)(2,1)S(1)}, bf16[2,2048,256]{2,1,0:T(8,128)(2,1)}, u32[]{:S(2)}, u32[]{:S(2)}) collective-permute-start(bf16[2,2048,256]{2,1,0:T(8,128)(2,1)S(1)} %bitcast.142), channel_id=1, source_target_pairs={{0,16},{16,0},{32,48},{48,32},{64,80},{80,64},{96,112},{112,96},{1... | collective-permute-start | bytes 6291464 | tf_op jit(solution)/shard_map/ppermute | solution.py:11
  48.2 23.9 %collective-permute-start.5 = (bf16[256,2048]{1,0:T(8,128)(2,1)}, bf16[256,2048]{1,0:T(8,128)(2,1)}, u32[]{:S(2)}, u32[]{:S(2)}) collective-permute-start(bf16[256,2048]{1,0:T(8,128)(2,1)} %param.18), channel_id=1, source_target_pairs={{0,16},{16,0},{32,48},{48,32},{64,80},{80,64},{96,112},{112,96},{1... | collective-permute-start | bytes 3145736 | tf_op jit(solution)/shard_map/ppermute | solution.py:11
  67.8 21.5 %all-to-all-start.2 = ((bf16[16,8,2048]{2,1,0:T(8,128)(2,1)}), bf16[16,8,2048]{2,1,0:T(8,128)(2,1)}, u32[]{:S(2)}, u32[]{:S(2)}) async-start(bf16[16,8,2048]{2,1,0:T(8,128)(2,1)} %broadcast_in_dim.41), calls=%async_computation.2 | async-start | bytes 1048576 | tf_op jit(solution)/shard_map/all_to_all | solution.py:20
  79.1 13.1 %copy-start.5 = (bf16[512,2048]{1,0:T(8,128)(2,1)S(1)}, bf16[512,2048]{1,0:T(8,128)(2,1)}, u32[]{:S(2)}) copy-start(bf16[512,2048]{1,0:T(8,128)(2,1)} %pad_maximum_fusion.1) | copy-start | bytes 6291460
  95.6 34.5 %copy-start.11 = (bf16[256,2,64]{0,2,1:T(8,128)(2,1)S(1)}, bf16[256,2,64]{0,2,1:T(8,128)(2,1)}, u32[]{:S(2)}) copy-start(bf16[256,2,64]{0,2,1:T(8,128)(2,1)} %copy-done.10) | copy-start | bytes 196612
  95.6 34.5 %copy-start.16 = (f32[1,64,64]{1,2,0:T(8,128)S(1)}, f32[1,64,64]{1,2,0:T(8,128)}, u32[]{:S(2)}) copy-start(f32[1,64,64]{1,2,0:T(8,128)} %copy-done.15) | copy-start | bytes 49156
  95.6 34.5 %copy-start.18 = (bf16[128,2,64]{0,2,1:T(8,128)(2,1)S(1)}, bf16[128,2,64]{0,2,1:T(8,128)(2,1)}, u32[]{:S(2)}) copy-start(bf16[128,2,64]{0,2,1:T(8,128)(2,1)} %copy-done.17) | copy-start | bytes 98308
  95.6 34.5 %copy-start.22 = (f32[1,66,64]{1,2,0:T(8,128)S(1)}, f32[1,66,64]{1,2,0:T(8,128)}, u32[]{:S(2)}) copy-start(f32[1,66,64]{1,2,0:T(8,128)} %copy-done.21) | copy-start | bytes 50692
  95.6 34.5 %copy-start.25 = (bf16[128,2,64]{0,2,1:T(8,128)(2,1)S(1)}, bf16[128,2,64]{0,2,1:T(8,128)(2,1)}, u32[]{:S(2)}) copy-start(bf16[128,2,64]{0,2,1:T(8,128)(2,1)} %copy-done.24) | copy-start | bytes 98308
  115.6 29.6 %copy-start.4 = (bf16[1,2048,192]{1,2,0:T(8,128)(2,1)S(1)}, bf16[1,2048,192]{1,2,0:T(8,128)(2,1)}, u32[]{:S(2)}) copy-start(bf16[1,2048,192]{1,2,0:T(8,128)(2,1)} %copy-done.3) | copy-start | bytes 2359300
  116.5 8.1 %collective-permute-start.6 = (bf16[8,2048]{1,0:T(8,128)(2,1)S(1)}, bf16[8,2048]{1,0:T(8,128)(2,1)S(1)}, u32[]{:S(2)}, u32[]{:S(2)}) collective-permute-start(bf16[8,2048]{1,0:T(8,128)(2,1)S(1)} %fusion.60), channel_id=1, source_target_pairs={{0,32},{16,48},{32,64},{48,80},{64,96},{80,112},{96,128},{112,144}... | collective-permute-start | bytes 98312 | tf_op jit(solution)/shard_map/ppermute | solution.py:16
  126.5 18.4 %all-to-all-start.4 = ((bf16[16,8,2048]{2,1,0:T(8,128)(2,1)}), bf16[16,8,2048]{2,1,0:T(8,128)(2,1)S(1)}, u32[]{:S(2)}, u32[]{:S(2)}) async-start(bf16[16,8,2048]{2,1,0:T(8,128)(2,1)} %broadcast_in_dim.42), calls=%async_computation.4 | async-start | bytes 1048576 | tf_op jit(solution)/shard_map/all_to_all | solution.py:20
  130.1 18.8 %copy-start.8 = (pred[128,256]{1,0:T(8,128)(4,1)S(1)}, pred[128,256]{1,0:T(8,128)(4,1)}, u32[]{:S(2)}) copy-start(pred[128,256]{1,0:T(8,128)(4,1)} %copy-done.7) | copy-start | bytes 98308
  130.4 20.0 %copy-start.28 = (f32[2,64,64]{1,2,0:T(8,128)}, f32[2,64,64]{1,2,0:T(8,128)S(1)}, u32[]{:S(2)}) copy-start(f32[2,64,64]{1,2,0:T(8,128)S(1)} %convolution_add_fusion) | copy-start | bytes 98308
  130.4 19.2 %copy-start.30 = (f32[1,64]{1,0:T(1,128)S(1)}, f32[1,64]{1,0:T(1,128)}, u32[]{:S(2)}) copy-start(f32[1,64]{1,0:T(1,128)} %param.20) | copy-start | bytes 772
  130.4 20.0 %copy-start.35 = (f32[2]{0:T(128)S(1)}, f32[2]{0:T(128)}, u32[]{:S(2)}) copy-start(f32[2]{0:T(128)} %copy-done.34) | copy-start | bytes 28
  145.6 3.1 %collective-permute-start.7 = (bf16[128,2,128]{0,2,1:T(8,128)(2,1)S(1)}, bf16[128,2,128]{0,2,1:T(8,128)(2,1)S(1)}, u32[]{:S(2)}, u32[]{:S(2)}) collective-permute-start(bf16[128,2,128]{0,2,1:T(8,128)(2,1)S(1)} %pad_maximum_fusion.8), channel_id=1, source_target_pairs={{0,16},{16,0},{32,48},{48,32},{64,80},{80,64},{96,112},{112,96},{1... | collective-permute-start | bytes 196616 | tf_op jit(solution)/shard_map/ppermute | solution.py:11
  151.3 44.7 %copy-start.1 = (bf16[2,2048,512]{2,1,0:T(8,128)(2,1)S(1)}, bf16[2,2048,512]{2,1,0:T(8,128)(2,1)}, u32[]{:S(2)}) copy-start(bf16[2,2048,512]{2,1,0:T(8,128)(2,1)} %pad_maximum_fusion) | copy-start | bytes 12582916
  174.9 21.5 %copy-start.6 = (bf16[512,2048]{1,0:T(8,128)(2,1)S(1)}, bf16[512,2048]{1,0:T(8,128)(2,1)}, u32[]{:S(2)}) copy-start(bf16[512,2048]{1,0:T(8,128)(2,1)} %pad_maximum_fusion.1) | copy-start | bytes 6291460
  199.7 21.8 %all-to-all-start.7 = ((bf16[16,8,2048]{2,1,0:T(8,128)(2,1)}), bf16[16,8,2048]{2,1,0:T(8,128)(2,1)S(1)}, u32[]{:S(2)}, u32[]{:S(2)}) async-start(bf16[16,8,2048]{2,1,0:T(8,128)(2,1)} %fusion.5), calls=%async_computation.7 | async-start | bytes 1048576 | tf_op jit(solution)/shard_map/all_to_all | solution.py:20
  (17 other events, 97.6 us)
